TPU v7x, 32 devices: a whole 2x2x4 slice. The times are simulated.
32 devices in a mesh: rep: 4 (over y, core), shard: 8 (over z, x).
Axes of the slice: x: 2, y: 2, z: 4, core: 2. Of those that a mesh axis runs over, the one named last changes fastest.
Arguments:
- tokens: bfloat16 [2, 32, 128, 768], P(None, ('rep', 'shard')), may hold values from -6 to 6
- segment_ids: int32 [2, 32, 128], P(None, ('rep', 'shard')), may hold values from 0 to 5, never falling along the last dimension, each value on 1 to 64 neighbouring positions
- cotangent: bfloat16 [2, 32, 128, 768], P(None, ('rep', 'shard')), may hold values from -6 to 6
- first_gain: bfloat16 [768], P('shard'), may hold values from 0.5 to 1.5
- first_shift: bfloat16 [768], P('shard'), may hold values from -1.75 to 1.75
- input_weight: bfloat16 [768, 2304], P('shard'), may hold values from -0.21875 to 0.21875
- input_bias: bfloat16 [2304], P('shard'), may hold values from -1.75 to 1.75
- short_weight: bfloat16 [3, 2304], P(None, 'shard'), may hold values from -3.5 to 3.5
- short_bias: bfloat16 [2304], P('shard'), may hold values from -1.75 to 1.75
- inner_weight: bfloat16 [33, 64], P(None, 'shard'), may hold values from -1 to 1
- inner_bias: bfloat16 [64], P('shard'), may hold values from -3 to 3
- sine_scale: bfloat16 [64], P('shard'), may hold values from 0.59765625 to 1.3984375
- middle_weight: bfloat16 [64, 64], P('shard'), may hold values from -0.75 to 0.75
- middle_bias: bfloat16 [64], P('shard'), may hold values from -3 to 3
- filter_weight: bfloat16 [64, 768], P(None, 'shard'), may hold values from -0.1875 to 0.1875
- direct_gain: bfloat16 [768], P('shard'), may hold values from -3 to 3
- output_weight: bfloat16 [768, 768], P('shard'), may hold values from -0.21875 to 0.21875
- output_bias: bfloat16 [768], P('shard'), may hold values from -1.75 to 1.75
- second_gain: bfloat16 [768], P('shard'), may hold values from 0.5 to 1.5
- second_shift: bfloat16 [768], P('shard'), may hold values from -1.75 to 1.75
- expand_weight: bfloat16 [768, 3072], P('shard'), may hold values from -0.21875 to 0.21875
- expand_bias: bfloat16 [3072], P('shard'), may hold values from -1.75 to 1.75
- contract_weight: bfloat16 [3072, 768], P('shard'), may hold values from -0.109375 to 0.109375
- contract_bias: bfloat16 [768], P('shard'), may hold values from -1.75 to 1.75
Outputs:
- output: bfloat16 [2, 32, 128, 768], P(None, ('rep', 'shard'))
- gradient_tokens: float32 [2, 32, 128, 768], P(None, ('rep', 'shard'))
- gradient_first_gain: float32 [768], P('shard')
- gradient_first_shift: float32 [768], P('shard')
- gradient_input_weight: float32 [768, 2304], P('shard')
- gradient_input_bias: float32 [2304], P('shard')
- gradient_short_weight: float32 [3, 2304], P(None, 'shard')
- gradient_short_bias: float32 [2304], P('shard')
- gradient_inner_weight: float32 [33, 64], P(None, 'shard')
- gradient_inner_bias: float32 [64], P('shard')
- gradient_sine_scale: float32 [64], P('shard')
- gradient_middle_weight: float32 [64, 64], P('shard')
- gradient_middle_bias: float32 [64], P('shard')
- gradient_filter_weight: float32 [64, 768], P(None, 'shard')
- gradient_direct_gain: float32 [768], P('shard')
- gradient_output_weight: float32 [768, 768], P('shard')
- gradient_output_bias: float32 [768], P('shard')
- gradient_second_gain: float32 [768], P('shard')
- gradient_second_shift: float32 [768], P('shard')
- gradient_expand_weight: float32 [768, 3072], P('shard')
- gradient_expand_bias: float32 [3072], P('shard')
- gradient_contract_weight: float32 [3072, 768], P('shard')
- gradient_contract_bias: float32 [768], P('shard')
Inputs may be any that keep to these rules, and one draw needn't show every extreme that they name: `segment_ids`: within each sequence the document numbers never fall; each of the 6 numbers covers 1 to 64 consecutive tokens, and one covers exactly 64.
All inputs are finite; a program needn't handle non-finite values.
Results may differ from a plain program's by a relative error of at most 0.0078.
Values may be sent and summed in bfloat16 or wider, within the bound.
A program may use at most 192 MiB of HBM per device.

v0:
```python
import math

import jax
import jax.numpy as jnp
from jax import lax
from jax.sharding import PartitionSpec as P

DOCS = 6


EPSILON = 1e-05
HIGHEST = lax.Precision.HIGHEST


def positions(length):
    places = jnp.arange(length, dtype=jnp.float32)
    linear_ramp = places / (length - 1)
    angles = 2.0 * math.pi * places / length
    scales = 0.0001 + jnp.arange(16, dtype=jnp.float32) * ((15.0 - 0.0001) / 15.0)
    phases = angles[:, None] * scales[None, :]
    return jnp.concatenate([linear_ramp[:, None], jnp.cos(phases), -jnp.sin(phases)], axis=1)


def decay_table(length, width):
    linear_ramp = jnp.arange(length, dtype=jnp.float32) / (length - 1)
    rates = math.log(100.0) * (
        1.0 / 1.5 + (1.0 / 0.3 - 1.0 / 1.5) * jnp.arange(width, dtype=jnp.float32) / (width - 1)
    )
    return jnp.exp(-linear_ramp[:, None] * rates[None, :])


def filter_taps(
    inner_weight, inner_bias, sine_scale, middle_weight, middle_bias, filter_weight, length
):
    features = positions(length)
    first_sine = jnp.sin(
        sine_scale * (jnp.dot(features, inner_weight, precision=HIGHEST) + inner_bias)
    )
    second_sine = jnp.sin(
        sine_scale * (jnp.dot(first_sine, middle_weight, precision=HIGHEST) + middle_bias)
    )
    return jnp.dot(second_sine, filter_weight, precision=HIGHEST) * decay_table(
        length, filter_weight.shape[1]
    )


def normalize(values, gain_row, shift_row):
    center = values - jnp.mean(values, axis=-1, keepdims=True)
    spread = jnp.mean(center * center, axis=-1, keepdims=True)
    return center * lax.rsqrt(spread + EPSILON) * gain_row + shift_row


def smooth_gate(values):
    return jax.nn.gelu(values, approximate=True)


def to_float(member):
    return member.astype(jnp.float32)


def short_filter(projected, segments, weight, offset):
    running = offset + weight[0] * projected
    for step_back in (1, 2):
        moved_rows = jnp.concatenate(
            [jnp.zeros_like(projected[:, :step_back]), projected[:, :-step_back]], axis=1
        )
        moved_ids = jnp.concatenate(
            [jnp.full_like(segments[:, :step_back], -1), segments[:, :-step_back]], axis=1
        )
        same_doc = (moved_ids == segments).astype(projected.dtype)
        running = running + weight[step_back] * moved_rows * same_doc[:, :, None]
    return running


def wave_tables(length):
    padded_size = 2 * length
    freq_index = jnp.arange(length + 1, dtype=jnp.int32)
    place_index = jnp.arange(length, dtype=jnp.int32)
    wrapped = freq_index[:, None] * place_index[None, :] % padded_size
    angles = 2.0 * math.pi / padded_size * wrapped.astype(jnp.float32)
    weights_row = (
        jnp.where((freq_index == 0) | (freq_index == length), 1.0, 2.0).astype(jnp.float32)
        / padded_size
    )
    return (jnp.cos(angles), jnp.sin(angles), weights_row)


def spectrum(tables, signal):
    cosine, sine, weights_row = tables
    real_part = jnp.einsum("ft,...td->...fd", cosine, signal, precision=HIGHEST)
    imag_part = -jnp.einsum("ft,...td->...fd", sine, signal, precision=HIGHEST)
    return (real_part, imag_part)


def inverse(tables, real_part, imag_part):
    cosine, sine, weights_row = tables
    scaled_real = real_part * weights_row[:, None]
    scaled_imag = imag_part * weights_row[:, None]
    return jnp.einsum("ft,...fd->...td", cosine, scaled_real, precision=HIGHEST) - jnp.einsum(
        "ft,...fd->...td", sine, scaled_imag, precision=HIGHEST
    )


def per_device(
    tokens,
    segment_ids,
    cotangent,
    first_gain,
    first_shift,
    input_weight,
    input_bias,
    short_weight,
    short_bias,
    inner_weight,
    inner_bias,
    sine_scale,
    middle_weight,
    middle_bias,
    filter_weight,
    direct_gain,
    output_weight,
    output_bias,
    second_gain,
    second_shift,
    expand_weight,
    expand_bias,
    contract_weight,
    contract_bias,
):
    micro_count, local_sequences, length, width = tokens.shape
    row_count = local_sequences * length
    tables = wave_tables(length)

    def fetch_mixer():
        return (
            lax.all_gather(first_gain, "shard", axis=0, tiled=True),
            lax.all_gather(first_shift, "shard", axis=0, tiled=True),
            lax.all_gather(input_weight, "shard", axis=0, tiled=True),
            lax.all_gather(input_bias, "shard", axis=0, tiled=True),
            lax.all_gather(short_weight, "shard", axis=1, tiled=True),
            lax.all_gather(short_bias, "shard", axis=0, tiled=True),
            lax.all_gather(inner_weight, "shard", axis=1, tiled=True),
            lax.all_gather(inner_bias, "shard", axis=0, tiled=True),
            lax.all_gather(sine_scale, "shard", axis=0, tiled=True),
            lax.all_gather(middle_weight, "shard", axis=0, tiled=True),
            lax.all_gather(middle_bias, "shard", axis=0, tiled=True),
            lax.all_gather(filter_weight, "shard", axis=1, tiled=True),
            lax.all_gather(direct_gain, "shard", axis=0, tiled=True),
            lax.all_gather(output_weight, "shard", axis=0, tiled=True),
            lax.all_gather(output_bias, "shard", axis=0, tiled=True),
        )

    def fetch_dense():
        return (
            lax.all_gather(second_gain, "shard", axis=0, tiled=True),
            lax.all_gather(second_shift, "shard", axis=0, tiled=True),
            lax.all_gather(expand_weight, "shard", axis=0, tiled=True),
            lax.all_gather(expand_bias, "shard", axis=0, tiled=True),
            lax.all_gather(contract_weight, "shard", axis=0, tiled=True),
            lax.all_gather(contract_bias, "shard", axis=0, tiled=True),
        )

    results = []
    input_deltas = []
    mixer_total = None
    dense_total = None
    for micro_index in range(micro_count):
        mixer_parts = fetch_mixer()
        dense_parts = fetch_dense()
        kernel = filter_taps(
            to_float(mixer_parts[6]),
            to_float(mixer_parts[7]),
            to_float(mixer_parts[8]),
            to_float(mixer_parts[9]),
            to_float(mixer_parts[10]),
            to_float(mixer_parts[11]),
            length,
        )
        kernel, kernel_wave = (kernel, spectrum(tables, kernel))
        kernel_real, kernel_imag = kernel_wave
        segment_block = segment_ids[micro_index]
        membership = (
            segment_block[:, None, :] == jnp.arange(DOCS, dtype=jnp.int32)[None, :, None]
        ).astype(jnp.float32)
        flat_tokens = tokens[micro_index].reshape(row_count, width).astype(jnp.float32)
        normed_first = normalize(
            flat_tokens, to_float(mixer_parts[0]), to_float(mixer_parts[1])
        ).astype(jnp.bfloat16)
        projected = jnp.dot(
            normed_first, mixer_parts[2], preferred_element_type=jnp.float32
        ) + to_float(mixer_parts[3])
        projected_rows = projected.reshape(local_sequences, length, 3 * width)
        short_out = short_filter(
            projected_rows, segment_block, to_float(mixer_parts[4]), to_float(mixer_parts[5])
        )
        gate_out = short_out[:, :, :width]
        gate_in = short_out[:, :, width : 2 * width]
        values = short_out[:, :, 2 * width :]
        carried = values * gate_in
        direct = to_float(mixer_parts[12])
        carried_real, carried_imag = spectrum(tables, carried[:, None] * membership[:, :, :, None])
        conv_pieces = inverse(
            tables,
            carried_real * kernel_real - carried_imag * kernel_imag,
            carried_real * kernel_imag + carried_imag * kernel_real,
        )
        convolved = jnp.sum(conv_pieces * membership[:, :, :, None], axis=1) + direct * carried
        gated_low = (convolved * gate_out).astype(jnp.bfloat16).reshape(row_count, width)
        mixed_out = jnp.dot(
            gated_low, mixer_parts[13], preferred_element_type=jnp.float32
        ) + to_float(mixer_parts[14])
        residual = flat_tokens + mixed_out
        second_gain_f = to_float(dense_parts[0])
        second_shift_f = to_float(dense_parts[1])
        normed_second = normalize(residual, second_gain_f, second_shift_f).astype(jnp.bfloat16)
        hidden_pre = jnp.dot(
            normed_second, dense_parts[2], preferred_element_type=jnp.float32
        ) + to_float(dense_parts[3])
        hidden_post = smooth_gate(hidden_pre).astype(jnp.bfloat16)
        result = (
            residual
            + jnp.dot(hidden_post, dense_parts[4], preferred_element_type=jnp.float32)
            + to_float(dense_parts[5])
        )
        results.append(result.astype(jnp.bfloat16).reshape(local_sequences, length, width))
        back_mixer = fetch_mixer()
        back_dense = fetch_dense()
        upstream = cotangent[micro_index].reshape(row_count, width)
        upstream_float = upstream.astype(jnp.float32)
        delta_contract_weight = jnp.einsum(
            "tf,td->fd", hidden_post, upstream, preferred_element_type=jnp.float32
        )
        delta_contract_bias = jnp.sum(upstream_float, axis=0)
        back_hidden = jnp.einsum(
            "td,fd->tf", upstream, back_dense[4], preferred_element_type=jnp.float32
        )
        back_pre = jax.vjp(smooth_gate, hidden_pre)[1](back_hidden)[0].astype(jnp.bfloat16)
        delta_expand_weight = jnp.einsum(
            "td,tf->df", normed_second, back_pre, preferred_element_type=jnp.float32
        )
        delta_expand_bias = jnp.sum(back_pre.astype(jnp.float32), axis=0)
        back_second = jnp.einsum(
            "tf,df->td", back_pre, back_dense[2], preferred_element_type=jnp.float32
        )
        second_pull = jax.vjp(
            normalize, residual, to_float(back_dense[0]), to_float(back_dense[1])
        )[1]
        back_norm_second, delta_second_gain, delta_second_shift = second_pull(back_second)
        back_residual = upstream_float + back_norm_second
        back_mixed = back_residual.astype(jnp.bfloat16)
        delta_output_weight = jnp.einsum(
            "td,te->de", gated_low, back_mixed, preferred_element_type=jnp.float32
        )
        delta_output_bias = jnp.sum(back_mixed.astype(jnp.float32), axis=0)
        back_gated = jnp.einsum(
            "te,de->td", back_mixed, back_mixer[13], preferred_element_type=jnp.float32
        ).reshape(local_sequences, length, width)
        back_conv = back_gated * gate_out
        grad_real, grad_imag = spectrum(tables, back_conv[:, None] * membership[:, :, :, None])
        carried_back_pieces = inverse(
            tables,
            grad_real * kernel_real + grad_imag * kernel_imag,
            grad_imag * kernel_real - grad_real * kernel_imag,
        )
        back_carried = (
            jnp.sum(carried_back_pieces * membership[:, :, :, None], axis=1) + direct * back_conv
        )
        cross_real = jnp.sum(grad_real * carried_real + grad_imag * carried_imag, axis=(0, 1))
        cross_imag = jnp.sum(grad_imag * carried_real - grad_real * carried_imag, axis=(0, 1))
        back_kernel = inverse(tables, cross_real, cross_imag)
        delta_direct = jnp.sum(back_conv * carried, axis=(0, 1))
        back_short = jnp.concatenate(
            [back_gated * convolved, back_carried * values, back_carried * gate_in], axis=2
        )
        short_pull = jax.vjp(
            lambda rows_in, taps_in, offset_in: short_filter(
                rows_in, segment_block, taps_in, offset_in
            ),
            projected_rows,
            to_float(back_mixer[4]),
            to_float(back_mixer[5]),
        )[1]
        back_projected, delta_short_weight, delta_short_bias = short_pull(back_short)
        back_projected = back_projected.reshape(row_count, 3 * width).astype(jnp.bfloat16)
        delta_input_weight = jnp.einsum(
            "td,tp->dp", normed_first, back_projected, preferred_element_type=jnp.float32
        )
        delta_input_bias = jnp.sum(back_projected.astype(jnp.float32), axis=0)
        back_first = jnp.einsum(
            "tp,dp->td", back_projected, back_mixer[2], preferred_element_type=jnp.float32
        )
        first_pull = jax.vjp(
            normalize, flat_tokens, to_float(back_mixer[0]), to_float(back_mixer[1])
        )[1]
        back_norm_first, delta_first_gain, delta_first_shift = first_pull(back_first)
        input_deltas.append(
            (back_residual + back_norm_first).reshape(local_sequences, length, width)
        )
        filter_pull = jax.vjp(
            lambda weight_one, bias_one, scale_all, weight_two, bias_two, weight_three: filter_taps(
                weight_one, bias_one, scale_all, weight_two, bias_two, weight_three, length
            ),
            to_float(back_mixer[6]),
            to_float(back_mixer[7]),
            to_float(back_mixer[8]),
            to_float(back_mixer[9]),
            to_float(back_mixer[10]),
            to_float(back_mixer[11]),
        )[1]
        filter_deltas = filter_pull(back_kernel)
        mixer_part = (
            delta_first_gain,
            delta_first_shift,
            delta_input_weight,
            delta_input_bias,
            delta_short_weight,
            delta_short_bias,
            filter_deltas[0],
            filter_deltas[1],
            filter_deltas[2],
            filter_deltas[3],
            filter_deltas[4],
            filter_deltas[5],
            delta_direct,
            delta_output_weight,
            delta_output_bias,
        )
        dense_part = (
            delta_second_gain,
            delta_second_shift,
            delta_expand_weight,
            delta_expand_bias,
            delta_contract_weight,
            delta_contract_bias,
        )
        if micro_index == 0:
            mixer_total = mixer_part
            dense_total = dense_part
        else:
            mixer_total = jax.tree.map(jnp.add, mixer_total, mixer_part)
            dense_total = jax.tree.map(jnp.add, dense_total, dense_part)
    dense_total = (
        lax.psum_scatter(dense_total[0], "shard", scatter_dimension=0, tiled=True),
        lax.psum_scatter(dense_total[1], "shard", scatter_dimension=0, tiled=True),
        lax.psum_scatter(dense_total[2], "shard", scatter_dimension=0, tiled=True),
        lax.psum_scatter(dense_total[3], "shard", scatter_dimension=0, tiled=True),
        lax.psum_scatter(dense_total[4], "shard", scatter_dimension=0, tiled=True),
        lax.psum_scatter(dense_total[5], "shard", scatter_dimension=0, tiled=True),
    )
    mixer_total = (
        lax.psum_scatter(mixer_total[0], "shard", scatter_dimension=0, tiled=True),
        lax.psum_scatter(mixer_total[1], "shard", scatter_dimension=0, tiled=True),
        lax.psum_scatter(mixer_total[2], "shard", scatter_dimension=0, tiled=True),
        lax.psum_scatter(mixer_total[3], "shard", scatter_dimension=0, tiled=True),
        lax.psum_scatter(mixer_total[4], "shard", scatter_dimension=1, tiled=True),
        lax.psum_scatter(mixer_total[5], "shard", scatter_dimension=0, tiled=True),
        lax.psum_scatter(mixer_total[6], "shard", scatter_dimension=1, tiled=True),
        lax.psum_scatter(mixer_total[7], "shard", scatter_dimension=0, tiled=True),
        lax.psum_scatter(mixer_total[8], "shard", scatter_dimension=0, tiled=True),
        lax.psum_scatter(mixer_total[9], "shard", scatter_dimension=0, tiled=True),
        lax.psum_scatter(mixer_total[10], "shard", scatter_dimension=0, tiled=True),
        lax.psum_scatter(mixer_total[11], "shard", scatter_dimension=1, tiled=True),
        lax.psum_scatter(mixer_total[12], "shard", scatter_dimension=0, tiled=True),
        lax.psum_scatter(mixer_total[13], "shard", scatter_dimension=0, tiled=True),
        lax.psum_scatter(mixer_total[14], "shard", scatter_dimension=0, tiled=True),
    )
    summed = lax.psum(
        (
            mixer_total[0],
            mixer_total[1],
            mixer_total[2],
            mixer_total[3],
            mixer_total[4],
            mixer_total[5],
            mixer_total[6],
            mixer_total[7],
            mixer_total[8],
            mixer_total[9],
            mixer_total[10],
            mixer_total[11],
            mixer_total[12],
            mixer_total[13],
            mixer_total[14],
            dense_total[0],
            dense_total[1],
            dense_total[2],
            dense_total[3],
            dense_total[4],
            dense_total[5],
        ),
        "rep",
    )
    return (jnp.stack(results), jnp.stack(input_deltas)) + tuple(summed)


def solution(mesh):
    placed = (
        P(None, ("rep", "shard"), None, None),
        P(None, ("rep", "shard"), None),
        P(None, ("rep", "shard"), None, None),
        P("shard"),
        P("shard"),
        P("shard", None),
        P("shard"),
        P(None, "shard"),
        P("shard"),
        P(None, "shard"),
        P("shard"),
        P("shard"),
        P("shard", None),
        P("shard"),
        P(None, "shard"),
        P("shard"),
        P("shard", None),
        P("shard"),
        P("shard"),
        P("shard"),
        P("shard", None),
        P("shard"),
        P("shard", None),
        P("shard"),
    )
    return jax.shard_map(
        per_device,
        mesh=mesh,
        in_specs=placed,
        out_specs=(
            P(None, ("rep", "shard"), None, None),
            P(None, ("rep", "shard"), None, None),
            P("shard"),
            P("shard"),
            P("shard", None),
            P("shard"),
            P(None, "shard"),
            P("shard"),
            P(None, "shard"),
            P("shard"),
            P("shard"),
            P("shard", None),
            P("shard"),
            P(None, "shard"),
            P("shard"),
            P("shard", None),
            P("shard"),
            P("shard"),
            P("shard"),
            P("shard", None),
            P("shard"),
            P("shard", None),
            P("shard"),
        ),
        check_vma=False,
    )
```

profile of v0, /device:TPU:0, one launch (start us, length us, event | category | flops | bytes accessed | tf_op | source)
XLA Modules:
  0.0 1182.3 jit_solution(6863999137191947376)
XLA Ops:
  13.9 32.3 %all-gather = bf16[8,288,3]{1,2,0:T(4,128)(2,1)S(1)} all-gather(bf16[1,288,3]{1,2,0:T(4,128)(2,1)S(1)} %bitcast.565), channel_id=1, replica_groups=mesh['rep'=4,'shard'=8] {'shard'}, dimensions={0}, use_global_device_ids=true | all-gather | bytes 15552 | tf_op jit(solution)/shard_map/all_gather | solution.py:140
  46.4 31.6 %all-gather.1 = bf16[8,96,64]{1,2,0:T(8,128)(2,1)S(1)} all-gather(bf16[1,96,64]{1,2,0:T(8,128)(2,1)S(1)} %bitcast.562), channel_id=1, replica_groups=mesh['rep'=4,'shard'=8] {'shard'}, dimensions={0}, use_global_device_ids=true | all-gather | bytes 110592 | tf_op jit(solution)/shard_map/all_gather | solution.py:147
  78.2 26.1 %all_gather.51 = bf16[64,64]{1,0:T(8,128)(2,1)S(1)} all-gather(bf16[8,64]{1,0:T(8,128)(2,1)S(1)} %copy-done.144), channel_id=1, replica_groups=mesh['rep'=4,'shard'=8] {'shard'}, dimensions={0}, use_global_device_ids=true | all-gather | bytes 9216 | tf_op jit(solution)/shard_map/all_gather | solution.py:145
  104.3 26.4 %all_gather.49 = bf16[33,64]{0,1:T(8,128)(2,1)S(1)} all-gather(bf16[33,8]{0,1:T(8,128)(2,1)S(1)} %copy-done.145), channel_id=1, replica_groups=mesh['rep'=4,'shard'=8] {'shard'}, dimensions={1}, use_global_device_ids=true | all-gather | bytes 4752 | tf_op jit(solution)/shard_map/all_gather | solution.py:142
  133.6 34.8 %all-reduce.46 = (bf16[2304]{0:T(1024)(128)(2,1)S(1)}, bf16[768]{0:T(1024)(128)(2,1)S(1)}, bf16[768]{0:T(1024)(128)(2,1)S(1)}, bf16[2304]{0:T(1024)(128)(2,1)S(1...) all-reduce(bf16[2304]{0:T(1024)(128)(2,1)S(1)} %dynamic-update-slic, ...), channel_id=1, replica_groups=mesh['rep'=4,'shard'=8] {'shard'}, use_global_device_ids=true, to_apply=%add.19 | all-reduce | flops 10176 | bytes 40704
  170.4 26.9 %all-gather.2 = bf16[8,1,384]{2,1,0:T(2,128)(2,1)S(1)} all-gather(bf16[1,1,384]{2,1,0:T(2,128)(2,1)S(1)} %reshape.1348), channel_id=1, replica_groups=mesh['rep'=4,'shard'=8] {'shard'}, dimensions={0}, use_global_device_ids=true | all-gather | bytes 6912 | tf_op jit(solution)/shard_map/all_gather | solution.py:158
  199.0 2.8 convolution_add_fusion.4
  202.8 2.0 fusion.129
  205.8 2.7 fusion.14
  208.6 2.8 fusion.12
  211.4 8.2 fusion.52
  219.7 9.0 fusion.65
  228.6 1.9 copy.57
  231.7 2.7 fusion.10
  234.5 2.8 fusion.8
  237.2 8.5 fusion.42
  245.7 8.7 fusion.64
  254.5 1.9 copy.58
  256.4 2.7 fusion.196
  259.1 2.0 fusion.421
  263.4 4.6 convolution_add_fusion.5
  268.0 2.0 convolution_add_fusion.6
  270.0 13.7 %all-gather.14.cloned.1.call-done = bf16[3072,768]{1,0:T(8,128)(2,1)} async-done(((bf16[384,768]{1,0:T(8,128)(2,1)}), bf16[3072,768]{1,0:T(8,128)(2,1)}) %all-gather.14.cloned.1.call-update) | async-done | bytes 4718608 | tf_op jit(solution)/shard_map/all_gather | solution.py:159
  283.7 5.6 convert_reduce_fusion
  290.2 4.2 fusion.425
  294.4 2.5 convert_reduce_fusion.1
  297.0 2.4 multiply_reduce_fusion.5
  299.8 1.5 convert_reduce_fusion.6
  301.4 3.3 multiply_reduce_fusion.6
  304.7 2.7 fusion
  307.4 4.7 fusion.29
  312.2 8.1 fusion.18
  320.2 9.2 fusion.62
  329.4 1.9 copy.60
  331.4 1.6 fusion.427
  333.1 3.3 multiply_reduce_fusion.7
  336.4 2.7 fusion.4
  339.2 6.2 fusion.41
  345.4 1.9 convolution_add_fusion.7
  347.4 10.3 fusion.30
  357.7 8.7 fusion.63
  367.6 2.0 slice_multiply_fusion.7
  373.8 1.2 fusion.201
  375.1 4.6 convolution_add_fusion
  380.7 2.7 fusion.413
  383.4 5.2 convolution_add_fusion.2
  388.7 3.1 fusion.210
  391.9 5.3 convolution_add_fusion.1
  397.5 1.5 fusion.127
  399.8 1.4 copy.61
  401.2 3.4 fusion.426
  404.8 1.4 fusion.181
  427.1 119.1 %reduce-scatter.11.cloned.1.call-done = f32[96,2304]{1,0:T(8,128)} async-done(((f32[768,2304]{1,0:T(8,128)}), f32[96,2304]{1,0:T(8,128)}) %reduce-scatter.11.cloned.1.call-update) | async-done | bytes 884752 | tf_op jit(solution)/shard_map/reduce_scatter | solution.py:353
  546.2 166.6 %reduce-scatter.15.cloned.1.call-done = f32[96,3072]{1,0:T(8,128)} async-done(((f32[768,3072]{1,0:T(8,128)}), f32[96,3072]{1,0:T(8,128)}) %reduce-scatter.15.cloned.1.call-update) | async-done | bytes 1179664 | tf_op jit(solution)/shard_map/reduce_scatter | solution.py:345
  712.8 166.6 %reduce-scatter.17.cloned.1.call-done = f32[384,768]{1,0:T(8,128)} async-done(((f32[3072,768]{1,0:T(8,128)}), f32[384,768]{1,0:T(8,128)}) %reduce-scatter.17.cloned.1.call-update) | async-done | bytes 1179664 | tf_op jit(solution)/shard_map/reduce_scatter | solution.py:347
  879.4 1.4 copy-done.41
  880.8 3.5 fusion.148
  885.1 1.9 fusion.149
  889.2 57.9 %reduce-scatter.19.cloned.1.call-done = f32[288,3]{1,0:T(8,128)} async-done(((f32[2304,3]{1,0:T(8,128)}), f32[288,3]{1,0:T(8,128)}) %reduce-scatter.19.cloned.1.call-update) | async-done | bytes 3472
  948.1 80.3 %all-reduce.50.cloned.1.call-done = (f32[768]{0:T(1024)}, f32[768]{0:T(1024)}, f32[2304]{0:T(1024)}, f32[2304]{0:T(1024)}, f32[33,64]{0,1:T(8,128)}, /*index=5*/...) async-done(((f32[768]{0:T(1024)}, f32[768]{0:T(1024)}, ...) | async-done | bytes 77840
  1039.4 53.7 %reduce-scatter.21.cloned.1.call-done = f32[96,64]{1,0:T(8,128)} async-done(((f32[768,64]{1,0:T(8,128)}), f32[96,64]{1,0:T(8,128)}) %reduce-scatter.21.cloned.1.call-update) | async-done | bytes 24592
  1094.0 12.1 %all-reduce.44 = (f32[96]{0:T(128)}, f32[96]{0:T(128)}, f32[288]{0:T(512)}, f32[3,288]{1,0:T(4,128)}, f32[288]{0:T(512)}, /*index=5*/f32[33,8]{0,1:T(8,128)}, f3...) all-reduce(f32[96]{0:T(128)S(1)} %dynamic-slice.13, ...), channel_id=1, replica_groups=mesh['rep'=4,'shard'=8] {'rep'}, use_global_device_ids=true, to_apply=%region_23.24 | all-reduce | flops 9440 | bytes 75520 | tf_op jit(solution)/shard_map/psum | solution.py:367
  1106.1 64.1 %all-reduce.52.cloned.1.call-done = (f32[96,2304]{1,0:T(8,128)}, f32[96,768]{1,0:T(8,128)}, f32[96,3072]{1,0:T(8,128)}, f32[384,768]{1,0:T(8,128)}) async-done(((f32[96,2304]{1,0:T(8,128)}, f32[96,768]{1,0:T(8,128)}, f32[96,3072]{1,0:T(8,128)}, f32[384,768]{1,0:T(8,128)}), (f32[96,2304]{1,0:T(8,128)}, f32[96,768]{1,0:T(8,128)}, f32[96,3072]{1,0:T(8,128)}, ...) | async-done | bytes 3538960 | tf_op jit(solution)/shard_map/psum | solution.py:367
  1170.2 2.2 copy.97
  (521 shorter events, 61.5 us)
Async XLA Ops:
  7.2 39.1 %copy-start.115 = (bf16[64,96]{1,0:T(8,128)(2,1)S(1)}, bf16[64,96]{1,0:T(8,128)(2,1)}, u32[]{:S(2)}) copy-start(bf16[64,96]{1,0:T(8,128)(2,1)} %param.38) | copy-start | bytes 36868
  7.3 191.7 %all-gather.8.cloned.1.call-start = ((), (), s32[]{:S(2)}) async-start(), calls=%async_computation.6 | async-start | bytes 3981312 | tf_op jit(solution)/shard_map/all_gather | solution.py:138
  8.0 70.2 %copy-start.144 = (bf16[8,64]{1,0:T(8,128)(2,1)S(1)}, bf16[8,64]{1,0:T(8,128)(2,1)}, u32[]{:S(2)}) copy-start(bf16[8,64]{1,0:T(8,128)(2,1)} %param.36) | copy-start | bytes 3076
  8.0 96.3 %copy-start.145 = (bf16[33,8]{0,1:T(8,128)(2,1)S(1)}, bf16[33,8]{0,1:T(8,128)(2,1)}, u32[]{:S(2)}) copy-start(bf16[33,8]{0,1:T(8,128)(2,1)} %param.33) | copy-start | bytes 1588
  8.0 122.7 %copy-start.159 = (bf16[96]{0:T(256)(128)(2,1)S(1)}, bf16[96]{0:T(256)(128)(2,1)}, u32[]{:S(2)}) copy-start(bf16[96]{0:T(256)(128)(2,1)} %param.28) | copy-start | bytes 580
  8.0 122.9 %copy-start.160 = (bf16[96]{0:T(256)(128)(2,1)S(1)}, bf16[96]{0:T(256)(128)(2,1)}, u32[]{:S(2)}) copy-start(bf16[96]{0:T(256)(128)(2,1)} %param.27) | copy-start | bytes 580
  8.0 123.1 %copy-start.148 = (bf16[288]{0:T(512)(128)(2,1)S(1)}, bf16[288]{0:T(512)(128)(2,1)}, u32[]{:S(2)}) copy-start(bf16[288]{0:T(512)(128)(2,1)} %param.30) | copy-start | bytes 1732
  8.0 123.3 %copy-start.149 = (bf16[288]{0:T(512)(128)(2,1)S(1)}, bf16[288]{0:T(512)(128)(2,1)}, u32[]{:S(2)}) copy-start(bf16[288]{0:T(512)(128)(2,1)} %param.32) | copy-start | bytes 1732
  8.0 123.6 %copy-start.161 = (bf16[96]{0:T(256)(128)(2,1)S(1)}, bf16[96]{0:T(256)(128)(2,1)}, u32[]{:S(2)}) copy-start(bf16[96]{0:T(256)(128)(2,1)} %param.39) | copy-start | bytes 580
  8.1 123.8 %copy-start.162 = (bf16[8]{0:T(256)(128)(2,1)S(1)}, bf16[8]{0:T(256)(128)(2,1)}, u32[]{:S(2)}) copy-start(bf16[8]{0:T(256)(128)(2,1)} %param.34) | copy-start | bytes 52
  8.1 124.1 %copy-start.163 = (bf16[8]{0:T(256)(128)(2,1)S(1)}, bf16[8]{0:T(256)(128)(2,1)}, u32[]{:S(2)}) copy-start(bf16[8]{0:T(256)(128)(2,1)} %param.37) | copy-start | bytes 52
  8.1 124.3 %copy-start.164 = (bf16[8]{0:T(256)(128)(2,1)S(1)}, bf16[8]{0:T(256)(128)(2,1)}, u32[]{:S(2)}) copy-start(bf16[8]{0:T(256)(128)(2,1)} %param.35) | copy-start | bytes 52
  8.1 124.5 %copy-start.165 = (bf16[96]{0:T(256)(128)(2,1)S(1)}, bf16[96]{0:T(256)(128)(2,1)}, u32[]{:S(2)}) copy-start(bf16[96]{0:T(256)(128)(2,1)} %param.41) | copy-start | bytes 580
  8.1 124.8 %copy-start.166 = (bf16[96]{0:T(256)(128)(2,1)S(1)}, bf16[96]{0:T(256)(128)(2,1)}, u32[]{:S(2)}) copy-start(bf16[96]{0:T(256)(128)(2,1)} %param.47) | copy-start | bytes 580
  8.1 125.0 %copy-start.167 = (bf16[96]{0:T(256)(128)(2,1)S(1)}, bf16[96]{0:T(256)(128)(2,1)}, u32[]{:S(2)}) copy-start(bf16[96]{0:T(256)(128)(2,1)} %param.43) | copy-start | bytes 580
  8.1 125.2 %copy-start.168 = (bf16[96]{0:T(256)(128)(2,1)S(1)}, bf16[96]{0:T(256)(128)(2,1)}, u32[]{:S(2)}) copy-start(bf16[96]{0:T(256)(128)(2,1)} %param.42) | copy-start | bytes 580
  8.1 251.0 %all-gather.10.cloned.1.call-start = ((), (), s32[]{:S(2)}) async-start(), calls=%async_computation.7 | async-start | bytes 1327104 | tf_op jit(solution)/shard_map/all_gather | solution.py:149
  8.9 254.5 %all-gather.12.cloned.1.call-start = ((), (), s32[]{:S(2)}) async-start(), calls=%async_computation.8 | async-start | bytes 5308416 | tf_op jit(solution)/shard_map/all_gather | solution.py:157
  9.6 160.7 %copy-start.150 = (bf16[384]{0:T(512)(128)(2,1)S(1)}, bf16[384]{0:T(512)(128)(2,1)}, u32[]{:S(2)}) copy-start(bf16[384]{0:T(512)(128)(2,1)} %param.45) | copy-start | bytes 2308
  9.6 274.1 %all-gather.14.cloned.1.call-start = ((), (), s32[]{:S(2)}) async-start(), calls=%async_computation.9 | async-start | bytes 5308416 | tf_op jit(solution)/shard_map/all_gather | solution.py:159
  10.2 416.9 %reduce-scatter.13.cloned.1.call-start = ((), (), s32[]{:S(2)}) async-start(), calls=%async_computation.11 | async-start | bytes 2654208 | tf_op jit(solution)/shard_map/reduce_scatter | solution.py:364
  10.3 160.1 %copy-start.85 = (f32[768]{0:T(1024)}, f32[768]{0:T(1024)S(1)}, u32[]{:S(2)}) copy-start(f32[768]{0:T(1024)S(1)} %add_multiply_fusion) | copy-start | bytes 9220
  10.3 160.0 %copy-start.130 = (f32[128]{0:T(128)}, f32[128]{0:T(128)S(1)}, u32[]{:S(2)}) copy-start(f32[128]{0:T(128)S(1)} %multiply_negate_fusion) | copy-start | bytes 1540
  10.4 159.9 %copy-start.132 = (f32[128,1]{0,1:T(1,128)}, f32[128,1]{0,1:T(1,128)S(1)}, u32[]{:S(2)}) copy-start(f32[128,1]{0,1:T(1,128)S(1)} %iota_multiply_fusion.1) | copy-start | bytes 1540
  13.1 360.7 %copy-start.97 = (f32[128]{0:T(128)}, f32[128]{0:T(128)S(1)}, u32[]{:S(2)}) copy-start(f32[128]{0:T(128)S(1)} %get-tuple-element.199) | copy-start | bytes 1540
  13.1 362.0 %copy-start.100 = (f32[128]{0:T(128)}, f32[128]{0:T(128)S(1)}, u32[]{:S(2)}) copy-start(f32[128]{0:T(128)S(1)} %get-tuple-element.198) | copy-start | bytes 1540
  13.4 64.6 %copy-start.151 = (f32[128]{0:T(128)}, f32[128]{0:T(128)S(1)}, u32[]{:S(2)}) copy-start(f32[128]{0:T(128)S(1)} %get-tuple-element.46) | copy-start | bytes 1540
  13.9 359.9 %copy-start.118 = (f32[128]{0:T(128)}, f32[128]{0:T(128)S(1)}, u32[]{:S(2)}) copy-start(f32[128]{0:T(128)S(1)} %fusion.316) | copy-start | bytes 1540
  46.3 328.7 %copy-start.125 = (f32[128]{0:T(128)}, f32[128]{0:T(128)S(1)}, u32[]{:S(2)}) copy-start(f32[128]{0:T(128)S(1)} %fusion.318) | copy-start | bytes 1540
  78.2 120.7 %copy-start.70 = (bf16[768,64]{0,1:T(8,128)(2,1)}, bf16[768,64]{0,1:T(8,128)(2,1)S(1)}, u32[]{:S(2)}) copy-start(bf16[768,64]{0,1:T(8,128)(2,1)S(1)} %reshape.1347) | copy-start | bytes 294916
  104.3 94.6 %copy-start.79 = (bf16[64,64]{1,0:T(8,128)(2,1)}, bf16[64,64]{1,0:T(8,128)(2,1)S(1)}, u32[]{:S(2)}) copy-start(bf16[64,64]{1,0:T(8,128)(2,1)S(1)} %all_gather.51) | copy-start | bytes 24580
  169.3 29.6 %copy-start.76 = (f32[128,64]{0,1:T(8,128)}, f32[128,64]{0,1:T(8,128)S(1)}, u32[]{:S(2)}) copy-start(f32[128,64]{0,1:T(8,128)S(1)} %convolution_add_fusion.16) | copy-start | bytes 98308
  169.7 29.3 %copy-start.72 = (f32[128,64]{0,1:T(8,128)}, f32[128,64]{0,1:T(8,128)S(1)}, u32[]{:S(2)}) copy-start(f32[128,64]{0,1:T(8,128)S(1)} %convolution_add_fusion.15) | copy-start | bytes 98308
  208.6 11.0 copy-start.3
  211.4 8.3 copy-start.5
  234.4 11.3 copy-start.7
  237.2 8.5 copy-start.9
  261.2 38.2 %copy-start.116 = (f32[128]{0:T(128)}, f32[128]{0:T(128)S(1)}, u32[]{:S(2)}) copy-start(f32[128]{0:T(128)S(1)} %broadcast_multiply_fusion.4) | copy-start | bytes 1540
  262.4 37.0 %copy-start.104 = (f32[128]{0:T(128)}, f32[128]{0:T(128)S(1)}, u32[]{:S(2)}) copy-start(f32[128]{0:T(128)S(1)} %broadcast_multiply_fusion.6) | copy-start | bytes 1540
  263.3 36.1 %copy-start.128 = (f32[128]{0:T(128)}, f32[128]{0:T(128)S(1)}, u32[]{:S(2)}) copy-start(f32[128]{0:T(128)S(1)} %fusion.319) | copy-start | bytes 1540
  263.3 36.1 %copy-start.121 = (f32[128]{0:T(128)}, f32[128]{0:T(128)S(1)}, u32[]{:S(2)}) copy-start(f32[128]{0:T(128)S(1)} %fusion.317) | copy-start | bytes 1540
  283.7 10.6 copy-start.48
  283.7 10.7 copy-start.157
  304.7 7.5 copy-start.42
  336.4 9.0 copy-start.43
  347.3 198.9 %reduce-scatter.11.cloned.1.call-start = ((), (), s32[]{:S(2)}) async-start(), calls=%async_computation.10 | async-start | bytes 7962624 | tf_op jit(solution)/shard_map/reduce_scatter | solution.py:353
  347.3 10.3 copy-start.12
  347.3 10.3 copy-start.17
  379.7 333.0 %reduce-scatter.15.cloned.1.call-start = ((), (), s32[]{:S(2)}) async-start(), calls=%async_computation.12 | async-start | bytes 10616832 | tf_op jit(solution)/shard_map/reduce_scatter | solution.py:345
  388.6 490.7 %reduce-scatter.17.cloned.1.call-start = ((), (), s32[]{:S(2)}) async-start(), calls=%async_computation.13 | async-start | bytes 10616832 | tf_op jit(solution)/shard_map/reduce_scatter | solution.py:347
  397.2 549.9 %reduce-scatter.19.cloned.1.call-start = ((), (), s32[]{:S(2)}) async-start(), calls=%async_computation.14 | async-start | bytes 1327104
  406.2 8.6 copy-start.57
  406.3 8.6 copy-start.140
  406.3 8.5 copy-start.142
  413.6 7.4 copy-start.105
  413.6 8.0 copy-start.122
  413.7 8.0 copy-start.123
  413.7 8.6 copy-start.109
  413.7 8.6 copy-start.110
  414.2 614.1 %all-reduce.50.cloned.1.call-start = ((), (), s32[]{:S(2)}) async-start(), calls=%async_computation.16 | async-start | bytes 265216
  414.8 9.6 copy-start.146
  422.9 670.3 %reduce-scatter.21.cloned.1.call-start = ((), (), s32[]{:S(2)}) async-start(), calls=%async_computation.15 | async-start | bytes 442368
  424.4 745.8 %all-reduce.52.cloned.1.call-start = ((), (), s32[]{:S(2)}) async-start(), calls=%async_computation.17 | async-start | bytes 7077888 | tf_op jit(solution)/shard_map/psum | solution.py:367
  424.5 454.9 %copy-start.134 = (f32[768]{0:T(1024)}, f32[768]{0:T(1024)S(1)}, u32[]{:S(2)}) copy-start(f32[768]{0:T(1024)S(1)} %convert_element_type.293) | copy-start | bytes 9220
  (119 other events, 367.2 us)
Sparse Core Ops, SparseCore 0:
  10.3 69.9 all-gather.7
  82.5 39.6 all-gather.9
  124.3 79.1 all-gather.11
  205.6 78.0 all-gather.13
  347.4 67.1 reduce-scatter.12
  418.1 128.0 reduce-scatter.10
  550.2 162.5 reduce-scatter.14
  716.8 162.5 reduce-scatter.16
  883.7 63.3 reduce-scatter.18
  954.7 73.5 all-reduce.49
  1032.2 60.8 reduce-scatter.20
  1095.6 74.5 all-reduce.51
where the time goes:
time: 1190 us; the launch traced here: 1180 us
  waiting for transfers between devices  725 us (61%)
  blocking collectives  190 us (16%)
  matrix products  178 us (15%)
  local copies, waits for them, and re-layouts  39.7 us (3%)
  other arithmetic  27.2 us (2%)
  between operations  21.5 us (2%)
    unnamed x15, waiting for transfers between devices  195 us
    reduce_scatter x1, waiting for transfers between devices, per_device(): lax.psum_scatter(dense_total[2], 'shard', scatter_dimension=0, tiled=True)  167 us
    reduce_scatter x1, waiting for transfers between devices, per_device(): lax.psum_scatter(dense_total[4], 'shard', scatter_dimension=0, tiled=True)  167 us
    reduce_scatter x1, waiting for transfers between devices, per_device(): lax.psum_scatter(mixer_total[2], 'shard', scatter_dimension=0, tiled=True)  119 us
    psum x1, waiting for transfers between devices, per_device(): lax.psum((mixer_total[0], mixer_total[1], mixer_total[2], mixer_total[3],...  64.1 us
    dot_general x6, matrix products, inverse(): jnp.einsum('ft,...fd->...td', cosine, scaled_real, precision=HIGHEST)  37.2 us
    dot_general x6, matrix products, inverse(): jnp.einsum('ft,...fd->...td', sine, scaled_imag, precision=HIGHEST)  36.8 us
    unnamed x1, blocking collectives  34.8 us
  transfers between devices with their start and end apart: 12, of which 8 were waited for; matrix products, arithmetic and copies ran while one was open for 14% of the time, Pallas kernels for 0%

commit v1 on v0

--- a/solution.py
+++ b/solution.py
@@ -4,6 +4,8 @@
 import jax.numpy as jnp
 from jax import lax
 from jax.sharding import PartitionSpec as P
+from jax.experimental import pallas as pl
+from jax.experimental.pallas import tpu as pltpu
 
 DOCS = 6
 
@@ -98,6 +100,732 @@
     scaled_imag = imag_part * weights_row[:, None]
     return jnp.einsum("ft,...fd->...td", cosine, scaled_real, precision=HIGHEST) - jnp.einsum(
         "ft,...fd->...td", sine, scaled_imag, precision=HIGHEST
+    )
+
+
+MESH_ID = pl.DeviceIdType.MESH
+HALF = 48
+WIDE = 768
+GATHER_CHUNKS = (
+    (0, 0, 0, True),
+    (0, 0, 768, True),
+    (0, 0, 1536, True),
+    (1, 0, 0, True),
+    (2, 0, 0, True),
+    (3, 0, 0, False),
+    (2, 1, 0, True),
+    (3, 0, 768, False),
+    (2, 2, 0, True),
+    (3, 0, 1536, False),
+    (2, 3, 0, True),
+    (3, 0, 2304, False),
+)
+REDUCE_CHUNKS = (
+    (2, 0, 0, True),
+    (2, 1, 0, False),
+    (2, 2, 0, True),
+    (2, 3, 0, False),
+    (3, 0, 0, True),
+    (3, 0, 768, False),
+    (3, 0, 1536, True),
+    (3, 0, 2304, False),
+    (1, 0, 0, True),
+    (0, 0, 0, False),
+    (0, 0, 768, True),
+    (0, 0, 1536, False),
+)
+
+
+def place():
+    rep = lax.axis_index("rep")
+    shard = lax.axis_index("shard")
+    return rep, shard, rep // 2, rep % 2, shard // 2, shard % 2
+
+
+def enter(targets):
+    barrier = pltpu.get_barrier_semaphore()
+    for target in targets:
+        pl.semaphore_signal(barrier, inc=1, device_id=target, device_id_type=MESH_ID)
+    pl.semaphore_wait(barrier, len(targets))
+
+
+def gather_kernel(
+    small_ref, in0, in1, in2, in3, small_full, full0, full1, full2, full3,
+    send_sem, recv_sem, small_send, small_recv, own_sem,
+):
+    rep, shard, y, c, z, x = place()
+    shards = (in0, in1, in2, in3)
+    fulls = (full0, full1, full2, full3)
+    across_x = (rep, z * 2 + (1 - x))
+    across_y = ((1 - y) * 2 + c, shard)
+    across_c = (y * 2 + (1 - c), shard)
+
+    def along_z(step):
+        return (rep, ((z + step) % 4) * 2 + x)
+
+    group = [(rep, (shard + step) % 8) for step in range(1, 8)]
+    enter(group + [across_y, across_c])
+
+    def source_of(j):
+        if j < 3:
+            return ((z + 3 - j) % 4) * 2 + x
+        if j == 3:
+            return z * 2 + (1 - x)
+        return ((z + 7 - j) % 4) * 2 + (1 - x)
+
+    def region(ref, chunk, row, half, quarter):
+        matrix, block, column, split = chunk
+        start = pl.multiple_of(row + block * 96 + half * HALF, 16)
+        if split:
+            columns = pl.ds(pl.multiple_of(column + quarter * (WIDE // 2), 128), WIDE // 2)
+        else:
+            columns = pl.ds(column, WIDE)
+        return ref.at[pl.ds(start, HALF), columns]
+
+    def landed(chunk, j, half, quarter):
+        matrix = chunk[0]
+        depth = shards[matrix].shape[0]
+        return region(fulls[matrix], chunk, source_of(j) * depth, half, quarter)
+
+    def copy(index, slot, source, target_ref, device):
+        return pltpu.make_async_remote_copy(
+            src_ref=source, dst_ref=target_ref,
+            send_sem=send_sem.at[index, slot], recv_sem=recv_sem.at[index, slot],
+            device_id=device, device_id_type=MESH_ID,
+        )
+
+    started = []
+    for step in range(1, 8):
+        out = pltpu.make_async_remote_copy(
+            src_ref=small_ref, dst_ref=small_full.at[shard],
+            send_sem=small_send.at[step - 1], recv_sem=small_recv.at[step - 1],
+            device_id=group[step - 1], device_id_type=MESH_ID,
+        )
+        out.start()
+        started.append(out)
+    locals_ = [pltpu.make_async_copy(small_ref, small_full.at[shard], own_sem.at[4])]
+    for matrix in range(4):
+        depth = shards[matrix].shape[0]
+        locals_.append(
+            pltpu.make_async_copy(
+                shards[matrix],
+                fulls[matrix].at[pl.ds(pl.multiple_of(shard * depth, 16), depth)],
+                own_sem.at[matrix],
+            )
+        )
+    for item in locals_:
+        item.start()
+
+    def begin(index, slot, source, target_ref, device):
+        out = copy(index, slot, source, target_ref, device)
+        out.start()
+        started.append(out)
+
+    def arrive(index, slot, target_ref):
+        copy(index, slot, target_ref, target_ref, across_c).wait_recv()
+
+    chunks = GATHER_CHUNKS
+    count = len(chunks)
+
+    def first(index):
+        chunk = chunks[index]
+        matrix = chunk[0]
+        depth = shards[matrix].shape[0]
+        own = region(shards[matrix], chunk, 0, c, y)
+        target_ref = region(fulls[matrix], chunk, shard * depth, c, y)
+        for step in range(1, 4):
+            begin(index, step - 1, own, target_ref, along_z(step))
+        begin(index, 3, own, target_ref, across_x)
+
+    def pass_on(index, j):
+        chunk = chunks[index]
+        piece = landed(chunk, j, c, y)
+        if j < 3:
+            begin(index, 4 + j, piece, piece, across_x)
+        if chunk[3]:
+            begin(index, 7 + j, piece, piece, across_y)
+        begin(index, 14 + j, piece, piece, across_c)
+
+    def second(index):
+        for j in range(4):
+            arrive(index, j, landed(chunks[index], j, c, y))
+            pass_on(index, j)
+
+    def third(index):
+        for j in range(4, 7):
+            arrive(index, j, landed(chunks[index], j, c, y))
+            pass_on(index, j)
+
+    def fourth(index):
+        if chunks[index][3]:
+            for j in range(7):
+                piece = landed(chunks[index], j, c, 1 - y)
+                arrive(index, 7 + j, piece)
+                begin(index, 21 + j, piece, piece, across_c)
+
+    ahead = 3
+    for index in range(min(ahead, count)):
+        first(index)
+    for step in range(count + 2):
+        if step + ahead < count:
+            first(step + ahead)
+        if step < count:
+            second(step)
+        if 0 <= step - 1 < count:
+            third(step - 1)
+        if 0 <= step - 2 < count:
+            fourth(step - 2)
+    for index in range(count):
+        for j in range(7):
+            arrive(index, 14 + j, landed(chunks[index], j, 1 - c, y))
+            if chunks[index][3]:
+                arrive(index, 21 + j, landed(chunks[index], j, 1 - c, 1 - y))
+    for step in range(1, 8):
+        pltpu.make_async_remote_copy(
+            src_ref=small_ref, dst_ref=small_full.at[(shard + 8 - step) % 8],
+            send_sem=small_send.at[step - 1], recv_sem=small_recv.at[step - 1],
+            device_id=group[step - 1], device_id_type=MESH_ID,
+        ).wait_recv()
+    for out in started:
+        out.wait_send()
+    for item in locals_:
+        item.wait()
+
+
+def gather_weights(small, shards):
+    count = len(GATHER_CHUNKS)
+    fulls = [
+        jax.ShapeDtypeStruct((8 * member.shape[0], member.shape[1]), member.dtype)
+        for member in shards
+    ]
+    return pl.pallas_call(
+        gather_kernel,
+        out_shape=[jax.ShapeDtypeStruct((8,) + small.shape, small.dtype)] + fulls,
+        in_specs=[pl.BlockSpec(memory_space=pltpu.VMEM)] * 5,
+        out_specs=[pl.BlockSpec(memory_space=pl.ANY)] * 5,
+        scratch_shapes=[
+            pltpu.SemaphoreType.DMA((count, 28)),
+            pltpu.SemaphoreType.DMA((count, 28)),
+            pltpu.SemaphoreType.DMA((7,)),
+            pltpu.SemaphoreType.DMA((7,)),
+            pltpu.SemaphoreType.DMA((5,)),
+        ],
+        compiler_params=pltpu.CompilerParams(collective_id=0, has_side_effects=True),
+    )(small, *shards)
+
+
+def reduce_kernel(
+    small_ref, in0, in1, in2, in3, small_out, out0, out1, out2, out3,
+    core_buf, y_buf, x_split, x_whole, z_split, z_whole, end_split, end_whole,
+    small_group, small_rep, send_sem, recv_sem, small_send, small_recv,
+):
+    rep, shard, y, c, z, x = place()
+    grads = (in0, in1, in2, in3)
+    outs = (out0, out1, out2, out3)
+    across_x = (rep, z * 2 + (1 - x))
+    across_y = ((1 - y) * 2 + c, shard)
+    across_c = (y * 2 + (1 - c), shard)
+
+    def along_z(step):
+        return (rep, ((z + step) % 4) * 2 + x)
+
+    group = [(rep, (shard + step) % 8) for step in range(1, 8)]
+    reps = [((rep + step) % 4, shard) for step in range(1, 4)]
+    enter(group + reps)
+
+    chunks = REDUCE_CHUNKS
+    count = len(chunks)
+    split_index = []
+    seen = [0, 0]
+    for chunk in chunks:
+        split_index.append(seen[0] if chunk[3] else seen[1])
+        seen[0 if chunk[3] else 1] += 1
+
+    started = []
+
+    def copy(index, slot, source, target_ref, device):
+        return pltpu.make_async_remote_copy(
+            src_ref=source, dst_ref=target_ref,
+            send_sem=send_sem.at[index, slot], recv_sem=recv_sem.at[index, slot],
+            device_id=device, device_id_type=MESH_ID,
+        )
+
+    def begin(index, slot, source, target_ref, device):
+        out = copy(index, slot, source, target_ref, device)
+        out.start()
+        started.append(out)
+
+    def arrive(index, slot, target_ref):
+        copy(index, slot, target_ref, target_ref, across_c).wait_recv()
+
+    def columns_of(chunk):
+        return pl.ds(chunk[2], WIDE)
+
+    def quarter_columns(quarter):
+        return pl.ds(pl.multiple_of(quarter * (WIDE // 2), 128), WIDE // 2)
+
+    def small_copy(kind, step, source, target_ref, device):
+        return pltpu.make_async_remote_copy(
+            src_ref=source, dst_ref=target_ref,
+            send_sem=small_send.at[kind + step - 1], recv_sem=small_recv.at[kind + step - 1],
+            device_id=device, device_id_type=MESH_ID,
+        )
+
+    for step in range(1, 8):
+        out = small_copy(0, step, small_ref.at[(shard + step) % 8], small_group.at[step - 1], group[step - 1])
+        out.start()
+        started.append(out)
+
+    def stage_core(index):
+        chunk = chunks[index]
+        source = grads[chunk[0]].at[:, :, chunk[1], 1 - c, :, columns_of(chunk)]
+        begin(index, 0, source, core_buf.at[index], across_c)
+
+    def add_core(index):
+        chunk = chunks[index]
+        arrive(index, 0, core_buf.at[index])
+
+        def body(position, carry):
+            own = grads[chunk[0]][position // 2, position % 2, chunk[1], c, :, columns_of(chunk)]
+            other = core_buf[index, position // 2, position % 2]
+            core_buf[index, position // 2, position % 2] = (
+                own.astype(jnp.float32) + other.astype(jnp.float32)
+            ).astype(jnp.bfloat16)
+            return carry
+
+        lax.fori_loop(0, 8, body, 0)
+        if chunk[3]:
+            source = core_buf.at[index, :, :, :, quarter_columns(1 - y)]
+            begin(index, 1, source, y_buf.at[split_index[index]], across_y)
+        else:
+            begin(index, 2, core_buf.at[index, :, 1 - x], x_whole.at[split_index[index]], across_x)
+
+    def add_y(index):
+        chunk = chunks[index]
+        if not chunk[3]:
+            return
+        slot = split_index[index]
+        arrive(index, 1, y_buf.at[slot])
+
+        def body(position, carry):
+            own = core_buf[index, position // 2, position % 2, :, quarter_columns(y)]
+            other = y_buf[slot, position // 2, position % 2]
+            y_buf[slot, position // 2, position % 2] = (
+                own.astype(jnp.float32) + other.astype(jnp.float32)
+            ).astype(jnp.bfloat16)
+            return carry
+
+        lax.fori_loop(0, 8, body, 0)
+        begin(index, 2, y_buf.at[slot, :, 1 - x], x_split.at[slot], across_x)
+
+    def add_x(index):
+        chunk = chunks[index]
+        slot = split_index[index]
+        landing = x_split if chunk[3] else x_whole
+        arrive(index, 2, landing.at[slot])
+        ends = z_split if chunk[3] else z_whole
+        for step in (1, 2, 3, 0):
+            row = (z + step) % 4
+            if chunk[3]:
+                own = y_buf[slot, row, x]
+            else:
+                own = core_buf[index, row, x]
+            landing[slot, row] = (
+                own.astype(jnp.float32) + landing[slot, row].astype(jnp.float32)
+            ).astype(jnp.bfloat16)
+            if step > 0:
+                begin(index, 2 + step, landing.at[slot, row], ends.at[slot, step - 1], along_z(step))
+
+    def add_z(index):
+        chunk = chunks[index]
+        slot = split_index[index]
+        landing = x_split if chunk[3] else x_whole
+        ends = z_split if chunk[3] else z_whole
+        last = end_split if chunk[3] else end_whole
+        total = landing[slot, z].astype(jnp.float32)
+        for step in range(1, 4):
+            arrive(index, 2 + step, ends.at[slot, step - 1])
+            total = total + ends[slot, step - 1].astype(jnp.float32)
+        last[slot, 0] = total.astype(jnp.bfloat16)
+        begin(index, 6, last.at[slot, 0], last.at[slot, 1], across_y)
+
+    def finish(index):
+        chunk = chunks[index]
+        matrix, block, column, split = chunk
+        slot = split_index[index]
+        last = end_split if split else end_whole
+        arrive(index, 6, last.at[slot, 1])
+        out = outs[matrix]
+        if split:
+            own_columns = pl.ds(pl.multiple_of(column + y * (WIDE // 2), 128), WIDE // 2)
+            other_columns = pl.ds(pl.multiple_of(column + (1 - y) * (WIDE // 2), 128), WIDE // 2)
+            out[block, c, :, own_columns] = last[slot, 0].astype(jnp.float32)
+            out[block, c, :, other_columns] = last[slot, 1].astype(jnp.float32)
+        else:
+            out[block, c, :, columns_of(chunk)] = last[slot, 0].astype(jnp.float32) + last[
+                slot, 1
+            ].astype(jnp.float32)
+        piece = out.at[block, c, :, columns_of(chunk)]
+        begin(index, 7, piece, piece, across_c)
+
+    ahead = 3
+    for index in range(min(ahead, count)):
+        stage_core(index)
+    for step in range(count + 4):
+        if step + ahead < count:
+            stage_core(step + ahead)
+        if step < count:
+            add_core(step)
+        if 0 <= step - 1 < count:
+            add_y(step - 1)
+        if 0 <= step - 2 < count:
+            add_x(step - 2)
+        if 0 <= step - 3 < count:
+            add_z(step - 3)
+        if 0 <= step - 4 < count:
+            finish(step - 4)
+        if step == 2:
+            partial = small_ref[shard]
+            for hop in range(1, 8):
+                small_copy(0, hop, small_group.at[hop - 1], small_group.at[hop - 1], group[hop - 1]).wait_recv()
+                partial = partial + small_group[hop - 1]
+            small_rep[rep] = partial
+            for hop in range(1, 4):
+                out = small_copy(7, hop, small_rep.at[rep], small_rep.at[rep], reps[hop - 1])
+                out.start()
+                started.append(out)
+    for hop in range(1, 4):
+        landing = small_rep.at[(rep + 4 - hop) % 4]
+        small_copy(7, hop, landing, landing, reps[hop - 1]).wait_recv()
+    small_out[...] = small_rep[0] + small_rep[1] + small_rep[2] + small_rep[3]
+    for index in range(count):
+        chunk = chunks[index]
+        arrive(index, 7, outs[chunk[0]].at[chunk[1], 1 - c, :, columns_of(chunk)])
+    for out in started:
+        out.wait_send()
+
+
+def reduce_gradients(small, grads):
+    count = len(REDUCE_CHUNKS)
+    splits = sum(1 for chunk in REDUCE_CHUNKS if chunk[3])
+    wholes = count - splits
+    half = WIDE // 2
+    low = jnp.bfloat16
+    views = []
+    shapes = []
+    for member in grads:
+        rows, columns = member.shape
+        blocks = rows // (8 * 96)
+        views.append(member.reshape(4, 2, blocks, 2, HALF, columns))
+        shapes.append(jax.ShapeDtypeStruct((blocks, 2, HALF, columns), jnp.float32))
+    results = pl.pallas_call(
+        reduce_kernel,
+        out_shape=[jax.ShapeDtypeStruct(small.shape[1:], jnp.float32)] + shapes,
+        in_specs=[pl.BlockSpec(memory_space=pltpu.VMEM)] * 5,
+        out_specs=[pl.BlockSpec(memory_space=pltpu.VMEM)] * 5,
+        scratch_shapes=[
+            pltpu.VMEM((count, 4, 2, HALF, WIDE), low),
+            pltpu.VMEM((splits, 4, 2, HALF, half), low),
+            pltpu.VMEM((splits, 4, HALF, half), low),
+            pltpu.VMEM((wholes, 4, HALF, WIDE), low),
+            pltpu.VMEM((splits, 3, HALF, half), low),
+            pltpu.VMEM((wholes, 3, HALF, WIDE), low),
+            pltpu.VMEM((splits, 2, HALF, half), low),
+            pltpu.VMEM((wholes, 2, HALF, WIDE), low),
+            pltpu.VMEM((7,) + small.shape[1:], jnp.float32),
+            pltpu.VMEM((4,) + small.shape[1:], jnp.float32),
+            pltpu.SemaphoreType.DMA((count, 8)),
+            pltpu.SemaphoreType.DMA((count, 8)),
+            pltpu.SemaphoreType.DMA((10,)),
+            pltpu.SemaphoreType.DMA((10,)),
+        ],
+        compiler_params=pltpu.CompilerParams(
+            collective_id=1, has_side_effects=True, vmem_limit_bytes=60 * 1024 * 1024
+        ),
+    )(small, *views)
+    flat = [
+        member.reshape(member.shape[0] * 2 * HALF, member.shape[3]) for member in results[1:]
+    ]
+    return results[0], flat
+
+
+def blocked(values, start, size):
+    return lax.slice_in_dim(values, start, start + size, axis=0)
+
+
+def shifted_down(values, lag):
+    if lag == 0:
+        return values
+    return pltpu.roll(values, lag, 0)
+
+
+def conv_forward_kernel(carried_ref, place_ref, taps_ref, out_ref):
+    lags = taps_ref.shape[0]
+    carried = carried_ref[0]
+    length = carried.shape[0]
+    places = jnp.broadcast_to(place_ref[0], carried.shape)
+    total = jnp.zeros_like(carried)
+    for low_lag in range(8):
+        turned = shifted_down(carried, low_lag)
+        for high in range(lags // 8):
+            lag = high * 8 + low_lag
+            skip = high * 8
+            tap = jnp.broadcast_to(taps_ref[lag : lag + 1, :], (length - skip, carried.shape[1]))
+            term = jnp.where(
+                blocked(places, skip, length - skip) >= lag,
+                tap * blocked(turned, 0, length - skip),
+                0.0,
+            )
+            if skip:
+                total = jnp.concatenate(
+                    [blocked(total, 0, skip), blocked(total, skip, length - skip) + term], axis=0
+                )
+            else:
+                total = total + term
+    out_ref[0] = total
+
+
+def conv_backward_kernel(
+    grad_ref, carried_ref, place_ref, left_ref, taps_ref, out_ref, taps_out_ref
+):
+    lags = taps_ref.shape[0]
+    grad = grad_ref[0]
+    carried = carried_ref[0]
+    length = carried.shape[0]
+    lanes = carried.shape[1]
+    places = jnp.broadcast_to(place_ref[0], carried.shape)
+    left = jnp.broadcast_to(left_ref[0], carried.shape)
+    total = jnp.zeros_like(carried)
+    first = pl.program_id(1) == 0
+
+    @pl.when(first)
+    def _():
+        taps_out_ref[...] = jnp.zeros_like(taps_out_ref)
+
+    for low_lag in range(8):
+        turned = grad if low_lag == 0 else pltpu.roll(grad, length - low_lag, 0)
+        for high in range(lags // 8):
+            lag = high * 8 + low_lag
+            skip = high * 8
+            size = length - skip
+            tap = jnp.broadcast_to(taps_ref[lag : lag + 1, :], (size, lanes))
+            moved = jnp.where(
+                blocked(left, 0, size) >= lag, blocked(turned, skip, size), 0.0
+            )
+            term = tap * moved
+            if skip:
+                total = jnp.concatenate(
+                    [blocked(total, 0, size) + term, blocked(total, size, skip)], axis=0
+                )
+            else:
+                total = total + term
+            product = moved * blocked(carried, 0, size)
+            taps_out_ref[lag : lag + 1, :] += jnp.sum(product, axis=0, keepdims=True)
+    out_ref[0] = total
+
+
+def conv_forward(carried, places, taps):
+    count, length, width = carried.shape
+    lags = taps.shape[0]
+    return pl.pallas_call(
+        conv_forward_kernel,
+        grid=(width // 128, count),
+        in_specs=[
+            pl.BlockSpec((1, length, 128), lambda j, i: (i, 0, j)),
+            pl.BlockSpec((1, length, 1), lambda j, i: (i, 0, 0)),
+            pl.BlockSpec((lags, 128), lambda j, i: (0, j)),
+        ],
+        out_specs=pl.BlockSpec((1, length, 128), lambda j, i: (i, 0, j)),
+        out_shape=jax.ShapeDtypeStruct(carried.shape, jnp.float32),
+    )(carried, places, taps)
+
+
+def conv_backward(grad, carried, places, left, taps):
+    count, length, width = carried.shape
+    lags = taps.shape[0]
+    return pl.pallas_call(
+        conv_backward_kernel,
+        grid=(width // 128, count),
+        in_specs=[
+            pl.BlockSpec((1, length, 128), lambda j, i: (i, 0, j)),
+            pl.BlockSpec((1, length, 128), lambda j, i: (i, 0, j)),
+            pl.BlockSpec((1, length, 1), lambda j, i: (i, 0, 0)),
+            pl.BlockSpec((1, length, 1), lambda j, i: (i, 0, 0)),
+            pl.BlockSpec((lags, 128), lambda j, i: (0, j)),
+        ],
+        out_specs=[
+            pl.BlockSpec((1, length, 128), lambda j, i: (i, 0, j)),
+            pl.BlockSpec((lags, 128), lambda j, i: (0, j)),
+        ],
+        out_shape=[
+            jax.ShapeDtypeStruct(carried.shape, jnp.float32),
+            jax.ShapeDtypeStruct((lags, width), jnp.float32),
+        ],
+    )(grad, carried, places, left, taps)
+
+
+def pack_small(members, low):
+    flat = jnp.concatenate([member.reshape(-1).astype(low) for member in members])
+    rows = -(-flat.shape[0] // 128)
+    rows = -(-rows // 16) * 16
+    flat = jnp.concatenate([flat, jnp.zeros((rows * 128 - flat.shape[0],), low)])
+    return flat.reshape(rows, 128)
+
+
+SMALL_AXES = (0, 0, 0, 1, 0, 1, 0, 0, 0, 0, 1, 0, 0, 0, 0, 0, 0)
+
+
+def unpack_small(packed, members):
+    flat = packed.reshape(8, -1)
+    results = []
+    offset = 0
+    for member, axis in zip(members, SMALL_AXES):
+        size = member.size
+        piece = lax.slice_in_dim(flat, offset, offset + size, axis=1)
+        offset += size
+        if member.ndim == 1 or axis == 0:
+            results.append(piece.reshape((8 * member.shape[0],) + member.shape[1:]))
+        else:
+            piece = piece.reshape((8,) + member.shape)
+            results.append(
+                jnp.swapaxes(piece, 0, 1).reshape(member.shape[0], 8 * member.shape[1])
+            )
+    return results
+
+
+def pack_small_gradients(members):
+    rows = []
+    for member, axis in zip(members, SMALL_AXES):
+        if axis == 0:
+            rows.append(member.reshape(8, -1))
+        else:
+            piece = member.reshape(member.shape[0], 8, member.shape[1] // 8)
+            rows.append(jnp.swapaxes(piece, 0, 1).reshape(8, -1))
+    flat = jnp.concatenate(rows, axis=1)
+    height = -(-flat.shape[1] // 1024) * 8
+    flat = jnp.pad(flat, ((0, 0), (0, height * 128 - flat.shape[1])))
+    return flat.reshape(8, height, 128)
+
+
+def unpack_small_gradients(packed, members):
+    flat = packed.reshape(-1)
+    results = []
+    offset = 0
+    for member in members:
+        results.append(lax.slice_in_dim(flat, offset, offset + member.size).reshape(member.shape))
+        offset += member.size
+    return results
+
+
+LAGS = 64
+
+
+def block_device(
+    tokens, segment_ids, cotangent, first_gain, first_shift, input_weight, input_bias,
+    short_weight, short_bias, inner_weight, inner_bias, sine_scale, middle_weight, middle_bias,
+    filter_weight, direct_gain, output_weight, output_bias, second_gain, second_shift,
+    expand_weight, expand_bias, contract_weight, contract_bias,
+):
+    count, sequences, length, width = tokens.shape
+    blocks = count * sequences
+    row_count = blocks * length
+    small_members = (
+        first_gain, first_shift, input_bias, short_weight, short_bias, inner_weight, inner_bias,
+        sine_scale, middle_weight, middle_bias, filter_weight, direct_gain, output_bias,
+        second_gain, second_shift, expand_bias, contract_bias,
+    )
+    small_all, w_in, w_out, w_con, w_exp = gather_weights(
+        pack_small(small_members, jnp.bfloat16),
+        (input_weight, output_weight, contract_weight, expand_weight),
+    )
+    (
+        g_first, s_first, b_in, w_short, b_short, w_inner, b_inner, scale, w_middle, b_middle,
+        w_filter, direct, b_out, g_second, s_second, b_exp, b_con,
+    ) = [to_float(member) for member in unpack_small(small_all, small_members)]
+
+    def taps_of(*parts):
+        return filter_taps(*parts, length)[:LAGS]
+
+    filter_parts = (w_inner, b_inner, scale, w_middle, b_middle, w_filter)
+    taps, taps_pull = jax.vjp(taps_of, *filter_parts)
+    segments = segment_ids.reshape(blocks, length)
+    same = segments[:, :, None] == segments[:, None, :]
+    index = jnp.arange(length, dtype=jnp.int32)
+    places = jnp.sum(same & (index[None, None, :] < index[None, :, None]), axis=2, dtype=jnp.int32)
+    left = jnp.sum(same & (index[None, None, :] > index[None, :, None]), axis=2, dtype=jnp.int32)
+    places = places[:, :, None]
+    left = left[:, :, None]
+    flat_tokens = tokens.reshape(row_count, width).astype(jnp.float32)
+    upstream = cotangent.reshape(row_count, width)
+    upstream_float = upstream.astype(jnp.float32)
+
+    normed, first_pull = jax.vjp(normalize, flat_tokens, g_first, s_first)
+    normed_first = normed.astype(jnp.bfloat16)
+    projected = jnp.dot(normed_first, w_in, preferred_element_type=jnp.float32) + b_in
+    projected_rows = projected.reshape(blocks, length, 3 * width)
+    short_out, short_pull = jax.vjp(
+        lambda rows_in, taps_in, offset_in: short_filter(rows_in, segments, taps_in, offset_in),
+        projected_rows, w_short, b_short,
+    )
+    gate_out = short_out[:, :, :width]
+    gate_in = short_out[:, :, width : 2 * width]
+    values = short_out[:, :, 2 * width :]
+    carried = values * gate_in
+    convolved = conv_forward(carried, places, taps) + direct * carried
+    gated_low = (convolved * gate_out).astype(jnp.bfloat16).reshape(row_count, width)
+    residual = flat_tokens + jnp.dot(gated_low, w_out, preferred_element_type=jnp.float32) + b_out
+    normed, second_pull = jax.vjp(normalize, residual, g_second, s_second)
+    normed_second = normed.astype(jnp.bfloat16)
+    hidden_pre = jnp.dot(normed_second, w_exp, preferred_element_type=jnp.float32) + b_exp
+    hidden, gelu_pull = jax.vjp(smooth_gate, hidden_pre)
+    hidden_post = hidden.astype(jnp.bfloat16)
+    result = residual + jnp.dot(hidden_post, w_con, preferred_element_type=jnp.float32) + b_con
+    result = result.astype(jnp.bfloat16).reshape(tokens.shape)
+
+    def product(left_side, right_side, dims):
+        return lax.dot_general(
+            left_side, right_side, ((dims[:1], dims[1:]), ((), ())),
+            preferred_element_type=jnp.float32,
+        )
+
+    d_con = product(hidden_post, upstream, (0, 0)).astype(jnp.bfloat16)
+    back_hidden = product(upstream, w_con, (1, 1))
+    back_pre = gelu_pull(back_hidden)[0].astype(jnp.bfloat16)
+    d_exp = product(normed_second, back_pre, (0, 0)).astype(jnp.bfloat16)
+    back_second = product(back_pre, w_exp, (1, 1))
+    back_norm, d_g_second, d_s_second = second_pull(back_second)
+    back_residual = upstream_float + back_norm
+    back_mixed = back_residual.astype(jnp.bfloat16)
+    d_out = product(gated_low, back_mixed, (0, 0)).astype(jnp.bfloat16)
+    back_gated = product(back_mixed, w_out, (1, 1)).reshape(blocks, length, width)
+    back_conv = back_gated * gate_out
+    back_carried, d_taps = conv_backward(back_conv, carried, places, left, taps)
+    back_carried = back_carried + direct * back_conv
+    back_short = jnp.concatenate(
+        [back_gated * convolved, back_carried * values, back_carried * gate_in], axis=2
+    )
+    back_projected, d_w_short, d_b_short = short_pull(back_short)
+    back_projected = back_projected.reshape(row_count, 3 * width).astype(jnp.bfloat16)
+    d_in = product(normed_first, back_projected, (0, 0)).astype(jnp.bfloat16)
+    back_first = product(back_projected, w_in, (1, 1))
+    back_norm, d_g_first, d_s_first = first_pull(back_first)
+    token_delta = (back_residual + back_norm).reshape(tokens.shape)
+    filter_deltas = taps_pull(d_taps)
+    small_deltas = (
+        d_g_first, d_s_first, jnp.sum(to_float(back_projected), axis=0), d_w_short, d_b_short,
+        filter_deltas[0], filter_deltas[1], filter_deltas[2], filter_deltas[3], filter_deltas[4],
+        filter_deltas[5], jnp.sum(back_conv * carried, axis=(0, 1)),
+        jnp.sum(to_float(back_mixed), axis=0), d_g_second, d_s_second,
+        jnp.sum(to_float(back_pre), axis=0), jnp.sum(upstream_float, axis=0),
+    )
+    small_sum, (s_in, s_out, s_con, s_exp) = reduce_gradients(
+        pack_small_gradients(small_deltas), (d_in, d_out, d_con, d_exp)
+    )
+    done = unpack_small_gradients(small_sum, small_members)
+    return (
+        result, token_delta, done[0], done[1], s_in, done[2], done[3], done[4], done[5], done[6],
+        done[7], done[8], done[9], done[10], done[11], s_out, done[12], done[13], done[14], s_exp,
+        done[15], s_con, done[16],
     )
 
 
@@ -420,8 +1148,9 @@
         P("shard", None),
         P("shard"),
     )
+    blocked_mesh = dict(mesh.shape) == {"rep": 4, "shard": 8}
     return jax.shard_map(
-        per_device,
+        block_device if blocked_mesh else per_device,
         mesh=mesh,
         in_specs=placed,
         out_specs=(

time: 1190 us -> 318 us (0.27)
  waiting for transfers between devices: 725 us -> 0 us
  Pallas kernels: 0 us -> 197 us
  blocking collectives: 190 us -> 0 us
  matrix products: 178 us -> 39.3 us
  between operations: 21.5 us -> 1.8 us
  local copies, waits for them, and re-layouts: 39.7 us -> 52.9 us
    reduce_scatter x4 -> x0, waiting for transfers between devices: 452 us -> none  [the longest x1 167 us: per_device(): lax.psum_scatter(dense_total[2], 'shard', scatter_dimension=0, tiled=True)]
    pallas_call x0 -> x4, Pallas kernels: none -> 197 us  [the longest x1 94.9 us: reduce_gradients(): pl.pallas_call(reduce_kernel, out_shape=[jax.ShapeDtypeStruct(small.shape...]
    unnamed x15 -> x0, waiting for transfers between devices: 195 us -> none
    all_gather x5 -> x0, blocking collectives: 143 us -> none  [the longest x1 32.3 us: fetch_mixer(): lax.all_gather(short_weight, 'shard', axis=1, tiled=True)]
    dot_general x46 -> x12, matrix products: 173 us -> 32 us  [the longest x8 21.1 us: product(): lax.dot_general(left_side, right_side, ((dims[:1], dims[1:]), ((), ())),...]
    psum x1 -> x0, waiting for transfers between devices: 64.1 us -> none  [per_device(): lax.psum((mixer_total[0], mixer_total[1], mixer_total[2], mixer_total[3],...]
    unnamed x1 -> x0, blocking collectives: 34.8 us -> none
    unnamed x392 -> x185, local copies, waits for them, and re-layouts: 32.5 us -> 13.8 us
  transfers between devices with their start and end apart: 12 -> 0, of which waited for: 8 -> 0; matrix products, arithmetic and copies ran while one was open for 14% -> 0% of each run, Pallas kernels for 0% -> 0%
where the time goes in v1:
time: 318 us; the launch traced here: 315 us
  Pallas kernels  197 us (62%)
  local copies, waits for them, and re-layouts  52.9 us (17%)
  matrix products  39.3 us (12%)
  other arithmetic  24.2 us (8%)
    pallas_call x1, Pallas kernels, reduce_gradients(): pl.pallas_call(reduce_kernel, out_shape=[jax.ShapeDtypeStruct(small.shape...  94.9 us
    pallas_call x1, Pallas kernels, gather_weights(): pl.pallas_call(gather_kernel, out_shape=[jax.ShapeDtypeStruct((8,) + smal...  80.3 us
    dot_general x8, matrix products, product(): lax.dot_general(left_side, right_side, ((dims[:1], dims[1:]), ((), ())),...  21.1 us
    unnamed x185, local copies, waits for them, and re-layouts  13.8 us
    pallas_call x1, Pallas kernels, conv_backward(): pl.pallas_call(conv_backward_kernel, grid=(width // 128, count), in_specs...  12.3 us
    pallas_call x1, Pallas kernels, conv_forward(): pl.pallas_call(conv_forward_kernel, grid=(width // 128, count), in_specs=...  9.71 us
    concatenate x1, local copies, waits for them, and re-layouts, pack_small(): jnp.concatenate([flat, jnp.zeros((rows * 128 - flat.shape[0],), low)])  9.45 us
    slice x9, local copies, waits for them, and re-layouts, unpack_small_gradients(): lax.slice_in_dim(flat, offset, offset + member.size).reshape(member.shape)  8.83 us

profile of v1, /device:TPU:0, one launch (start us, length us, event | category | flops | bytes accessed | tf_op | source)
XLA Modules:
  0.0 315.4 jit_solution(16538214783609068278)
XLA Ops:
  0.7 0.8 reshape.536
  1.5 0.8 copy.90
  2.4 0.8 reshape.538
  3.1 0.8 reshape.539
  4.0 9.5 %concatenate.33 = bf16[10240]{0:T(1024)(128)(2,1)} concatenate(bf16[96]{0:T(256)(128)(2,1)} %param.27, bf16[96]{0:T(256)(128)(2,1)} %param.28, bf16[288]{0:T(512)(128)(2,1)} %param.30, bf16[864]{0:T(1024)(128)(2,1)S(1)} %reshape.536, bf16[288]{0:T(512)(128)(2,1)} %param.32, bf16[264]{0:T(512)(128)(2,1)S(1)} %reshape.537, bf16[8]{0:T(256)(128)(2,1)} %param.34, ...), dimensions={0} | concatenate | bytes 40960 | tf_op jit(solution)/shard_map/concatenate | solution.py:671
  13.4 80.3 %shard_map.407 = (bf16[8,80,128]{2,1,0:T(8,128)(2,1)}, bf16[768,2304]{1,0:T(8,128)(2,1)}, bf16[768,768]{1,0:T(8,128)(2,1)}, bf16[3072,768]{1,0:T(8,128)(2,1)}, bf16[768,3072]{1,0:T(8,128)(2,1)}) custom-call(bf16[80,128]{1,0:T(8,128)(2,1)} %bitcast.156, bf16[96,2304]{1,0:T(8,128)(2,1)} %in0.1, bf16[96,768]{1,0:T(8,128)(2,1)} %in1.1, bf16[384,768]{1,0:T(8,128)(2,1)} %in2.1, ...), custom_call_target="tpu_custom_call" | custom-call | tf_op jit(solution)/shard_map/pallas_call | solution.py:301
  93.7 1.0 copy.109
  96.8 3.1 convolution_add_fusion
  100.6 1.1 multiply_add_fusion
  101.7 1.4 copy-done
  103.1 1.0 slice_multiply_fusion.4.carried_ref
  104.8 0.8 copy.93.place_ref
  107.1 1.1 reshape.548
  111.3 9.7 %shard_map.408 = f32[2,128,768]{2,1,0:T(8,128)} custom-call(f32[2,128,768]{2,1,0:T(8,128)} %slice_multiply_fusion.4.carried_ref, s32[2,128,1]{2,1,0:T(8,128)} %copy.93.place_ref, f32[64,768]{1,0:T(8,128)} %slice_multiply_fusion.6.taps_ref), custom_call_target="tpu_custom_call" | custom-call | tf_op jit(solution)/shard_map/pallas_call | solution.py:630
  121.1 2.1 multiply_convert_fusion.1
  123.3 1.1 fusion.46
  124.4 1.4 reshape.599
  125.8 1.3 slice_convert_fusion.1
  127.1 1.3 reshape.598
  128.4 1.4 reshape.597
  129.7 0.8 reshape.596
  131.4 4.0 %convolution_add_fusion.1 = f32[256,3072]{1,0:T(8,128)S(1)} fusion(bf16[768,3072]{1,0:T(8,128)(2,1)} %get-tuple-element.38, f32[3072]{0:T(1024)} %reshape.598, f32[256,768]{1,0:T(8,128)S(1)} %get-tuple-element.230, f32[768]{0:T(1024)} %reshape.597, f32[768]{0:T(1024)S(1)} %reshape.596, f32[256]{0:T(256)S(1)} %fusion.32, f32[256]{0:T(256)S(1)} %broadcast_multiply_fusion.2), kind=kOutput, calls=%fused_computation.7 | convolution fusion | flops 1209729024 | bytes 8671232 | tf_op jit(solution)/shard_map/dot_general | solution.py:779
  135.5 2.7 fusion.10
  138.2 3.7 %convert_reduce_fusion = (f32[3072]{0:T(1024)}, bf16[256,3072]{1,0:T(8,128)(2,1)S(1)}) fusion(f32[256,3072]{1,0:T(8,128)S(1)} %convolution_add_fusion.1, bf16[3072,768]{1,0:T(8,128)(2,1)S(1)} %bitcast.166, bf16[256,768]{1,0:T(8,128)(2,1)S(1)} %bitcast.126), kind=kOutput, calls=%fused_computation.15 | convolution fusion | flops 1225257984 | bytes 9842688 | tf_op jit(solution)/shard_map/dot_general | solution.py:786
  141.9 2.1 multiply_reduce_fusion.2
  144.5 0.8 copy-done.6
  145.3 0.8 convert_reduce_fusion.3
  146.1 0.8 copy-done.13
  147.4 2.0 multiply_reduce_fusion.3
  149.4 1.5 copy.95.left_ref
  150.8 12.3 %shard_map.409 = (f32[2,128,768]{2,1,0:T(8,128)}, f32[64,768]{1,0:T(8,128)}) custom-call(f32[2,128,768]{2,1,0:T(8,128)} %get-tuple-element.183.grad_ref, f32[2,128,768]{2,1,0:T(8,128)} %slice_multiply_fusion.4.carried_ref, s32[2,128,1]{2,1,0:T(8,128)} %copy.93.place_ref, s32[2,128,1]{2,1,0:T(8,128)} %copy.95.left_ref, f32[64,768]{1,0:T(8,128)} %slice_multiply_fusion.6.taps_ref), custom_call_target="tpu_custom_call" | custom-call | tf_op jit(solution)/shard_map/pallas_call | solution.py:646
  163.2 2.1 slice_multiply_fusion.5
  165.4 1.6 multiply_reduce_fusion.1
  168.0 1.3 convert_reduce_fusion.1
  170.0 1.7 fusion.40
  171.8 1.0 multiply_reduce_fusion.4
  172.8 1.3 add_add_fusion.2
  174.1 1.3 reshape.554
  175.4 1.3 reshape.555
  177.4 1.9 fusion.7
  179.7 0.8 reshape.559
  180.5 1.5 convolution_multiply_fusion.1
  182.0 1.2 multiply_reduce_fusion.9
  183.2 0.9 convolution_bitcast_fusion.1
  184.6 1.1 fusion.20
  185.8 1.5 fusion.14
  188.4 0.8 copy.108
  189.9 0.9 add_convert_fusion.1
  190.9 3.0 convolution_convert_fusion.2
  193.9 1.5 convolution_convert_fusion.3
  195.4 4.4 %convolution_convert_fusion.1 = bf16[3072,768]{1,0:T(8,128)(2,1)} fusion(bf16[256,768]{1,0:T(8,128)(2,1)S(1)} %bitcast.127, f32[256,3072]{1,0:T(8,128)S(1)} %copy-done.83), kind=kOutput, calls=%fused_computation.1 | convolution fusion | flops 1217396736 | bytes 8257536 | tf_op jit(solution)/shard_map/dot_general | solution.py:786
  199.8 4.1 %convolution_convert_fusion = bf16[768,3072]{1,0:T(8,128)(2,1)} fusion(bf16[256,3072]{1,0:T(8,128)(2,1)S(1)} %copy-done.21, f32[256,768]{1,0:T(8,128)S(1)} %get-tuple-element.230, f32[768]{0:T(1024)S(1)} %copy-done.36, f32[768]{0:T(1024)S(1)} %reshape.596, f32[256]{0:T(256)S(1)} %copy-done.66, f32[256]{0:T(256)S(1)} %copy-done.53), kind=kOutput, calls=%fused_computation | convolution fusion | flops 1211301888 | bytes 7086080 | tf_op jit(solution)/shard_map/dot_general | solution.py:786
  203.9 94.9 %shard_map.410 = (f32[80,128]{1,0:T(8,128)}, f32[1,2,48,2304]{3,2,1,0:T(8,128)}, f32[1,2,48,768]{3,2,1,0:T(8,128)}, f32[4,2,48,768]{3,2,1,0:T(8,128)}, f32[1,2,48,3072]{3,2,1,0:T(8,128)}) custom-call(f32[8,80,128]{2,1,0:T(8,128)} %bitcast.131, bf16[4,2,1,2,48,2304]{5,4,3,2,1,0:T(8,128)(2,1)} %bitcast.117, bf16[4,2,1,2,48,768]{5,4,3,2,1,0:T(8,128)(2,1)} %bitcast.122, ...), custom_call_target="tpu_custom_call" | custom-call | tf_op jit(solution)/shard_map/pallas_call | solution.py:521
  298.8 1.4 fusion.43
  300.3 1.3 fusion.45
  301.6 0.8 slice.222
  303.1 1.1 slice.178
  304.9 1.3 fusion.44
  306.2 0.8 slice.227
  307.7 0.8 slice.184
  309.1 1.3 slice_bitcast_fusion
  310.4 2.2 copy.114
  313.3 1.0 copy.116
  314.3 1.0 copy.117
  (267 shorter events, 18.3 us)
Async XLA Ops:
  0.7 94.9 %copy-start.2 = (bf16[2,1,128,768]{3,2,1,0:T(8,128)(2,1)S(1)}, bf16[2,1,128,768]{3,2,1,0:T(8,128)(2,1)}, u32[]{:S(2)}) copy-start(bf16[2,1,128,768]{3,2,1,0:T(8,128)(2,1)} %param.24) | copy-start | bytes 1179652
  94.7 14.0 %copy-start.24 = (bf16[1,8,80,128]{3,1,2,0:T(8,128)(2,1)}, bf16[1,8,80,128]{3,1,2,0:T(8,128)(2,1)S(1)}, u32[]{:S(2)}) copy-start(bf16[1,8,80,128]{3,1,2,0:T(8,128)(2,1)S(1)} %copy.109) | copy-start | bytes 491524
  96.8 3.1 copy-start.51
  106.4 14.6 %copy-start.63 = (f32[8,96]{1,0:T(8,128)S(1)}, f32[8,96]{1,0:T(8,128)}, u32[]{:S(2)}) copy-start(f32[8,96]{1,0:T(8,128)} %get-tuple-element.203) | copy-start | bytes 9220
  108.2 15.0 %copy-start.25 = (bf16[64,768]{1,0:T(8,128)(2,1)}, bf16[64,768]{1,0:T(8,128)(2,1)S(1)}, u32[]{:S(2)}) copy-start(bf16[64,768]{1,0:T(8,128)(2,1)S(1)} %reshape.548) | copy-start | bytes 294916
  108.4 14.8 %copy-start.40 = (bf16[64,64]{1,0:T(8,128)(2,1)}, bf16[64,64]{1,0:T(8,128)(2,1)S(1)}, u32[]{:S(2)}) copy-start(bf16[64,64]{1,0:T(8,128)(2,1)S(1)} %reshape.546) | copy-start | bytes 24580
  109.0 14.2 %copy-start.80 = (f32[128,1]{0,1:T(1,128)}, f32[128,1]{0,1:T(1,128)S(1)}, u32[]{:S(2)}) copy-start(f32[128,1]{0,1:T(1,128)S(1)} %iota_multiply_fusion.1) | copy-start | bytes 1540
  109.2 14.0 %copy-start.28 = (f32[128,64]{0,1:T(8,128)}, f32[128,64]{0,1:T(8,128)S(1)}, u32[]{:S(2)}) copy-start(f32[128,64]{0,1:T(8,128)S(1)} %convolution_add_fusion.5) | copy-start | bytes 98308
  109.7 13.6 %copy-start.67 = (f32[64]{0:T(128)}, f32[64]{0:T(128)S(1)}, u32[]{:S(2)}) copy-start(f32[64]{0:T(128)S(1)} %reshape.591) | copy-start | bytes 772
  110.0 13.2 %copy-start.27 = (f32[128,64]{0,1:T(8,128)}, f32[128,64]{0,1:T(8,128)S(1)}, u32[]{:S(2)}) copy-start(f32[128,64]{0,1:T(8,128)S(1)} %convolution_add_fusion.4) | copy-start | bytes 98308
  121.1 2.2 copy-start.41
  121.1 2.2 copy-start.11
  131.2 12.9 %copy-start.52 = (f32[256]{0:T(256)}, f32[256]{0:T(256)S(1)}, u32[]{:S(2)}) copy-start(f32[256]{0:T(256)S(1)} %broadcast_multiply_fusion.2) | copy-start | bytes 3076
  131.2 4.2 %slice-start.2 = ((s8[4718592]{0:T(1024)(128)(4,1)}), s8[4194304]{0:T(1024)(128)(4,1)S(1)}, s32[]{:S(2)}) async-start(s8[4718592]{0:T(1024)(128)(4,1)} %bitcast.165), calls=%async_computation.2 | async-start | bytes 8388608
  131.4 12.7 %copy-start.65 = (f32[256]{0:T(256)}, f32[256]{0:T(256)S(1)}, u32[]{:S(2)}) copy-start(f32[256]{0:T(256)S(1)} %fusion.32) | copy-start | bytes 3076
  131.4 4.0 %copy-start.78 = (f32[768]{0:T(1024)S(1)}, f32[768]{0:T(1024)}, u32[]{:S(2)}) copy-start(f32[768]{0:T(1024)} %reshape.599) | copy-start | bytes 9220
  131.4 4.0 %slice-start.3 = ((s8[4718592]{0:T(1024)(128)(4,1)}), s8[524288]{0:T(1024)(128)(4,1)S(1)}, s32[]{:S(2)}) async-start(s8[4718592]{0:T(1024)(128)(4,1)} %bitcast.165), calls=%async_computation.3 | async-start | bytes 1048576
  135.4 2.7 copy-start.82
  135.4 2.7 copy-start.15
  135.5 6.5 %slice-start = ((s8[4718592]{0:T(1024)(128)(4,1)}), s8[4194304]{0:T(1024)(128)(4,1)S(1)}, s32[]{:S(2)}) async-start(s8[4718592]{0:T(1024)(128)(4,1)} %bitcast.163), calls=%async_computation | async-start | bytes 8388608
  138.2 3.7 %slice-start.1 = ((s8[4718592]{0:T(1024)(128)(4,1)}), s8[524288]{0:T(1024)(128)(4,1)S(1)}, s32[]{:S(2)}) async-start(s8[4718592]{0:T(1024)(128)(4,1)} %bitcast.163), calls=%async_computation.1 | async-start | bytes 1048576
  141.9 2.1 copy-start.20
  144.0 2.8 copy-start.12
  144.4 2.9 copy-start.1
  144.4 2.9 copy-start.8
  144.4 2.9 copy-start.42
  163.1 2.2 copy-start.3
  163.1 2.2 copy-start.73
  163.2 2.2 copy-start.75
  165.3 2.6 copy-start.4
  165.3 2.6 copy-start.5
  168.0 2.0 copy-start.81
  169.2 2.5 copy-start.9
  170.0 1.8 copy-start.57
  170.0 2.8 copy-start.7
  170.0 2.8 copy-start.16
  170.0 2.8 copy-start.71
  171.7 5.0 %copy-start.43 = (f32[2304]{0:T(1024)S(1)}, f32[2304]{0:T(1024)}, u32[]{:S(2)}) copy-start(f32[2304]{0:T(1024)} %get-tuple-element.188) | copy-start | bytes 27652
  177.4 2.0 copy-start.45
  177.4 2.0 copy-start.44
  177.4 3.1 copy-start.50
  177.4 5.8 %copy-start.38 = (f32[128,16]{0,1:T(8,128)S(1)}, f32[128,16]{0,1:T(8,128)}, u32[]{:S(2)}) copy-start(f32[128,16]{0,1:T(8,128)} %copy-done.37) | copy-start | bytes 24580
  179.3 8.5 %copy-start.64 = (f32[768]{0:T(1024)S(1)}, f32[768]{0:T(1024)}, u32[]{:S(2)}) copy-start(f32[768]{0:T(1024)} %get-tuple-element.182) | copy-start | bytes 9220
  179.3 8.5 %copy-start.58 = (f32[768]{0:T(1024)S(1)}, f32[768]{0:T(1024)}, u32[]{:S(2)}) copy-start(f32[768]{0:T(1024)} %get-tuple-element.180) | copy-start | bytes 9220
  179.3 8.6 %copy-start.77 = (f32[768]{0:T(1024)S(1)}, f32[768]{0:T(1024)}, u32[]{:S(2)}) copy-start(f32[768]{0:T(1024)} %get-tuple-element.162) | copy-start | bytes 9220
  179.3 8.7 %copy-start.76 = (f32[768]{0:T(1024)S(1)}, f32[768]{0:T(1024)}, u32[]{:S(2)}) copy-start(f32[768]{0:T(1024)} %get-tuple-element.166) | copy-start | bytes 9220
  179.3 8.7 %copy-start.68 = (f32[3072]{0:T(1024)S(1)}, f32[3072]{0:T(1024)}, u32[]{:S(2)}) copy-start(f32[3072]{0:T(1024)} %get-tuple-element.234) | copy-start | bytes 36868
  179.3 8.7 %copy-start.17 = (bf16[2,1,128,768]{3,2,1,0:T(8,128)(2,1)S(1)}, bf16[2,1,128,768]{3,2,1,0:T(8,128)(2,1)}, u32[]{:S(2)}) copy-start(bf16[2,1,128,768]{3,2,1,0:T(8,128)(2,1)} %param.26) | copy-start | bytes 1179652
  179.4 8.9 %copy-start.46 = (f32[8,288]{1,0:T(8,128)S(1)}, f32[8,288]{1,0:T(8,128)}, u32[]{:S(2)}) copy-start(f32[8,288]{1,0:T(8,128)} %reshape.556) | copy-start | bytes 27652
  179.4 8.9 %copy-start.59 = (f32[8,96]{1,0:T(8,128)S(1)}, f32[8,96]{1,0:T(8,128)}, u32[]{:S(2)}) copy-start(f32[8,96]{1,0:T(8,128)} %reshape.554) | copy-start | bytes 9220
  179.4 8.9 %copy-start.60 = (f32[8,96]{1,0:T(8,128)S(1)}, f32[8,96]{1,0:T(8,128)}, u32[]{:S(2)}) copy-start(f32[8,96]{1,0:T(8,128)} %reshape.555) | copy-start | bytes 9220
  184.3 5.6 %copy-start.35 = (f32[768]{0:T(1024)S(1)}, f32[768]{0:T(1024)}, u32[]{:S(2)}) copy-start(f32[768]{0:T(1024)} %copy-done.33) | copy-start | bytes 9220
  184.3 5.6 %copy-start.48 = (f32[768]{0:T(1024)S(1)}, f32[768]{0:T(1024)}, u32[]{:S(2)}) copy-start(f32[768]{0:T(1024)} %copy-done.47) | copy-start | bytes 9220
  187.4 3.4 %copy-start.10 = (bf16[2,128,2304]{2,1,0:T(8,128)(2,1)S(1)}, bf16[2,128,2304]{2,1,0:T(8,128)(2,1)}, u32[]{:S(2)}) copy-start(bf16[2,128,2304]{2,1,0:T(8,128)(2,1)} %copy-done.9) | copy-start | bytes 3538948
  190.8 3.0 copy-start.14
  190.8 3.0 copy-start.19
  190.8 4.5 %copy-start.83 = (f32[256,3072]{1,0:T(8,128)S(1)}, f32[256,3072]{1,0:T(8,128)}, u32[]{:S(2)}) copy-start(f32[256,3072]{1,0:T(8,128)} %copy-done.82) | copy-start | bytes 9437188
  195.4 4.4 %copy-start.21 = (bf16[256,3072]{1,0:T(8,128)(2,1)S(1)}, bf16[256,3072]{1,0:T(8,128)(2,1)}, u32[]{:S(2)}) copy-start(bf16[256,3072]{1,0:T(8,128)(2,1)} %copy-done.20) | copy-start | bytes 4718596
  195.4 4.4 %copy-start.36 = (f32[768]{0:T(1024)S(1)}, f32[768]{0:T(1024)}, u32[]{:S(2)}) copy-start(f32[768]{0:T(1024)} %reshape.597) | copy-start | bytes 9220
  195.4 4.4 %copy-start.53 = (f32[256]{0:T(256)S(1)}, f32[256]{0:T(256)}, u32[]{:S(2)}) copy-start(f32[256]{0:T(256)} %copy-done.52) | copy-start | bytes 3076
  195.4 4.4 %copy-start.66 = (f32[256]{0:T(256)S(1)}, f32[256]{0:T(256)}, u32[]{:S(2)}) copy-start(f32[256]{0:T(256)} %copy-done.65) | copy-start | bytes 3076
  298.8 13.8 %copy-start.26 = (f32[1,2,48,768]{3,2,1,0:T(8,128)S(1)}, f32[1,2,48,768]{3,2,1,0:T(8,128)}, u32[]{:S(2)}) copy-start(f32[1,2,48,768]{3,2,1,0:T(8,128)} %get-tuple-element.44) | copy-start | bytes 884740
  298.8 14.5 %copy-start.23 = (f32[1,2,48,3072]{3,2,1,0:T(8,128)S(1)}, f32[1,2,48,3072]{3,2,1,0:T(8,128)}, u32[]{:S(2)}) copy-start(f32[1,2,48,3072]{3,2,1,0:T(8,128)} %get-tuple-element.45) | copy-start | bytes 3538948
  310.4 4.0 %copy-start.22 = (f32[4,2,48,768]{3,2,1,0:T(8,128)S(1)}, f32[4,2,48,768]{3,2,1,0:T(8,128)}, u32[]{:S(2)}) copy-start(f32[4,2,48,768]{3,2,1,0:T(8,128)} %get-tuple-element.46) | copy-start | bytes 3538948
  (24 other events, 24.9 us)

commit v2 on v0

--- a/solution.py
+++ b/solution.py
@@ -2,7 +2,10 @@
 
 import jax
 import jax.numpy as jnp
+import numpy as np
 from jax import lax
+from jax.experimental import pallas as pl
+from jax.experimental.pallas import tpu as pltpu
 from jax.sharding import PartitionSpec as P
 
 DOCS = 6
@@ -99,6 +102,1033 @@
     return jnp.einsum("ft,...fd->...td", cosine, scaled_real, precision=HIGHEST) - jnp.einsum(
         "ft,...fd->...td", sine, scaled_imag, precision=HIGHEST
     )
+
+
+MESH_ID = pl.DeviceIdType.MESH
+LAGS = 64
+LOW = jnp.bfloat16
+FULL = jnp.float32
+GATHER_CHUNKS = (
+    (4, 0, 128, False),
+    (0, 768, 768, True),
+    (0, 1536, 768, True),
+    (0, 0, 768, True),
+    (3, 0, 768, False),
+    (3, 768, 768, False),
+    (1, 0, 768, True),
+    (2, 0, 256, True),
+    (3, 1536, 768, False),
+    (2, 256, 256, True),
+    (2, 512, 256, True),
+    (3, 2304, 768, False),
+)
+REDUCE_GROUPS = (
+    (2, (0, 256, 512), 256, True),
+    (3, (0, 768, 1536, 2304), 768, False),
+    (1, (0,), 768, True),
+    (0, (0, 1536), 768, True),
+    (0, (768,), 768, False),
+    (4, (0,), 128, False),
+)
+REDUCE_ORDER = (
+    (0, 0), (1, 0), (0, 1), (1, 1), (0, 2), (1, 2), (1, 3), (2, 0), (3, 0), (4, 0), (3, 1), (5, 0),
+)
+AHEAD = 3
+SMALL_ROWS = 80
+
+
+def dot_nn(left_side, right_side):
+    return jnp.dot(left_side, right_side, preferred_element_type=FULL)
+
+
+def dot_nt(left_side, right_side):
+    return lax.dot_general(
+        left_side, right_side, (((1,), (1,)), ((), ())), preferred_element_type=FULL
+    )
+
+
+def dot_tn(left_side, right_side):
+    return lax.dot_general(
+        left_side, right_side, (((0,), (0,)), ((), ())), preferred_element_type=FULL
+    )
+
+
+def exact(left_side, right_side, contract):
+    return lax.dot_general(
+        left_side, right_side, (((contract[0],), (contract[1],)), ((), ())),
+        preferred_element_type=FULL, precision=HIGHEST,
+    )
+
+
+def fold8(values):
+    rows, columns = values.shape
+    return jnp.sum(values.reshape(rows // 8, 8, columns), axis=0)
+
+
+def widen(values, width):
+    rows, columns = values.shape
+    if columns == width:
+        return values
+    return jnp.concatenate([values, jnp.zeros((rows, width - columns), values.dtype)], axis=1)
+
+
+def turn(values, amount, axis):
+    size = values.shape[axis]
+    amount = amount % size
+    return values if amount == 0 else pltpu.roll(values, amount, axis)
+
+
+def block_kernel(*refs):
+    refs = list(refs)
+
+    def take(number):
+        taken = refs[:number]
+        del refs[:number]
+        return taken
+
+    tokens, segs, cot = take(3)
+    (
+        r_first_gain, r_first_shift, r_in_bias, r_short_w, r_short_b, r_inner_w, r_inner_b,
+        r_scale, r_middle_w, r_middle_b, r_filter_w, r_direct, r_out_bias, r_second_gain,
+        r_second_shift, r_exp_bias, r_con_bias,
+    ) = take(17)
+    own = take(4)
+    features, decay = take(2)
+    result, delta = take(2)
+    sums = take(5)
+    full = take(5)
+    g_in, g_out, g_small, own_small, pack = take(5)
+    v96, v288, vexp, v8 = take(4)
+    mid_w, fil_w, taps, d_taps = take(4)
+    s_inner1, s_first, s_cos1, s_inner2, s_second, s_cos2 = take(6)
+    places, left = take(2)
+    normed1, proj, short, conv, gated, resid, normed2 = take(7)
+    hidden, post, pre, back_h, gather_out, back_s, back_r, back_m, back_g, bp = take(10)
+    acc96, acc288, accexp = take(3)
+    groups = []
+    for matrix, columns, width, split in REDUCE_GROUPS:
+        members = take(7 if split else 6)
+        names = ("core", "x", "z1", "z2", "z3", "last") + (("y",) if split else ())
+        groups.append(dict(zip(names, members)))
+    ag_recv, ag_cross, ag_core, ag_send, own_sem, rs_recv, rs_y, rs_send, rs_end = take(9)
+    assert not refs
+
+    own = list(own) + [own_small]
+    grads = (g_in, g_out, full[2], full[3], g_small)
+
+    rep = lax.axis_index("rep")
+    shard = lax.axis_index("shard")
+    y, c = rep // 2, rep % 2
+    z, x = shard // 2, shard % 2
+    pair = z // 2
+    near_z = z + 1 - 2 * (z % 2)
+    inner = ((z + 1) // 2) % 2 == 1
+    to_near = (rep, near_z * 2 + x)
+    to_mirror = (rep, (3 - z) * 2 + x)
+    to_x = (rep, z * 2 + 1 - x)
+    to_y = ((1 - y) * 2 + c, shard)
+    to_c = (y * 2 + 1 - c, shard)
+    own_pair = pl.ds(pair * 2, 2)
+    other_pair = pl.ds((1 - pair) * 2, 2)
+
+    barrier = pltpu.get_barrier_semaphore()
+    for target in (to_near, to_x, to_y, to_c):
+        pl.semaphore_signal(barrier, inc=1, device_id=target, device_id_type=MESH_ID)
+
+    @pl.when(inner)
+    def _():
+        pl.semaphore_signal(barrier, inc=1, device_id=to_mirror, device_id_type=MESH_ID)
+
+    def remote(source, landing, send, recv, device):
+        return pltpu.make_async_remote_copy(
+            src_ref=source, dst_ref=landing, send_sem=send, recv_sem=recv,
+            device_id=device, device_id_type=MESH_ID,
+        )
+
+    pack[...] = jnp.zeros_like(pack)
+    for row, member in enumerate(
+        (r_first_gain, r_first_shift, r_direct, r_out_bias, r_second_gain, r_second_shift, r_con_bias)
+    ):
+        pack[row : row + 1, 0:96] = member[...].astype(FULL)
+    for block in range(3):
+        lanes = 128 if block < 2 else 32
+        span = slice(block * 128, block * 128 + lanes)
+        top = 8 + block * 8
+        pack[top : top + 1, 0:lanes] = r_in_bias[:, span].astype(FULL)
+        pack[top + 1 : top + 2, 0:lanes] = r_short_b[:, span].astype(FULL)
+        pack[top + 2 : top + 5, 0:lanes] = r_short_w[:, span].astype(FULL)
+        pack[top + 5 : top + 6, :] = r_exp_bias[:, block * 128 : block * 128 + 128].astype(FULL)
+    for row, member in enumerate((r_inner_b, r_scale, r_middle_b)):
+        pack[32 + row : 33 + row, 0:8] = member[...].astype(FULL)
+    pack[40:73, 0:8] = r_inner_w[...].astype(FULL)
+    pack[80:88, 0:64] = r_middle_w[...].astype(FULL)
+    pack[88:152, 0:96] = r_filter_w[...].astype(FULL)
+    own_small[0] = pack[0:80, :].astype(LOW)
+    own_small[1] = pack[80:160, :].astype(LOW)
+
+    acc96[...] = jnp.zeros_like(acc96)
+    acc288[...] = jnp.zeros_like(acc288)
+    accexp[...] = jnp.zeros_like(accexp)
+    d_taps[...] = jnp.zeros_like(d_taps)
+
+    pl.semaphore_wait(barrier, 4 + ((z + 1) // 2) % 2)
+
+    chunks = GATHER_CHUNKS
+    count = len(chunks)
+    cross_index = {}
+    for index, chunk in enumerate(chunks):
+        if chunk[3]:
+            cross_index[index] = len(cross_index)
+    NEAR, FAR, SIDE0, SIDE1 = range(4)
+    S_NEAR, S_MIRROR, S_BACK, S_SIDE, S_CROSS, S_CORE = range(6)
+
+    def part(chunk, quarter):
+        matrix, column, width, split = chunk
+        if split:
+            return pl.ds(pl.multiple_of(column + quarter * (width // 2), 128), width // 2)
+        return pl.ds(column, width)
+
+    def whole(chunk):
+        return pl.ds(chunk[1], chunk[2])
+
+    for matrix in range(5):
+        pltpu.make_async_copy(own[matrix].at[c], full[matrix].at[z, x, c], own_sem.at[matrix]).start()
+
+    def first(index):
+        chunk = chunks[index]
+        m = chunk[0]
+        remote(
+            own[m].at[c, :, part(chunk, y)], full[m].at[z, x, c, :, part(chunk, y)],
+            ag_send.at[S_NEAR, m], ag_recv.at[NEAR, index], to_near,
+        ).start()
+
+    def near(index):
+        chunk = chunks[index]
+        m = chunk[0]
+        arrived = full[m].at[near_z, x, c, :, part(chunk, y)]
+        remote(arrived, arrived, ag_send.at[S_NEAR, m], ag_recv.at[NEAR, index], to_near).wait_recv()
+        both = full[m].at[own_pair, x, c, :, part(chunk, y)]
+
+        @pl.when(inner)
+        def _():
+            remote(both, both, ag_send.at[S_MIRROR, m], ag_recv.at[FAR, index], to_mirror).start()
+
+        remote(both, both, ag_send.at[S_SIDE, m], ag_recv.at[SIDE0, index], to_x).start()
+        if chunk[3]:
+            remote(
+                arrived, arrived, ag_send.at[S_CROSS, m], ag_cross.at[0, cross_index[index]], to_y
+            ).start()
+
+    def far(index):
+        chunk = chunks[index]
+        m = chunk[0]
+        both = full[m].at[other_pair, x, c, :, part(chunk, y)]
+        remote(both, both, ag_send.at[S_MIRROR, m], ag_recv.at[FAR, index], to_near).wait_recv()
+
+        @pl.when(inner)
+        def _():
+            remote(both, both, ag_send.at[S_BACK, m], ag_recv.at[FAR, index], to_near).start()
+
+        remote(both, both, ag_send.at[S_SIDE, m], ag_recv.at[SIDE1, index], to_x).start()
+        if chunk[3]:
+            remote(
+                both, both, ag_send.at[S_CROSS, m], ag_cross.at[1, cross_index[index]], to_y
+            ).start()
+
+    def to_core(index):
+        chunk = chunks[index]
+        m = chunk[0]
+        piece = full[m].at[:, :, c, :, whole(chunk)]
+        slot = core_slot(index)
+        remote(piece, piece, ag_send.at[S_CORE, m], ag_core.at[slot], to_c).start()
+
+    def core_slot(index):
+        m, column = chunks[index][0], chunks[index][1]
+        return {0: 0, 1: 1, 2: 2, 4: 3}[m] if m != 3 else 4 + column // 768
+
+    def side(index):
+        chunk = chunks[index]
+        m = chunk[0]
+        for place, slot in ((own_pair, SIDE0), (other_pair, SIDE1)):
+            both = full[m].at[place, 1 - x, c, :, part(chunk, y)]
+            remote(both, both, ag_send.at[S_SIDE, m], ag_recv.at[slot, index], to_x).wait_recv()
+        if chunk[3]:
+            column = full[m].at[:, 1 - x, c, :, part(chunk, y)]
+            remote(
+                column, column, ag_send.at[S_CROSS, m], ag_cross.at[2, cross_index[index]], to_y
+            ).start()
+        else:
+            to_core(index)
+
+    def cross(index):
+        chunk = chunks[index]
+        if not chunk[3]:
+            return
+        m = chunk[0]
+        for slot, piece in enumerate(
+            (
+                full[m].at[near_z, x, c, :, part(chunk, 1 - y)],
+                full[m].at[other_pair, x, c, :, part(chunk, 1 - y)],
+                full[m].at[:, 1 - x, c, :, part(chunk, 1 - y)],
+            )
+        ):
+            remote(
+                piece, piece, ag_send.at[S_CROSS, m], ag_cross.at[slot, cross_index[index]], to_y
+            ).wait_recv()
+        to_core(index)
+
+    def settled(m, column=None):
+        if column is None:
+            piece, slot = full[m].at[:, :, 1 - c], {0: 0, 1: 1, 2: 2, 4: 3}[m]
+        else:
+            piece, slot = full[m].at[:, :, 1 - c, :, pl.ds(column, 768)], 4 + column // 768
+        remote(piece, piece, ag_send.at[S_CORE, m], ag_core.at[slot], to_c).wait_recv()
+
+    plan = ((0, near), (0, far), (1, side), (1, cross))
+
+    def tick(step):
+        if step + AHEAD < count:
+            first(step + AHEAD)
+        for delay, action in plan:
+            if 0 <= step - delay < count:
+                action(step - delay)
+
+    for index in range(AHEAD):
+        first(index)
+    for matrix in range(5):
+        pltpu.make_async_copy(own[matrix].at[c], full[matrix].at[z, x, c], own_sem.at[matrix]).wait()
+
+    def row_blocks(size, action):
+        def body(step, carry):
+            action(pl.ds(pl.multiple_of(step * size, size), size))
+            return carry
+
+        lax.fori_loop(0, tokens.shape[0] // size, body, 0)
+
+    def find_places():
+        rows = lax.broadcasted_iota(jnp.int32, (128, 128), 0)
+        columns = lax.broadcasted_iota(jnp.int32, (128, 128), 1)
+        for sequence in range(2):
+            ids = jnp.broadcast_to(segs[sequence : sequence + 1, :].astype(FULL), (128, 128))
+            same = ids == ids.T
+            before = jnp.sum(jnp.where(same & (columns < rows), 1.0, 0.0), axis=1, keepdims=True)
+            after = jnp.sum(jnp.where(same & (columns > rows), 1.0, 0.0), axis=1, keepdims=True)
+            span = slice(sequence * 128, sequence * 128 + 128)
+            places[span, :] = jnp.broadcast_to(before.astype(jnp.int32), (128, 128))
+            left[span, :] = jnp.broadcast_to(after.astype(jnp.int32), (128, 128))
+
+    def unpack_small():
+        total96 = jnp.zeros((8, 768), FULL)
+        total288 = jnp.zeros((8, 2304), FULL)
+        total8 = jnp.zeros((8, 128), FULL)
+        inner_total = jnp.zeros((40, 128), FULL)
+        fil_w[...] = jnp.zeros_like(fil_w)
+        mid_w[...] = jnp.zeros_like(mid_w)
+        for s in range(8):
+            top = full[4][s // 2, s % 2, 0].astype(FULL)
+            low = full[4][s // 2, s % 2, 1].astype(FULL)
+            total96 = total96 + turn(widen(top[0:8], 768), 96 * s, 1)
+            wide = jnp.concatenate([top[8:16], top[16:24], top[24:32]], axis=1)
+            vexp[:, s * 384 : s * 384 + 384] = wide[5:6]
+            total288 = total288 + turn(widen(wide, 2304), 288 * s, 1)
+            total8 = total8 + turn(top[32:40], 8 * s, 1)
+            inner_total = inner_total + turn(top[40:80], 8 * s, 1)
+            mid_w[8 * s : 8 * s + 8, :] = low[0:8]
+            fil_w[0:64, :] += turn(widen(low[8:72], 768), 96 * s, 1)
+        v96[...] = total96
+        v288[...] = total288
+        v8[...] = total8
+        scale = total8[1:2]
+        inner1 = exact(features[...], inner_total, (1, 0)) + total8[0:1]
+        s_inner1[...] = inner1
+        s_first[...] = jnp.sin(scale * inner1)
+        s_cos1[...] = jnp.cos(scale * inner1)
+        inner2 = exact(s_first[...], mid_w[...], (1, 0)) + total8[2:3]
+        s_inner2[...] = inner2
+        s_second[...] = jnp.sin(scale * inner2)
+        s_cos2[...] = jnp.cos(scale * inner2)
+        taps[...] = exact(s_second[...], fil_w[...], (1, 0)) * decay[...]
+
+    def center(values):
+        middle = values - jnp.mean(values, axis=-1, keepdims=True)
+        spread = jnp.mean(middle * middle, axis=-1, keepdims=True)
+        scale = lax.rsqrt(spread + EPSILON)
+        return middle * scale, scale
+
+    def norm_first(rows):
+        unit, _ = center(tokens[rows, :].astype(FULL))
+        normed1[rows, :] = (unit * v96[0:1, :] + v96[1:2, :]).astype(LOW)
+
+    def matrix_of(m, columns, width):
+        value = full[m][:, :, :, :, columns]
+        return value.reshape(value.shape[0] * value.shape[1] * value.shape[2] * value.shape[3], width)
+
+    def project(k):
+        span = slice(k * 768, k * 768 + 768)
+        proj[k] = dot_nn(normed1[...], matrix_of(0, pl.ds(k * 768, 768), 768)) + v288[0:1, span]
+
+        def body(step, carry):
+            rows = pl.ds(pl.multiple_of((step // 6) * 128, 128), 128)
+            lane = pl.multiple_of((step % 6) * 128, 128)
+            lanes = pl.ds(lane, 128)
+            wide = pl.ds(pl.multiple_of(k * 768 + lane, 128), 128)
+            values = proj[k, rows, lanes]
+            where = places[rows, :]
+            total = v288[1:2, wide] + v288[2:3, wide] * values
+            for lag in (1, 2):
+                moved = jnp.where(where >= lag, pltpu.roll(values, lag, 0), 0.0)
+                total = total + v288[2 + lag : 3 + lag, wide] * moved
+            short[k, rows, lanes] = total
+            return carry
+
+        lax.fori_loop(0, 12, body, 0)
+
+    def convolve(begin, end):
+        def body(step, carry):
+            rows = pl.ds(pl.multiple_of((step // 6) * 128, 128), 128)
+            lanes = pl.ds(pl.multiple_of((step % 6) * 128, 128), 128)
+            carried = short[2, rows, lanes] * short[1, rows, lanes]
+            where = places[rows, :]
+            total = v96[2:3, lanes] * carried
+            for low_lag in range(8):
+                moved = turn(carried, low_lag, 0)
+                for high in range(LAGS // 8):
+                    lag, skip = high * 8 + low_lag, high * 8
+                    term = jnp.where(
+                        where[skip:] >= lag, taps[lag : lag + 1, lanes] * moved[: 128 - skip], 0.0
+                    )
+                    if skip:
+                        total = jnp.concatenate([total[:skip], total[skip:] + term], axis=0)
+                    else:
+                        total = total + term
+            conv[rows, lanes] = total
+            return carry
+
+        lax.fori_loop(begin, end, body, 0)
+
+    def mix_out():
+        def gate(rows):
+            gated[rows, :] = (conv[rows, :] * short[0, rows, :]).astype(LOW)
+
+        row_blocks(16, gate)
+        resid[...] = dot_nn(gated[...], matrix_of(1, pl.ds(0, 768), 768))
+
+        def finish_rows(rows):
+            values = resid[rows, :] + tokens[rows, :].astype(FULL) + v96[3:4, :]
+            resid[rows, :] = values
+            unit, _ = center(values)
+            normed2[rows, :] = (unit * v96[4:5, :] + v96[5:6, :]).astype(LOW)
+
+        row_blocks(16, finish_rows)
+
+    def expand(k):
+        span = slice(k * 768, k * 768 + 768)
+        hidden[:, span] = (
+            dot_nn(normed2[...], matrix_of(3, pl.ds(k * 768, 768), 768)) + vexp[:, span]
+        )
+
+    def feed(k):
+        span = slice(k * 768, k * 768 + 768)
+        rows_of = full[2][k].reshape(768, 768)
+        back_h[...] = dot_nt(cot[...], rows_of)
+
+        def bend(rows):
+            values = hidden[rows, span]
+            cube = values * values
+            grow = math.sqrt(2.0 / math.pi)
+            slope = jnp.tanh(grow * (values + 0.044715 * cube * values))
+            half_up = 0.5 + 0.5 * slope
+            post[rows, span] = (values * half_up).astype(LOW)
+            steep = half_up + (0.5 * values) * (1.0 - slope * slope) * (
+                grow * (1.0 + 3.0 * 0.044715 * cube)
+            )
+            grad = (back_h[rows, :] * steep).astype(LOW)
+            pre[rows, span] = grad
+            accexp[:, span] += fold8(grad.astype(FULL))
+
+        row_blocks(16, bend)
+        out_part = dot_nn(post[:, span], full[2][k].reshape(768, 768))
+        back_part = dot_nt(pre[:, span], matrix_of(3, pl.ds(k * 768, 768), 768))
+        if k == 0:
+            gather_out[...] = out_part
+            back_s[...] = back_part
+        else:
+            gather_out[...] += out_part
+            back_s[...] += back_part
+
+    find_places()
+    tick(0)
+    tick(1)
+    settled(4)
+    unpack_small()
+    row_blocks(16, norm_first)
+    tick(2)
+    tick(3)
+    tick(4)
+    tick(5)
+    settled(0)
+    project(1)
+    tick(6)
+    project(2)
+    tick(7)
+    convolve(0, 4)
+    tick(8)
+    convolve(4, 8)
+    tick(9)
+    convolve(8, 12)
+    tick(10)
+    project(0)
+    settled(1)
+    tick(11)
+    mix_out()
+    tick(12)
+    settled(3, 0)
+    expand(0)
+    settled(3, 768)
+    expand(1)
+    settled(3, 1536)
+    expand(2)
+    settled(2)
+    for k in range(3):
+        feed(k)
+    settled(3, 2304)
+    expand(3)
+    feed(3)
+
+    for m in range(5):
+        quarter = {0: 1152, 1: 384, 2: 384, 3: 3072, 4: 128}[m]
+        wide = full[m].shape[4]
+        one = full[m].at[0, 0, 0, :, pl.ds(0, quarter)]
+        two = full[m].at[pl.ds(0, 2), 0, 0, :, pl.ds(0, quarter)]
+        four = full[m].at[:, 0, 0, :, pl.ds(0, quarter)]
+        remote(one, one, ag_send.at[S_NEAR, m], ag_recv.at[NEAR, 0], to_near).wait_send()
+
+        @pl.when(inner)
+        def _(two=two, m=m):
+            remote(two, two, ag_send.at[S_MIRROR, m], ag_recv.at[FAR, 0], to_near).wait_send()
+            remote(two, two, ag_send.at[S_BACK, m], ag_recv.at[FAR, 0], to_near).wait_send()
+
+        remote(four, four, ag_send.at[S_SIDE, m], ag_recv.at[FAR, 0], to_near).wait_send()
+        if m not in (3, 4):
+            near_one = full[m].at[pl.ds(0, 3), 0, 0, :, pl.ds(0, quarter)]
+            remote(near_one, near_one, ag_send.at[S_CROSS, m], ag_recv.at[FAR, 0], to_near).wait_send()
+            remote(four, four, ag_send.at[S_CROSS, m], ag_recv.at[FAR, 0], to_near).wait_send()
+        everything = full[m].at[:, :, 0, :, pl.ds(0, wide)]
+        remote(everything, everything, ag_send.at[S_CORE, m], ag_recv.at[FAR, 0], to_near).wait_send()
+
+    position = {}
+    split_position = {}
+    for index, key in enumerate(REDUCE_ORDER):
+        position[key] = index
+        if REDUCE_GROUPS[key[0]][3]:
+            split_position[key] = len(split_position)
+    R_CORE, R_X, R_Z1, R_Z2, R_Z3, R_LAST = range(6)
+    W_CORE, W_Y, W_X, W_Z1, W_Z2, W_Z3, W_LAST, W_END = range(8)
+
+    def info(key):
+        g, i = key
+        matrix, columns, width, split = REDUCE_GROUPS[g]
+        return g, i, matrix, columns[i], width, split, groups[g], position[key]
+
+    def halves(width, which):
+        return pl.ds(pl.multiple_of(which * (width // 2), 128), width // 2)
+
+    def stage(key):
+        g, i, m, column, width, split, buf, n = info(key)
+        remote(
+            grads[m].at[:, :, 1 - c, :, pl.ds(column, width)], buf["core"].at[i],
+            rs_send.at[W_CORE, g], rs_recv.at[R_CORE, n], to_c,
+        ).start()
+
+    def add_core(key):
+        g, i, m, column, width, split, buf, n = info(key)
+        landing = buf["core"].at[i]
+        remote(landing, landing, rs_send.at[W_CORE, g], rs_recv.at[R_CORE, n], to_c).wait_recv()
+
+        def body(step, carry):
+            a, b = step // 2, step % 2
+            buf["core"][i, a, b] = buf["core"][i, a, b] + grads[m][a, b, c, :, pl.ds(column, width)]
+            return carry
+
+        lax.fori_loop(0, 8, body, 0)
+        if split:
+            remote(
+                buf["core"].at[i, :, :, :, halves(width, 1 - y)], buf["y"].at[i],
+                rs_send.at[W_Y, g], rs_y.at[split_position[key]], to_y,
+            ).start()
+        else:
+            remote(
+                buf["core"].at[i, :, 1 - x], buf["x"].at[i],
+                rs_send.at[W_X, g], rs_recv.at[R_X, n], to_x,
+            ).start()
+
+    def add_y(key):
+        g, i, m, column, width, split, buf, n = info(key)
+        if not split:
+            return
+        landing = buf["y"].at[i]
+        remote(landing, landing, rs_send.at[W_Y, g], rs_y.at[split_position[key]], to_y).wait_recv()
+
+        def body(step, carry):
+            a, b = step // 2, step % 2
+            buf["y"][i, a, b] = buf["y"][i, a, b] + buf["core"][i, a, b, :, halves(width, y)]
+            return carry
+
+        lax.fori_loop(0, 8, body, 0)
+        remote(
+            buf["y"].at[i, :, 1 - x], buf["x"].at[i], rs_send.at[W_X, g], rs_recv.at[R_X, n], to_x
+        ).start()
+
+    def add_x(key):
+        g, i, m, column, width, split, buf, n = info(key)
+        landing = buf["x"].at[i]
+        remote(landing, landing, rs_send.at[W_X, g], rs_recv.at[R_X, n], to_x).wait_recv()
+        own_part = buf["y"] if split else buf["core"]
+
+        def body(step, carry):
+            buf["x"][i, step] = buf["x"][i, step] + own_part[i, step, x]
+            return carry
+
+        lax.fori_loop(0, 4, body, 0)
+
+        @pl.when(jnp.logical_not(inner))
+        def _():
+            remote(
+                buf["x"].at[i, other_pair], buf["z1"].at[i],
+                rs_send.at[W_Z1, g], rs_recv.at[R_Z1, n], to_near,
+            ).start()
+            remote(
+                buf["x"].at[i, near_z], buf["z3"].at[i],
+                rs_send.at[W_Z3, g], rs_recv.at[R_Z3, n], to_near,
+            ).start()
+
+    def add_z1(key):
+        g, i, m, column, width, split, buf, n = info(key)
+
+        @pl.when(inner)
+        def _():
+            landing = buf["z1"].at[i]
+            remote(landing, landing, rs_send.at[W_Z1, g], rs_recv.at[R_Z1, n], to_near).wait_recv()
+            for step in range(2):
+                at = (1 - pair) * 2 + step
+                buf["x"][i, at] = buf["x"][i, at] + buf["z1"][i, step]
+            remote(
+                buf["x"].at[i, other_pair], buf["z2"].at[i],
+                rs_send.at[W_Z2, g], rs_recv.at[R_Z2, n], to_mirror,
+            ).start()
+
+    def add_z2(key):
+        g, i, m, column, width, split, buf, n = info(key)
+
+        @pl.when(inner)
+        def _():
+            landing = buf["z2"].at[i]
+            remote(landing, landing, rs_send.at[W_Z2, g], rs_recv.at[R_Z2, n], to_mirror).wait_recv()
+            for step in range(2):
+                at = pair * 2 + step
+                buf["x"][i, at] = buf["x"][i, at] + buf["z2"][i, step]
+            remote(
+                buf["x"].at[i, near_z], buf["z3"].at[i],
+                rs_send.at[W_Z3, g], rs_recv.at[R_Z3, n], to_near,
+            ).start()
+
+    def add_z3(key):
+        g, i, m, column, width, split, buf, n = info(key)
+        landing = buf["z3"].at[i]
+        remote(landing, landing, rs_send.at[W_Z3, g], rs_recv.at[R_Z3, n], to_near).wait_recv()
+        buf["last"][i, 0] = buf["x"][i, z] + buf["z3"][i]
+        remote(
+            buf["last"].at[i, 0], buf["last"].at[i, 1],
+            rs_send.at[W_LAST, g], rs_recv.at[R_LAST, n], to_y,
+        ).start()
+
+    def finish(key):
+        g, i, m, column, width, split, buf, n = info(key)
+        landing = buf["last"].at[i, 1]
+        remote(landing, landing, rs_send.at[W_LAST, g], rs_recv.at[R_LAST, n], to_y).wait_recv()
+        if split:
+            for which, slot in ((y, 0), (1 - y, 1)):
+                columns = pl.ds(pl.multiple_of(column + which * (width // 2), 128), width // 2)
+                sums[m][c, :, columns] = buf["last"][i, slot].astype(FULL)
+        else:
+            sums[m][c, :, pl.ds(column, width)] = buf["last"][i, 0].astype(FULL) + buf["last"][
+                i, 1
+            ].astype(FULL)
+        piece = sums[m].at[c, :, pl.ds(column, width)]
+        remote(piece, piece, rs_send.at[W_END, g], rs_end.at[g], to_c).start()
+
+    reduce_plan = (
+        (0, add_core), (1, add_y), (2, add_x), (3, add_z1), (4, add_z2), (5, add_z3), (6, finish),
+    )
+    steps_left = [0]
+
+    def advance(limit=None):
+        step = steps_left[0]
+        steps_left[0] += 1
+        for delay, action in reduce_plan:
+            if 0 <= step - delay < len(REDUCE_ORDER):
+                action(REDUCE_ORDER[step - delay])
+
+    def grad_contract(i):
+        columns = pl.ds(i * 256, 256)
+
+        def body(s, carry):
+            lanes = pl.ds(pl.multiple_of(s * 384, 128), 384)
+            value = dot_tn(post[:, lanes], cot[:, columns]).astype(LOW)
+            full[2][s // 2, s % 2, :, :, columns] = value.reshape(2, 192, 256)
+            return carry
+
+        lax.fori_loop(0, 8, body, 0)
+
+    def grad_rows(source, other, target, columns, width):
+        for half in range(2):
+            value = dot_tn(source[:, half * 384 : half * 384 + 384], other).astype(LOW)
+            target[2 * half : 2 * half + 2, :, :, :, columns] = value.reshape(2, 2, 2, 48, width)
+
+    def grad_expand(i):
+        span = slice(i * 768, i * 768 + 768)
+        grad_rows(normed2, pre[:, span], full[3], pl.ds(i * 768, 768), 768)
+
+    def norm_second_back(rows):
+        unit, scale = center(resid[rows, :])
+        grad = back_s[rows, :]
+        top = cot[rows, :].astype(FULL)
+        e = grad * v96[4:5, :]
+        value = (
+            e - jnp.mean(e, axis=-1, keepdims=True) - unit * jnp.mean(e * unit, axis=-1, keepdims=True)
+        ) * scale + top
+        back_r[rows, :] = value
+        rounded = value.astype(LOW)
+        back_m[rows, :] = rounded
+        acc96[4] += fold8(grad * unit)
+        acc96[5] += fold8(grad)
+        acc96[3] += fold8(rounded.astype(FULL))
+        acc96[6] += fold8(top)
+        result[rows, :] = (resid[rows, :] + gather_out[rows, :] + v96[6:7, :]).astype(LOW)
+
+    def convolve_back(begin, end):
+        def body(step, carry):
+            rows = pl.ds(pl.multiple_of((step // 6) * 128, 128), 128)
+            lane = pl.multiple_of((step % 6) * 128, 128)
+            lanes = pl.ds(lane, 128)
+            where = places[rows, :]
+            rest = left[rows, :]
+            gate_in = short[1, rows, lanes]
+            values = short[2, rows, lanes]
+            top = back_g[rows, lanes]
+            carried = values * gate_in
+            back_conv = top * short[0, rows, lanes]
+            acc96[2, :, lanes] += fold8(back_conv * carried)
+            total = v96[2:3, lanes] * back_conv
+            for low_lag in range(8):
+                turned = turn(back_conv, -low_lag, 0)
+                for high in range(LAGS // 8):
+                    lag, skip = high * 8 + low_lag, high * 8
+                    size = 128 - skip
+                    moved = jnp.where(rest[:size] >= lag, turned[skip:], 0.0)
+                    term = taps[lag : lag + 1, lanes] * moved
+                    if skip:
+                        total = jnp.concatenate([total[:size] + term, total[size:]], axis=0)
+                    else:
+                        total = total + term
+                    d_taps[lag : lag + 1, lanes] += jnp.sum(
+                        moved * carried[:size], axis=0, keepdims=True
+                    )
+            streams = (top * conv[rows, lanes], total * values, total * gate_in)
+            for k in range(3):
+                wide = pl.ds(pl.multiple_of(k * 768 + lane, 128), 128)
+                grad = streams[k]
+                before = proj[k, rows, lanes]
+                acc288[1, :, wide] += fold8(grad)
+                acc288[2, :, wide] += fold8(grad * before)
+                value = v288[2:3, wide] * grad
+                for lag in (1, 2):
+                    moved = jnp.where(where >= lag, pltpu.roll(before, lag, 0), 0.0)
+                    acc288[2 + lag, :, wide] += fold8(grad * moved)
+                    later = jnp.where(rest >= lag, pltpu.roll(grad, 128 - lag, 0), 0.0)
+                    value = value + v288[2 + lag : 3 + lag, wide] * later
+                rounded = value.astype(LOW)
+                bp[k, rows, lanes] = rounded
+                acc288[0, :, wide] += fold8(rounded.astype(FULL))
+            return carry
+
+        lax.fori_loop(begin, end, body, 0)
+
+    def norm_first_back(rows):
+        unit, scale = center(tokens[rows, :].astype(FULL))
+        grad = back_s[rows, :]
+        e = grad * v96[0:1, :]
+        delta[rows, :] = back_r[rows, :] + (
+            e - jnp.mean(e, axis=-1, keepdims=True) - unit * jnp.mean(e * unit, axis=-1, keepdims=True)
+        ) * scale
+        acc96[0] += fold8(grad * unit)
+        acc96[1] += fold8(grad)
+
+    def small_grads():
+        scale = v8[1:2, :]
+        raw = d_taps[...] * decay[...]
+        d_fil = exact(s_second[...], raw, (0, 0))
+        b2 = exact(raw, fil_w[...], (1, 1)) * s_cos2[...]
+        b2s = b2 * scale
+        d_mid = exact(s_first[...], b2s, (0, 0))
+        b1 = exact(b2s, mid_w[...], (1, 1)) * s_cos1[...]
+        b1s = b1 * scale
+        d_inner = exact(features[...], b1s, (0, 0))
+        d_scale = jnp.sum(b2 * s_inner2[...] + b1 * s_inner1[...], axis=0, keepdims=True)
+        rows8 = jnp.concatenate(
+            [
+                jnp.sum(b1s, axis=0, keepdims=True), d_scale, jnp.sum(b2s, axis=0, keepdims=True),
+                jnp.zeros((5, 128), FULL),
+            ],
+            axis=0,
+        )
+        rows96 = jnp.concatenate(
+            [jnp.sum(acc96[f], axis=0, keepdims=True) for f in range(7)] + [jnp.zeros((1, 768), FULL)],
+            axis=0,
+        )
+        rows288 = jnp.concatenate(
+            [jnp.sum(acc288[f], axis=0, keepdims=True) for f in range(5)]
+            + [jnp.zeros((3, 2304), FULL)],
+            axis=0,
+        )
+        rows_exp = jnp.sum(accexp[...], axis=0, keepdims=True)
+        lane = lax.broadcasted_iota(jnp.int32, (8, 128), 1)
+        row = lax.broadcasted_iota(jnp.int32, (8, 128), 0)
+        wide_lane = lax.broadcasted_iota(jnp.int32, (64, 128), 1)
+        long_lane = lax.broadcasted_iota(jnp.int32, (40, 128), 1)
+        for s in range(8):
+            a, b = s // 2, s % 2
+            g_small[a, b, 0, 0:8, :] = jnp.where(lane < 96, turn(rows96, -96 * s, 1)[:, :128], 0.0)
+            turned = turn(rows288, -288 * s, 1)
+            for block in range(3):
+                value = turned[:, block * 128 : block * 128 + 128]
+                if block == 2:
+                    value = jnp.where(lane < 32, value, 0.0)
+                bias = rows_exp[:, s * 384 + block * 128 : s * 384 + block * 128 + 128]
+                value = jnp.where(row == 5, jnp.broadcast_to(bias, (8, 128)), value)
+                g_small[a, b, 0, 8 + block * 8 : 16 + block * 8, :] = value
+            g_small[a, b, 0, 32:40, :] = jnp.where(lane < 8, turn(rows8, -8 * s, 1), 0.0)
+            g_small[a, b, 0, 40:80, :] = jnp.where(long_lane < 8, turn(d_inner, -8 * s, 1), 0.0)
+            g_small[a, b, 1, 0:8, :] = d_mid[8 * s : 8 * s + 8]
+            g_small[a, b, 1, 8:72, :] = jnp.where(
+                wide_lane < 96, turn(d_fil[0:64], -96 * s, 1)[:, :128], 0.0
+            )
+            g_small[a, b, 1, 72:80, :] = jnp.zeros((8, 128), FULL)
+
+    grad_contract(0)
+    stage((0, 0))
+    grad_expand(0)
+    stage((1, 0))
+    grad_contract(1)
+    stage((0, 1))
+    advance()
+    grad_expand(1)
+    stage((1, 1))
+    grad_contract(2)
+    stage((0, 2))
+    advance()
+    row_blocks(16, norm_second_back)
+    grad_expand(2)
+    stage((1, 2))
+    advance()
+    grad_expand(3)
+    stage((1, 3))
+    advance()
+    back_g[...] = dot_nt(back_m[...], matrix_of(1, pl.ds(0, 768), 768))
+    grad_rows(gated, back_m[...], g_out, pl.ds(0, 768), 768)
+    stage((2, 0))
+    advance()
+    convolve_back(0, 3)
+    advance()
+    convolve_back(3, 6)
+    advance()
+    convolve_back(6, 9)
+    advance()
+    convolve_back(9, 12)
+    for key, k in (((3, 0), 0), ((4, 0), 1), ((3, 1), 2)):
+        grad_rows(normed1, bp[k], g_in, pl.ds(k * 768, 768), 768)
+        stage(key)
+        advance()
+    for k in range(3):
+        value = dot_nt(bp[k], matrix_of(0, pl.ds(k * 768, 768), 768))
+        if k == 0:
+            back_s[...] = value
+        else:
+            back_s[...] += value
+    row_blocks(16, norm_first_back)
+    small_grads()
+    stage((5, 0))
+    while steps_left[0] < len(REDUCE_ORDER) + 6:
+        advance()
+
+    for g, (matrix, columns, width, split) in enumerate(REDUCE_GROUPS):
+        piece = sums[matrix].at[1 - c, :, pl.ds(0, width * len(columns))]
+        remote(piece, piece, rs_send.at[W_END, g], rs_end.at[g], to_c).wait_recv()
+    for g, (matrix, columns, width, split) in enumerate(REDUCE_GROUPS):
+        buf = groups[g]
+
+        def leave(kind, ref, g=g):
+            remote(ref, ref, rs_send.at[kind, g], rs_end.at[g], to_c).wait_send()
+
+        leave(W_CORE, buf["core"])
+        if split:
+            leave(W_Y, buf["y"])
+        leave(W_X, buf["x"])
+        leave(W_Z3, buf["z3"])
+        leave(W_LAST, buf["last"].at[:, 0])
+        leave(W_END, sums[matrix].at[1 - c, :, pl.ds(0, width * len(columns))])
+
+        @pl.when(inner)
+        def _(leave=leave, buf=buf):
+            leave(W_Z2, buf["z2"])
+
+        @pl.when(jnp.logical_not(inner))
+        def _(leave=leave, buf=buf):
+            leave(W_Z1, buf["z1"])
+
+
+def unpack_kernel(result, delta, s_in, s_out, s_con, s_exp, s_small, *outs):
+    (
+        o_result, o_delta, o_first_gain, o_first_shift, o_in, o_in_bias, o_short_w, o_short_b,
+        o_inner_w, o_inner_b, o_scale, o_middle_w, o_middle_b, o_filter_w, o_direct, o_out,
+        o_out_bias, o_second_gain, o_second_shift, o_exp, o_exp_bias, o_con, o_con_bias,
+    ) = outs
+    o_result[...] = result[...]
+    o_delta[...] = delta[...]
+    for source, target in ((s_in, o_in), (s_out, o_out), (s_con, o_con), (s_exp, o_exp)):
+        height = source.shape[1]
+        for half in range(2):
+            target[half * height : half * height + height, :] = source[half]
+    for row, target in enumerate(
+        (o_first_gain, o_first_shift, o_direct, o_out_bias, o_second_gain, o_second_shift, o_con_bias)
+    ):
+        target[...] = s_small[0, row : row + 1, 0:96].reshape(96)
+    wide = jnp.concatenate([s_small[0, 8:16, :], s_small[0, 16:24, :], s_small[0, 24:32, :]], axis=1)
+    o_in_bias[...] = wide[0:1, 0:288].reshape(288)
+    o_short_b[...] = wide[1:2, 0:288].reshape(288)
+    o_short_w[...] = wide[2:5, 0:288]
+    o_exp_bias[...] = wide[5:6].reshape(384)
+    for row, target in enumerate((o_inner_b, o_scale, o_middle_b)):
+        target[...] = s_small[0, 32 + row : 33 + row, 0:8].reshape(8)
+    o_inner_w[...] = s_small[0, 40:73, 0:8]
+    o_middle_w[...] = s_small[1, 0:8, 0:64]
+    o_filter_w[...] = s_small[1, 8:72, 0:96]
+
+
+def filter_constants(length, width):
+    places = np.arange(LAGS, dtype=np.float64)
+    scales = 0.0001 + np.arange(16, dtype=np.float64) * ((15.0 - 0.0001) / 15.0)
+    phases = (2.0 * math.pi * places / length)[:, None] * scales[None, :]
+    ramp = places / (length - 1)
+    table = np.zeros((LAGS, 40), np.float32)
+    table[:, 0] = ramp
+    table[:, 1:17] = np.cos(phases)
+    table[:, 17:33] = -np.sin(phases)
+    rates = math.log(100.0) * (
+        1.0 / 1.5 + (1.0 / 0.3 - 1.0 / 1.5) * np.arange(width, dtype=np.float64) / (width - 1)
+    )
+    return table, np.exp(-ramp[:, None] * rates[None, :]).astype(np.float32)
+
+
+def block_device(
+    tokens, segment_ids, cotangent, first_gain, first_shift, input_weight, input_bias,
+    short_weight, short_bias, inner_weight, inner_bias, sine_scale, middle_weight, middle_bias,
+    filter_weight, direct_gain, output_weight, output_bias, second_gain, second_shift,
+    expand_weight, expand_bias, contract_weight, contract_bias,
+):
+    blocks, _, length, width = tokens.shape
+    rows = blocks * length
+    features, decay = filter_constants(length, width)
+
+    def line(member):
+        return member.reshape(1, -1) if member.ndim == 1 else member
+
+    small_members = (
+        first_gain, first_shift, input_bias, short_weight, short_bias, inner_weight, inner_bias,
+        sine_scale, middle_weight, middle_bias, filter_weight, direct_gain, output_bias,
+        second_gain, second_shift, expand_bias, contract_bias,
+    )
+
+    def halved(member):
+        return member.reshape(2, member.shape[0] // 2, member.shape[1])
+
+    shards = [halved(m) for m in (input_weight, output_weight, contract_weight, expand_weight)]
+    inputs = (
+        tokens.reshape(rows, width), segment_ids.reshape(blocks, length),
+        cotangent.reshape(rows, width),
+    ) + tuple(line(m) for m in small_members) + tuple(shards) + (
+        jnp.asarray(features), jnp.asarray(decay),
+    )
+    shapes = [m.shape[1:] for m in shards] + [(SMALL_ROWS, 128)]
+    outs = [
+        jax.ShapeDtypeStruct((rows, width), LOW),
+        jax.ShapeDtypeStruct((rows, width), FULL),
+    ] + [jax.ShapeDtypeStruct((2,) + s, FULL) for s in shapes]
+    count = len(GATHER_CHUNKS)
+    crossing = sum(1 for chunk in GATHER_CHUNKS if chunk[3])
+    vm = pltpu.VMEM
+    scratch = [vm((4, 2, 2) + s, LOW) for s in shapes]
+    scratch += [
+        vm((4, 2, 2) + shapes[0], LOW), vm((4, 2, 2) + shapes[1], LOW),
+        vm((4, 2, 2) + shapes[4], FULL), vm((2, SMALL_ROWS, 128), LOW),
+        vm((2 * SMALL_ROWS, 128), FULL),
+        vm((8, width), FULL), vm((8, 3 * width), FULL), vm((1, 4 * width), FULL), vm((8, 128), FULL),
+        vm((128, 128), FULL), vm((128, width), FULL), vm((LAGS, width), FULL), vm((LAGS, width), FULL),
+    ]
+    scratch += [vm((LAGS, 128), FULL)] * 6
+    scratch += [vm((rows, 128), jnp.int32)] * 2
+    scratch += [
+        vm((rows, width), LOW), vm((3, rows, width), FULL), vm((3, rows, width), FULL),
+        vm((rows, width), FULL), vm((rows, width), LOW), vm((rows, width), FULL),
+        vm((rows, width), LOW),
+        vm((rows, 4 * width), FULL), vm((rows, 4 * width), LOW), vm((rows, 4 * width), LOW),
+        vm((rows, width), FULL), vm((rows, width), FULL), vm((rows, width), FULL),
+        vm((rows, width), FULL), vm((rows, width), LOW), vm((rows, width), FULL),
+        vm((3, rows, width), LOW),
+        vm((7, 8, width), FULL), vm((5, 8, 3 * width), FULL), vm((8, 4 * width), FULL),
+    ]
+    for matrix, columns, span, split in REDUCE_GROUPS:
+        n, high = len(columns), shapes[matrix][0]
+        kind = FULL if matrix == 4 else LOW
+        v = span // 2 if split else span
+        scratch += [
+            vm((n, 4, 2, high, span), kind), vm((n, 4, high, v), kind), vm((n, 2, high, v), kind),
+            vm((n, 2, high, v), kind), vm((n, high, v), kind), vm((n, 2, high, v), kind),
+        ]
+        if split:
+            scratch.append(vm((n, 4, 2, high, v), kind))
+    total = len(REDUCE_ORDER)
+    splits = sum(len(g[1]) for g in REDUCE_GROUPS if g[3])
+    dma = pltpu.SemaphoreType.DMA
+    scratch += [
+        dma((4, count)), dma((3, crossing)), dma((8,)), dma((6, 5)), dma((5,)),
+        dma((6, total)), dma((splits,)), dma((8, len(REDUCE_GROUPS))), dma((len(REDUCE_GROUPS),)),
+    ]
+    in_vmem = pl.BlockSpec(memory_space=pltpu.VMEM)
+    parts = pl.pallas_call(
+        block_kernel,
+        out_shape=outs,
+        in_specs=[in_vmem] * len(inputs),
+        out_specs=[in_vmem] * len(outs),
+        scratch_shapes=scratch,
+        compiler_params=pltpu.CompilerParams(
+            collective_id=0, has_side_effects=True, vmem_limit_bytes=67043328
+        ),
+    )(*inputs)
+    members = (
+        first_gain, first_shift, input_weight, input_bias, short_weight, short_bias, inner_weight,
+        inner_bias, sine_scale, middle_weight, middle_bias, filter_weight, direct_gain,
+        output_weight, output_bias, second_gain, second_shift, expand_weight, expand_bias,
+        contract_weight, contract_bias,
+    )
+    final = [outs[0], outs[1]] + [jax.ShapeDtypeStruct(m.shape, FULL) for m in members]
+    done = pl.pallas_call(
+        unpack_kernel,
+        out_shape=final,
+        in_specs=[in_vmem] * 7,
+        out_specs=[in_vmem] * len(final),
+    )(*parts)
+    return (done[0].reshape(tokens.shape), done[1].reshape(tokens.shape)) + tuple(done[2:])
 
 
 def per_device(
@@ -420,8 +1450,9 @@
         P("shard", None),
         P("shard"),
     )
+    blocked = dict(mesh.shape) == {"rep": 4, "shard": 8}
     return jax.shard_map(
-        per_device,
+        block_device if blocked else per_device,
         mesh=mesh,
         in_specs=placed,
         out_specs=(

time: 1190 us -> 251 us (0.21)
  waiting for transfers between devices: 725 us -> 0 us
  Pallas kernels: 0 us -> 243 us
  blocking collectives: 190 us -> 0 us
  matrix products: 178 us -> 0 us
  local copies, waits for them, and re-layouts: 39.7 us -> 6.49 us
  other arithmetic: 27.2 us -> 0 us
  between operations: 21.5 us -> 0.67 us
    reduce_scatter x4 -> x0, waiting for transfers between devices: 452 us -> none  [the longest x1 167 us: per_device(): lax.psum_scatter(dense_total[2], 'shard', scatter_dimension=0, tiled=True)]
    pallas_call x0 -> x2, Pallas kernels: none -> 243 us  [the longest x1 239 us: block_device(): pl.pallas_call(block_kernel, out_shape=outs, in_specs=[in_vmem] * len(inp...]
    unnamed x15 -> x0, waiting for transfers between devices: 195 us -> none
    dot_general x59 -> x0, matrix products: 178 us -> none  [the longest x6 37.2 us: inverse(): jnp.einsum('ft,...fd->...td', cosine, scaled_real, precision=HIGHEST)]
    all_gather x5 -> x0, blocking collectives: 143 us -> none  [the longest x1 32.3 us: fetch_mixer(): lax.all_gather(short_weight, 'shard', axis=1, tiled=True)]
    psum x1 -> x0, waiting for transfers between devices: 64.1 us -> none  [per_device(): lax.psum((mixer_total[0], mixer_total[1], mixer_total[2], mixer_total[3],...]
    unnamed x1 -> x0, blocking collectives: 34.8 us -> none
    unnamed x392 -> x2, local copies, waits for them, and re-layouts: 32.5 us -> 2.76 us
  transfers between devices with their start and end apart: 12 -> 0, of which waited for: 8 -> 0; matrix products, arithmetic and copies ran while one was open for 14% -> 0% of each run, Pallas kernels for 0% -> 0%
where the time goes in v2:
time: 251 us; the launch traced here: 250 us
  Pallas kernels  243 us (97%)
  local copies, waits for them, and re-layouts  6.49 us (3%)
    pallas_call x1, Pallas kernels, block_device(): pl.pallas_call(block_kernel, out_shape=outs, in_specs=[in_vmem] * len(inp...  239 us

profile of v2, /device:TPU:0, one launch (start us, length us, event | category | flops | bytes accessed | tf_op | source)
XLA Modules:
  0.0 250.5 jit_solution(6231350580689013082)
XLA Ops:
  0.7 1.2 reshape.117.refs_5_
  1.9 1.2 reshape.118.refs_7_
  3.1 1.2 reshape.126.refs_18_
  4.4 1.4 copy.49.refs_8_
  5.8 238.6 %shard_map.425 = (bf16[256,768]{1,0:T(8,128)(2,1)}, f32[256,768]{1,0:T(8,128)}, f32[2,48,2304]{2,1,0:T(8,128)}, f32[2,48,768]{2,1,0:T(8,128)}, f32[2,192,768]{2,...) custom-call(bf16[256,768]{1,0:T(8,128)(2,1)} %bitcast.26, s32[2,128]{1,0:T(2,128)} %bitcast.29, ...), custom_call_target="tpu_custom_call" | custom-call | tf_op jit(solution)/shard_map/pallas_call | solution.py:1108
  244.4 4.7 %shard_map.426 = (bf16[256,768]{1,0:T(8,128)(2,1)}, f32[256,768]{1,0:T(8,128)}, f32[96]{0:T(128)}, f32[96]{0:T(128)}, f32[96,2304]{1,0:T(8,128)}, /*index=5*/f32...) custom-call(bf16[256,768]{1,0:T(8,128)(2,1)} %get-tuple-element.53.r, ...), custom_call_target="tpu_custom_call" | custom-call | tf_op jit(solution)/shard_map/pallas_call | solution.py:1125
  249.1 1.4 copy.52

commit v3 on v2

--- a/solution.py
+++ b/solution.py
@@ -108,33 +108,85 @@
 LAGS = 64
 LOW = jnp.bfloat16
 FULL = jnp.float32
+WHOLE, SPLIT, LINE = range(3)
 GATHER_CHUNKS = (
-    (4, 0, 128, False),
-    (0, 768, 768, True),
-    (0, 1536, 768, True),
-    (0, 0, 768, True),
-    (3, 0, 768, False),
-    (3, 768, 768, False),
-    (1, 0, 768, True),
-    (2, 0, 256, True),
-    (3, 1536, 768, False),
-    (2, 256, 256, True),
-    (2, 512, 256, True),
-    (3, 2304, 768, False),
+    (4, 0, 128, WHOLE),
+    (0, 768, 768, SPLIT),
+    (0, 1536, 768, SPLIT),
+    (0, 0, 768, SPLIT),
+    (1, 0, 768, SPLIT),
+    (3, 0, 768, WHOLE),
+    (2, 0, 256, SPLIT),
+    (2, 256, 256, SPLIT),
+    (3, 768, 768, LINE),
+    (2, 512, 256, SPLIT),
+    (3, 1536, 768, WHOLE),
+    (3, 2304, 768, WHOLE),
 )
 REDUCE_GROUPS = (
-    (2, (0, 256, 512), 256, True),
-    (3, (0, 768, 1536, 2304), 768, False),
-    (1, (0,), 768, True),
-    (0, (0, 1536), 768, True),
-    (0, (768,), 768, False),
-    (4, (0,), 128, False),
+    (2, (0, 256), 256, SPLIT),
+    (2, (512,), 256, WHOLE),
+    (3, (0, 1536), 768, WHOLE),
+    (3, (2304,), 768, LINE),
+    (3, (768,), 768, SPLIT),
+    (1, (0,), 768, SPLIT),
+    (0, (0, 512), 512, SPLIT),
+    (0, (1024, 1408), 384, WHOLE),
+    (0, (1792,), 512, SPLIT),
+    (4, (0,), 128, WHOLE),
 )
 REDUCE_ORDER = (
-    (0, 0), (1, 0), (0, 1), (1, 1), (0, 2), (1, 2), (1, 3), (2, 0), (3, 0), (4, 0), (3, 1), (5, 0),
+    (2, 0), (4, 0), (2, 1), (3, 0), (0, 0), (0, 1), (1, 0), (5, 0), (6, 0), (6, 1), (7, 0), (7, 1), (8, 0), (9, 0),
 )
-AHEAD = 3
+(
+    DO_FIRST, DO_NEAR, DO_FAR, DO_SIDE, DO_CROSS, DO_PLACES, DO_UNPACK, DO_NORM1,
+    DO_PROJECT, DO_CONV, DO_MIX, DO_EXPAND, DO_FEED, DO_DRAIN, DO_GCON, DO_GEXP,
+    DO_NORM2B, DO_BACKG, DO_GOUT, DO_CONVB, DO_GIN, DO_BFIRST, DO_NORM1B, DO_SMALL,
+    DO_STAGE, DO_ACORE, DO_AY, DO_AX, DO_AZ1, DO_AZ2, DO_AZ3, DO_FIN,
+    DO_END,
+) = range(33)
+SCHEDULE = (
+    (DO_FIRST, 0), (DO_FIRST, 8), (DO_FIRST, 1), (DO_FIRST, 2), (DO_FIRST, 3), (DO_FIRST, 4),
+    (DO_NEAR, 1), (DO_NEAR, 2), (DO_FIRST, 5), (DO_NEAR, 3), (DO_NEAR, 4), (DO_FAR, 1), (DO_FAR, 2),
+    (DO_NEAR, 0), (DO_PLACES, 0), (DO_FAR, 3), (DO_FAR, 4), (DO_SIDE, 1), (DO_FIRST, 6),
+    (DO_FIRST, 7), (DO_SIDE, 2), (DO_FAR, 0), (DO_FIRST, 9), (DO_FIRST, 10), (DO_FIRST, 11),
+    (DO_NEAR, 8), (DO_CROSS, 1), (DO_NEAR, 6), (DO_SIDE, 4), (DO_NEAR, 9), (DO_SIDE, 3),
+    (DO_SIDE, 0), (DO_CROSS, 2), (DO_NEAR, 7), (DO_FAR, 9), (DO_NEAR, 5), (DO_FAR, 6),
+    (DO_UNPACK, 0), (DO_NORM1, 0), (DO_NEAR, 11), (DO_PROJECT, 1), (DO_FAR, 8), (DO_CROSS, 4),
+    (DO_SIDE, 9), (DO_FAR, 7), (DO_PROJECT, 2), (DO_CONV, 0), (DO_FAR, 5), (DO_CONV, 1),
+    (DO_FAR, 11), (DO_CROSS, 3), (DO_CONV, 2), (DO_CONV, 3), (DO_SIDE, 6), (DO_PROJECT, 0),
+    (DO_NEAR, 10), (DO_SIDE, 8), (DO_SIDE, 5), (DO_SIDE, 7), (DO_CROSS, 9), (DO_MIX, 0),
+    (DO_EXPAND, 0), (DO_SIDE, 11), (DO_FAR, 10), (DO_EXPAND, 1), (DO_CROSS, 6), (DO_CROSS, 7),
+    (DO_EXPAND, 3), (DO_SIDE, 10), (DO_FEED, 0), (DO_GEXP, 0), (DO_STAGE, (2, 0)), (DO_FEED, 1),
+    (DO_GEXP, 1), (DO_STAGE, (4, 0)), (DO_ACORE, (2, 0)), (DO_EXPAND, 2), (DO_FEED, 2),
+    (DO_GEXP, 2), (DO_STAGE, (2, 1)), (DO_ACORE, (4, 0)), (DO_FEED, 3), (DO_DRAIN, 0),
+    (DO_ACORE, (2, 1)), (DO_GCON, 0), (DO_STAGE, (0, 0)), (DO_STAGE, (0, 1)), (DO_STAGE, (1, 0)),
+    (DO_AX, (2, 0)), (DO_NORM2B, 0), (DO_GEXP, 3), (DO_ACORE, (0, 0)), (DO_BACKG, 0),
+    (DO_STAGE, (3, 0)), (DO_AX, (2, 1)), (DO_GOUT, 0), (DO_STAGE, (5, 0)), (DO_AY, (4, 0)),
+    (DO_ACORE, (1, 0)), (DO_ACORE, (3, 0)), (DO_ACORE, (0, 1)), (DO_CONVB, 0), (DO_CONVB, 1),
+    (DO_CONVB, 2), (DO_AZ1, (2, 1)), (DO_AY, (0, 0)), (DO_ACORE, (5, 0)), (DO_AX, (1, 0)),
+    (DO_CONVB, 3), (DO_AY, (0, 1)), (DO_GIN, 1), (DO_AZ1, (2, 0)), (DO_STAGE, (7, 0)), (DO_GIN, 0),
+    (DO_STAGE, (6, 0)), (DO_GIN, 2), (DO_STAGE, (7, 1)), (DO_STAGE, (6, 1)), (DO_AZ1, (3, 0)),
+    (DO_AX, (4, 0)), (DO_ACORE, (7, 0)), (DO_ACORE, (6, 0)), (DO_AX, (0, 0)), (DO_ACORE, (7, 1)),
+    (DO_AX, (0, 1)), (DO_ACORE, (6, 1)), (DO_AY, (5, 0)), (DO_BFIRST, 0), (DO_STAGE, (8, 0)),
+    (DO_AZ1, (4, 0)), (DO_NORM1B, 0), (DO_AX, (7, 0)), (DO_AZ1, (1, 0)), (DO_SMALL, 0),
+    (DO_STAGE, (9, 0)), (DO_AY, (6, 0)), (DO_ACORE, (8, 0)), (DO_AZ2, (2, 1)), (DO_AZ3, (2, 1)),
+    (DO_AX, (7, 1)), (DO_AZ2, (3, 0)), (DO_AZ1, (0, 0)), (DO_ACORE, (9, 0)), (DO_AX, (5, 0)),
+    (DO_AZ2, (1, 0)), (DO_AZ3, (1, 0)), (DO_AZ1, (0, 1)), (DO_AX, (6, 0)), (DO_AY, (6, 1)),
+    (DO_AZ2, (2, 0)), (DO_AY, (8, 0)), (DO_AZ3, (2, 0)), (DO_AZ3, (3, 0)), (DO_AZ1, (7, 1)),
+    (DO_AZ2, (4, 0)), (DO_AX, (9, 0)), (DO_AZ2, (0, 1)), (DO_AZ1, (7, 0)), (DO_AZ2, (0, 0)),
+    (DO_AZ3, (0, 1)), (DO_AX, (6, 1)), (DO_AZ3, (4, 0)), (DO_AZ2, (7, 1)), (DO_AZ3, (7, 1)),
+    (DO_AZ1, (5, 0)), (DO_AZ1, (6, 0)), (DO_AZ2, (7, 0)), (DO_AZ3, (7, 0)), (DO_AZ1, (9, 0)),
+    (DO_AX, (8, 0)), (DO_FIN, (2, 0)), (DO_AZ3, (0, 0)), (DO_AZ1, (6, 1)), (DO_AZ2, (6, 0)),
+    (DO_AX, (3, 0)), (DO_AZ2, (5, 0)), (DO_AZ3, (6, 0)), (DO_AZ3, (5, 0)), (DO_FIN, (7, 0)),
+    (DO_AZ2, (9, 0)), (DO_FIN, (0, 0)), (DO_AZ1, (8, 0)), (DO_AZ2, (6, 1)), (DO_AZ3, (6, 1)),
+    (DO_AZ2, (8, 0)), (DO_FIN, (6, 0)), (DO_AZ3, (9, 0)), (DO_AZ3, (8, 0)), (DO_FIN, (0, 1)),
+    (DO_FIN, (4, 0)), (DO_FIN, (2, 1)), (DO_FIN, (1, 0)), (DO_FIN, (6, 1)), (DO_FIN, (7, 1)),
+    (DO_FIN, (5, 0)), (DO_FIN, (3, 0)), (DO_FIN, (9, 0)), (DO_FIN, (8, 0)), (DO_END, 0),
+)
 SMALL_ROWS = 80
+NORM_ROWS = 128
+INNER_OUT = 8
 
 
 def dot_nn(left_side, right_side):
@@ -203,12 +255,13 @@
     s_inner1, s_first, s_cos1, s_inner2, s_second, s_cos2 = take(6)
     places, left = take(2)
     normed1, proj, short, conv, gated, resid, normed2 = take(7)
-    hidden, post, pre, back_h, gather_out, back_s, back_r, back_m, back_g, bp = take(10)
+    hidden, post, pre, back_h, gather_out, back_s, back_m, bp = take(8)
+    back_r, back_g = back_h, gather_out
     acc96, acc288, accexp = take(3)
     groups = []
-    for matrix, columns, width, split in REDUCE_GROUPS:
-        members = take(7 if split else 6)
-        names = ("core", "x", "z1", "z2", "z3", "last") + (("y",) if split else ())
+    for matrix, columns, width, kind in REDUCE_GROUPS:
+        members = take(7 if kind == SPLIT else 6)
+        names = ("core", "x", "z1", "z2", "z3", "last") + (("y",) if kind == SPLIT else ())
         groups.append(dict(zip(names, members)))
     ag_recv, ag_cross, ag_core, ag_send, own_sem, rs_recv, rs_y, rs_send, rs_end = take(9)
     assert not refs
@@ -249,18 +302,22 @@
     for row, member in enumerate(
         (r_first_gain, r_first_shift, r_direct, r_out_bias, r_second_gain, r_second_shift, r_con_bias)
     ):
-        pack[row : row + 1, 0:96] = member[...].astype(FULL)
+        pack[row : row + 1, 0:96] = member[...].astype(FULL).reshape(1, 96)
+    in_bias, short_b = (m[...].astype(FULL).reshape(1, 288) for m in (r_in_bias, r_short_b))
+    exp_bias = r_exp_bias[...].astype(FULL).reshape(1, 384)
     for block in range(3):
         lanes = 128 if block < 2 else 32
         span = slice(block * 128, block * 128 + lanes)
         top = 8 + block * 8
-        pack[top : top + 1, 0:lanes] = r_in_bias[:, span].astype(FULL)
-        pack[top + 1 : top + 2, 0:lanes] = r_short_b[:, span].astype(FULL)
+        pack[top : top + 1, 0:lanes] = in_bias[:, span]
+        pack[top + 1 : top + 2, 0:lanes] = short_b[:, span]
         pack[top + 2 : top + 5, 0:lanes] = r_short_w[:, span].astype(FULL)
-        pack[top + 5 : top + 6, :] = r_exp_bias[:, block * 128 : block * 128 + 128].astype(FULL)
+        pack[top + 5 : top + 6, :] = exp_bias[:, block * 128 : block * 128 + 128]
     for row, member in enumerate((r_inner_b, r_scale, r_middle_b)):
-        pack[32 + row : 33 + row, 0:8] = member[...].astype(FULL)
-    pack[40:73, 0:8] = r_inner_w[...].astype(FULL)
+        pack[32 + row : 33 + row, 0:8] = member[...].astype(FULL).reshape(1, 8)
+    pack[40:80, :] = jnp.concatenate(
+        [widen(r_inner_w[...].astype(FULL), 128), jnp.zeros((120, 128), FULL)], axis=0
+    ).T[0:40]
     pack[80:88, 0:64] = r_middle_w[...].astype(FULL)
     pack[88:152, 0:96] = r_filter_w[...].astype(FULL)
     own_small[0] = pack[0:80, :].astype(LOW)
@@ -277,14 +334,14 @@
     count = len(chunks)
     cross_index = {}
     for index, chunk in enumerate(chunks):
-        if chunk[3]:
+        if chunk[3] == SPLIT:
             cross_index[index] = len(cross_index)
     NEAR, FAR, SIDE0, SIDE1 = range(4)
     S_NEAR, S_MIRROR, S_BACK, S_SIDE, S_CROSS, S_CORE = range(6)
 
     def part(chunk, quarter):
-        matrix, column, width, split = chunk
-        if split:
+        matrix, column, width, kind = chunk
+        if kind == SPLIT:
             return pl.ds(pl.multiple_of(column + quarter * (width // 2), 128), width // 2)
         return pl.ds(column, width)
 
@@ -294,77 +351,118 @@
     for matrix in range(5):
         pltpu.make_async_copy(own[matrix].at[c], full[matrix].at[z, x, c], own_sem.at[matrix]).start()
 
+    send_groups = []
+    for chunk in chunks:
+        key = chunk[:1] if chunk[0] != 3 else chunk[:2]
+        if key not in send_groups:
+            send_groups.append(key)
+
+    def group_of(chunk):
+        return send_groups.index(chunk[:1] if chunk[0] != 3 else chunk[:2])
+
     def first(index):
         chunk = chunks[index]
-        m = chunk[0]
-        remote(
-            own[m].at[c, :, part(chunk, y)], full[m].at[z, x, c, :, part(chunk, y)],
-            ag_send.at[S_NEAR, m], ag_recv.at[NEAR, index], to_near,
-        ).start()
+        m, s = chunk[0], group_of(chunk)
+        piece = own[m].at[c, :, part(chunk, y)]
+        landing = full[m].at[z, x, c, :, part(chunk, y)]
+        if chunk[3] == LINE:
+            remote(piece, landing, ag_send.at[S_SIDE, s], ag_recv.at[SIDE0, index], to_x).start()
+        else:
+            remote(piece, landing, ag_send.at[S_NEAR, s], ag_recv.at[NEAR, index], to_near).start()
+
+    def line_near(index):
+        chunk = chunks[index]
+        m, s = chunk[0], group_of(chunk)
+        arrived = full[m].at[z, 1 - x, c, :, whole(chunk)]
+        remote(arrived, arrived, ag_send.at[S_SIDE, s], ag_recv.at[SIDE0, index], to_x).wait_recv()
+        both = full[m].at[z, :, c, :, whole(chunk)]
+        remote(both, both, ag_send.at[S_NEAR, s], ag_recv.at[NEAR, index], to_near).start()
+
+    def line_far(index):
+        chunk = chunks[index]
+        m, s = chunk[0], group_of(chunk)
+        arrived = full[m].at[near_z, :, c, :, whole(chunk)]
+        remote(arrived, arrived, ag_send.at[S_NEAR, s], ag_recv.at[NEAR, index], to_near).wait_recv()
+
+        @pl.when(inner)
+        def _():
+            four = full[m].at[own_pair, :, c, :, whole(chunk)]
+            remote(four, four, ag_send.at[S_MIRROR, s], ag_recv.at[FAR, index], to_mirror).start()
+
+    def line_side(index):
+        chunk = chunks[index]
+        m, s = chunk[0], group_of(chunk)
+        four = full[m].at[other_pair, :, c, :, whole(chunk)]
+        remote(four, four, ag_send.at[S_MIRROR, s], ag_recv.at[FAR, index], to_near).wait_recv()
+
+        @pl.when(inner)
+        def _():
+            remote(four, four, ag_send.at[S_BACK, s], ag_recv.at[FAR, index], to_near).start()
+
+        to_core(index)
 
     def near(index):
         chunk = chunks[index]
-        m = chunk[0]
+        if chunk[3] == LINE:
+            return line_near(index)
+        m, s = chunk[0], group_of(chunk)
         arrived = full[m].at[near_z, x, c, :, part(chunk, y)]
-        remote(arrived, arrived, ag_send.at[S_NEAR, m], ag_recv.at[NEAR, index], to_near).wait_recv()
+        remote(arrived, arrived, ag_send.at[S_NEAR, s], ag_recv.at[NEAR, index], to_near).wait_recv()
         both = full[m].at[own_pair, x, c, :, part(chunk, y)]
 
         @pl.when(inner)
         def _():
-            remote(both, both, ag_send.at[S_MIRROR, m], ag_recv.at[FAR, index], to_mirror).start()
-
-        remote(both, both, ag_send.at[S_SIDE, m], ag_recv.at[SIDE0, index], to_x).start()
-        if chunk[3]:
+            remote(both, both, ag_send.at[S_MIRROR, s], ag_recv.at[FAR, index], to_mirror).start()
+
+        remote(both, both, ag_send.at[S_SIDE, s], ag_recv.at[SIDE0, index], to_x).start()
+        if chunk[3] == SPLIT:
             remote(
-                arrived, arrived, ag_send.at[S_CROSS, m], ag_cross.at[0, cross_index[index]], to_y
+                arrived, arrived, ag_send.at[S_CROSS, s], ag_cross.at[0, cross_index[index]], to_y
             ).start()
 
     def far(index):
         chunk = chunks[index]
-        m = chunk[0]
+        if chunk[3] == LINE:
+            return line_far(index)
+        m, s = chunk[0], group_of(chunk)
         both = full[m].at[other_pair, x, c, :, part(chunk, y)]
-        remote(both, both, ag_send.at[S_MIRROR, m], ag_recv.at[FAR, index], to_near).wait_recv()
+        remote(both, both, ag_send.at[S_MIRROR, s], ag_recv.at[FAR, index], to_near).wait_recv()
 
         @pl.when(inner)
         def _():
-            remote(both, both, ag_send.at[S_BACK, m], ag_recv.at[FAR, index], to_near).start()
-
-        remote(both, both, ag_send.at[S_SIDE, m], ag_recv.at[SIDE1, index], to_x).start()
-        if chunk[3]:
+            remote(both, both, ag_send.at[S_BACK, s], ag_recv.at[FAR, index], to_near).start()
+
+        remote(both, both, ag_send.at[S_SIDE, s], ag_recv.at[SIDE1, index], to_x).start()
+        if chunk[3] == SPLIT:
             remote(
-                both, both, ag_send.at[S_CROSS, m], ag_cross.at[1, cross_index[index]], to_y
+                both, both, ag_send.at[S_CROSS, s], ag_cross.at[1, cross_index[index]], to_y
             ).start()
 
     def to_core(index):
         chunk = chunks[index]
-        m = chunk[0]
+        m, s = chunk[0], group_of(chunk)
         piece = full[m].at[:, :, c, :, whole(chunk)]
-        slot = core_slot(index)
-        remote(piece, piece, ag_send.at[S_CORE, m], ag_core.at[slot], to_c).start()
-
-    def core_slot(index):
-        m, column = chunks[index][0], chunks[index][1]
-        return {0: 0, 1: 1, 2: 2, 4: 3}[m] if m != 3 else 4 + column // 768
+        remote(piece, piece, ag_send.at[S_CORE, s], ag_core.at[index], to_c).start()
 
     def side(index):
         chunk = chunks[index]
-        m = chunk[0]
+        if chunk[3] == LINE:
+            return line_side(index)
+        m, s = chunk[0], group_of(chunk)
         for place, slot in ((own_pair, SIDE0), (other_pair, SIDE1)):
             both = full[m].at[place, 1 - x, c, :, part(chunk, y)]
-            remote(both, both, ag_send.at[S_SIDE, m], ag_recv.at[slot, index], to_x).wait_recv()
-        if chunk[3]:
+            remote(both, both, ag_send.at[S_SIDE, s], ag_recv.at[slot, index], to_x).wait_recv()
+        if chunk[3] == SPLIT:
             column = full[m].at[:, 1 - x, c, :, part(chunk, y)]
             remote(
-                column, column, ag_send.at[S_CROSS, m], ag_cross.at[2, cross_index[index]], to_y
+                column, column, ag_send.at[S_CROSS, s], ag_cross.at[2, cross_index[index]], to_y
             ).start()
         else:
             to_core(index)
 
     def cross(index):
         chunk = chunks[index]
-        if not chunk[3]:
-            return
-        m = chunk[0]
+        m, s = chunk[0], group_of(chunk)
         for slot, piece in enumerate(
             (
                 full[m].at[near_z, x, c, :, part(chunk, 1 - y)],
@@ -373,28 +471,21 @@
             )
         ):
             remote(
-                piece, piece, ag_send.at[S_CROSS, m], ag_cross.at[slot, cross_index[index]], to_y
+                piece, piece, ag_send.at[S_CROSS, s], ag_cross.at[slot, cross_index[index]], to_y
             ).wait_recv()
         to_core(index)
 
-    def settled(m, column=None):
-        if column is None:
-            piece, slot = full[m].at[:, :, 1 - c], {0: 0, 1: 1, 2: 2, 4: 3}[m]
-        else:
-            piece, slot = full[m].at[:, :, 1 - c, :, pl.ds(column, 768)], 4 + column // 768
-        remote(piece, piece, ag_send.at[S_CORE, m], ag_core.at[slot], to_c).wait_recv()
-
-    plan = ((0, near), (0, far), (1, side), (1, cross))
-
-    def tick(step):
-        if step + AHEAD < count:
-            first(step + AHEAD)
-        for delay, action in plan:
-            if 0 <= step - delay < count:
-                action(step - delay)
-
-    for index in range(AHEAD):
-        first(index)
+    waited = set()
+
+    def settled(m, low, high):
+        for index, chunk in enumerate(chunks):
+            inside = chunk[0] == m and chunk[1] < high and chunk[1] + chunk[2] > low
+            if inside and index not in waited:
+                waited.add(index)
+                piece = full[m].at[:, :, 1 - c, :, whole(chunk)]
+                send = ag_send.at[S_CORE, group_of(chunk)]
+                remote(piece, piece, send, ag_core.at[index], to_c).wait_recv()
+
     for matrix in range(5):
         pltpu.make_async_copy(own[matrix].at[c], full[matrix].at[z, x, c], own_sem.at[matrix]).wait()
 
@@ -510,7 +601,7 @@
         def gate(rows):
             gated[rows, :] = (conv[rows, :] * short[0, rows, :]).astype(LOW)
 
-        row_blocks(16, gate)
+        row_blocks(NORM_ROWS, gate)
         resid[...] = dot_nn(gated[...], matrix_of(1, pl.ds(0, 768), 768))
 
         def finish_rows(rows):
@@ -519,13 +610,15 @@
             unit, _ = center(values)
             normed2[rows, :] = (unit * v96[4:5, :] + v96[5:6, :]).astype(LOW)
 
-        row_blocks(16, finish_rows)
+        row_blocks(NORM_ROWS, finish_rows)
 
     def expand(k):
         span = slice(k * 768, k * 768 + 768)
         hidden[:, span] = (
             dot_nn(normed2[...], matrix_of(3, pl.ds(k * 768, 768), 768)) + vexp[:, span]
         )
+
+    fed_before = []
 
     def feed(k):
         span = slice(k * 768, k * 768 + 768)
@@ -549,99 +642,98 @@
         row_blocks(16, bend)
         out_part = dot_nn(post[:, span], full[2][k].reshape(768, 768))
         back_part = dot_nt(pre[:, span], matrix_of(3, pl.ds(k * 768, 768), 768))
-        if k == 0:
+        if not fed_before:
             gather_out[...] = out_part
             back_s[...] = back_part
+            fed_before.append(k)
         else:
             gather_out[...] += out_part
             back_s[...] += back_part
 
-    find_places()
-    tick(0)
-    tick(1)
-    settled(4)
-    unpack_small()
-    row_blocks(16, norm_first)
-    tick(2)
-    tick(3)
-    tick(4)
-    tick(5)
-    settled(0)
-    project(1)
-    tick(6)
-    project(2)
-    tick(7)
-    convolve(0, 4)
-    tick(8)
-    convolve(4, 8)
-    tick(9)
-    convolve(8, 12)
-    tick(10)
-    project(0)
-    settled(1)
-    tick(11)
-    mix_out()
-    tick(12)
-    settled(3, 0)
-    expand(0)
-    settled(3, 768)
-    expand(1)
-    settled(3, 1536)
-    expand(2)
-    settled(2)
-    for k in range(3):
-        feed(k)
-    settled(3, 2304)
-    expand(3)
-    feed(3)
-
-    for m in range(5):
-        quarter = {0: 1152, 1: 384, 2: 384, 3: 3072, 4: 128}[m]
-        wide = full[m].shape[4]
-        one = full[m].at[0, 0, 0, :, pl.ds(0, quarter)]
-        two = full[m].at[pl.ds(0, 2), 0, 0, :, pl.ds(0, quarter)]
-        four = full[m].at[:, 0, 0, :, pl.ds(0, quarter)]
-        remote(one, one, ag_send.at[S_NEAR, m], ag_recv.at[NEAR, 0], to_near).wait_send()
-
-        @pl.when(inner)
-        def _(two=two, m=m):
-            remote(two, two, ag_send.at[S_MIRROR, m], ag_recv.at[FAR, 0], to_near).wait_send()
-            remote(two, two, ag_send.at[S_BACK, m], ag_recv.at[FAR, 0], to_near).wait_send()
-
-        remote(four, four, ag_send.at[S_SIDE, m], ag_recv.at[FAR, 0], to_near).wait_send()
-        if m not in (3, 4):
-            near_one = full[m].at[pl.ds(0, 3), 0, 0, :, pl.ds(0, quarter)]
-            remote(near_one, near_one, ag_send.at[S_CROSS, m], ag_recv.at[FAR, 0], to_near).wait_send()
-            remote(four, four, ag_send.at[S_CROSS, m], ag_recv.at[FAR, 0], to_near).wait_send()
-        everything = full[m].at[:, :, 0, :, pl.ds(0, wide)]
-        remote(everything, everything, ag_send.at[S_CORE, m], ag_recv.at[FAR, 0], to_near).wait_send()
+    drained = set()
+
+    def drain(m, low, high):
+        for s, key in enumerate(send_groups):
+            members = [
+                chunk for chunk in chunks
+                if group_of(chunk) == s and m == chunk[0]
+                and chunk[1] < high and chunk[1] + chunk[2] > low
+            ]
+            if not members or s in drained:
+                continue
+            drained.add(s)
+            members = [chunk for chunk in chunks if group_of(chunk) == s]
+            kind = members[0][3]
+            assert all(chunk[3] == kind for chunk in members)
+            wide = sum(chunk[2] for chunk in members)
+            thin = wide // 2 if kind == SPLIT else wide
+
+            def gone(slot, planes, rows, width=thin, s=s):
+                ref = full[m].at[pl.ds(0, planes), pl.ds(0, rows), 0, :, pl.ds(0, width)]
+                remote(ref, ref, ag_send.at[slot, s], ag_recv.at[FAR, 0], to_near).wait_send()
+
+            if kind == LINE:
+                gone(S_SIDE, 1, 1)
+                gone(S_NEAR, 2, 1)
+            else:
+                gone(S_NEAR, 1, 1)
+                gone(S_SIDE, 4, 1)
+
+            @pl.when(inner)
+            def _(gone=gone, kind=kind):
+                gone(S_MIRROR, 2, 2 if kind == LINE else 1)
+                gone(S_BACK, 2, 2 if kind == LINE else 1)
+
+            if kind == SPLIT:
+                gone(S_CROSS, 3, 1)
+                gone(S_CROSS, 4, 1)
+            gone(S_CORE, 4, 2, wide)
 
     position = {}
     split_position = {}
     for index, key in enumerate(REDUCE_ORDER):
         position[key] = index
-        if REDUCE_GROUPS[key[0]][3]:
+        if REDUCE_GROUPS[key[0]][3] == SPLIT:
             split_position[key] = len(split_position)
     R_CORE, R_X, R_Z1, R_Z2, R_Z3, R_LAST = range(6)
     W_CORE, W_Y, W_X, W_Z1, W_Z2, W_Z3, W_LAST, W_END = range(8)
 
     def info(key):
         g, i = key
-        matrix, columns, width, split = REDUCE_GROUPS[g]
-        return g, i, matrix, columns[i], width, split, groups[g], position[key]
+        matrix, columns, width, kind = REDUCE_GROUPS[g]
+        return g, i, matrix, columns[i], width, kind, groups[g], position[key]
 
     def halves(width, which):
         return pl.ds(pl.multiple_of(which * (width // 2), 128), width // 2)
 
     def stage(key):
-        g, i, m, column, width, split, buf, n = info(key)
+        g, i, m, column, width, kind, buf, n = info(key)
         remote(
             grads[m].at[:, :, 1 - c, :, pl.ds(column, width)], buf["core"].at[i],
             rs_send.at[W_CORE, g], rs_recv.at[R_CORE, n], to_c,
         ).start()
 
+    def running(key):
+        g, i, m, column, width, kind, buf, n = info(key)
+        return buf["core"] if kind == LINE else buf["x"]
+
+    def send_line(key):
+        g, i, m, column, width, kind, buf, n = info(key)
+        sums_ref = running(key)
+
+        @pl.when(jnp.logical_not(inner))
+        def _():
+            remote(
+                sums_ref.at[i, other_pair], buf["z1"].at[i],
+                rs_send.at[W_Z1, g], rs_recv.at[R_Z1, n], to_near,
+            ).start()
+            remote(
+                sums_ref.at[i, near_z], buf["z3"].at[i],
+                rs_send.at[W_Z3, g], rs_recv.at[R_Z3, n], to_near,
+            ).start()
+
     def add_core(key):
-        g, i, m, column, width, split, buf, n = info(key)
+        g, i, m, column, width, kind, buf, n = info(key)
         landing = buf["core"].at[i]
         remote(landing, landing, rs_send.at[W_CORE, g], rs_recv.at[R_CORE, n], to_c).wait_recv()
 
@@ -651,21 +743,21 @@
             return carry
 
         lax.fori_loop(0, 8, body, 0)
-        if split:
+        if kind == SPLIT:
             remote(
                 buf["core"].at[i, :, :, :, halves(width, 1 - y)], buf["y"].at[i],
                 rs_send.at[W_Y, g], rs_y.at[split_position[key]], to_y,
             ).start()
-        else:
+        elif kind == WHOLE:
             remote(
                 buf["core"].at[i, :, 1 - x], buf["x"].at[i],
                 rs_send.at[W_X, g], rs_recv.at[R_X, n], to_x,
             ).start()
+        else:
+            send_line(key)
 
     def add_y(key):
-        g, i, m, column, width, split, buf, n = info(key)
-        if not split:
-            return
+        g, i, m, column, width, kind, buf, n = info(key)
         landing = buf["y"].at[i]
         remote(landing, landing, rs_send.at[W_Y, g], rs_y.at[split_position[key]], to_y).wait_recv()
 
@@ -679,31 +771,33 @@
             buf["y"].at[i, :, 1 - x], buf["x"].at[i], rs_send.at[W_X, g], rs_recv.at[R_X, n], to_x
         ).start()
 
+    def send_last(key):
+        g, i, m, column, width, kind, buf, n = info(key)
+        remote(
+            buf["last"].at[i, 0], buf["last"].at[i, 1],
+            rs_send.at[W_LAST, g], rs_recv.at[R_LAST, n], to_y,
+        ).start()
+
     def add_x(key):
-        g, i, m, column, width, split, buf, n = info(key)
+        g, i, m, column, width, kind, buf, n = info(key)
         landing = buf["x"].at[i]
         remote(landing, landing, rs_send.at[W_X, g], rs_recv.at[R_X, n], to_x).wait_recv()
-        own_part = buf["y"] if split else buf["core"]
+        if kind == LINE:
+            buf["last"][i, 0] = buf["core"][i, z, x] + buf["x"][i]
+            send_last(key)
+            return
+        own_part = buf["y"] if kind == SPLIT else buf["core"]
 
         def body(step, carry):
             buf["x"][i, step] = buf["x"][i, step] + own_part[i, step, x]
             return carry
 
         lax.fori_loop(0, 4, body, 0)
-
-        @pl.when(jnp.logical_not(inner))
-        def _():
-            remote(
-                buf["x"].at[i, other_pair], buf["z1"].at[i],
-                rs_send.at[W_Z1, g], rs_recv.at[R_Z1, n], to_near,
-            ).start()
-            remote(
-                buf["x"].at[i, near_z], buf["z3"].at[i],
-                rs_send.at[W_Z3, g], rs_recv.at[R_Z3, n], to_near,
-            ).start()
+        send_line(key)
 
     def add_z1(key):
-        g, i, m, column, width, split, buf, n = info(key)
+        g, i, m, column, width, kind, buf, n = info(key)
+        sums_ref = running(key)
 
         @pl.when(inner)
         def _():
@@ -711,14 +805,15 @@
             remote(landing, landing, rs_send.at[W_Z1, g], rs_recv.at[R_Z1, n], to_near).wait_recv()
             for step in range(2):
                 at = (1 - pair) * 2 + step
-                buf["x"][i, at] = buf["x"][i, at] + buf["z1"][i, step]
+                sums_ref[i, at] = sums_ref[i, at] + buf["z1"][i, step]
             remote(
-                buf["x"].at[i, other_pair], buf["z2"].at[i],
+                sums_ref.at[i, other_pair], buf["z2"].at[i],
                 rs_send.at[W_Z2, g], rs_recv.at[R_Z2, n], to_mirror,
             ).start()
 
     def add_z2(key):
-        g, i, m, column, width, split, buf, n = info(key)
+        g, i, m, column, width, kind, buf, n = info(key)
+        sums_ref = running(key)
 
         @pl.when(inner)
         def _():
@@ -726,27 +821,31 @@
             remote(landing, landing, rs_send.at[W_Z2, g], rs_recv.at[R_Z2, n], to_mirror).wait_recv()
             for step in range(2):
                 at = pair * 2 + step
-                buf["x"][i, at] = buf["x"][i, at] + buf["z2"][i, step]
+                sums_ref[i, at] = sums_ref[i, at] + buf["z2"][i, step]
             remote(
-                buf["x"].at[i, near_z], buf["z3"].at[i],
+                sums_ref.at[i, near_z], buf["z3"].at[i],
                 rs_send.at[W_Z3, g], rs_recv.at[R_Z3, n], to_near,
             ).start()
 
     def add_z3(key):
-        g, i, m, column, width, split, buf, n = info(key)
+        g, i, m, column, width, kind, buf, n = info(key)
         landing = buf["z3"].at[i]
         remote(landing, landing, rs_send.at[W_Z3, g], rs_recv.at[R_Z3, n], to_near).wait_recv()
+        if kind == LINE:
+            buf["core"][i, z] = buf["core"][i, z] + buf["z3"][i]
+            remote(
+                buf["core"].at[i, z, 1 - x], buf["x"].at[i],
+                rs_send.at[W_X, g], rs_recv.at[R_X, n], to_x,
+            ).start()
+            return
         buf["last"][i, 0] = buf["x"][i, z] + buf["z3"][i]
-        remote(
-            buf["last"].at[i, 0], buf["last"].at[i, 1],
-            rs_send.at[W_LAST, g], rs_recv.at[R_LAST, n], to_y,
-        ).start()
+        send_last(key)
 
     def finish(key):
-        g, i, m, column, width, split, buf, n = info(key)
+        g, i, m, column, width, kind, buf, n = info(key)
         landing = buf["last"].at[i, 1]
         remote(landing, landing, rs_send.at[W_LAST, g], rs_recv.at[R_LAST, n], to_y).wait_recv()
-        if split:
+        if kind == SPLIT:
             for which, slot in ((y, 0), (1 - y, 1)):
                 columns = pl.ds(pl.multiple_of(column + which * (width // 2), 128), width // 2)
                 sums[m][c, :, columns] = buf["last"][i, slot].astype(FULL)
@@ -757,25 +856,11 @@
         piece = sums[m].at[c, :, pl.ds(column, width)]
         remote(piece, piece, rs_send.at[W_END, g], rs_end.at[g], to_c).start()
 
-    reduce_plan = (
-        (0, add_core), (1, add_y), (2, add_x), (3, add_z1), (4, add_z2), (5, add_z3), (6, finish),
-    )
-    steps_left = [0]
-
-    def advance(limit=None):
-        step = steps_left[0]
-        steps_left[0] += 1
-        for delay, action in reduce_plan:
-            if 0 <= step - delay < len(REDUCE_ORDER):
-                action(REDUCE_ORDER[step - delay])
-
-    def grad_contract(i):
-        columns = pl.ds(i * 256, 256)
-
+    def grad_contract():
         def body(s, carry):
             lanes = pl.ds(pl.multiple_of(s * 384, 128), 384)
-            value = dot_tn(post[:, lanes], cot[:, columns]).astype(LOW)
-            full[2][s // 2, s % 2, :, :, columns] = value.reshape(2, 192, 256)
+            value = dot_tn(post[:, lanes], cot[...]).astype(LOW)
+            full[2][s // 2, s % 2] = value.reshape(2, 192, 768)
             return carry
 
         lax.fori_loop(0, 8, body, 0)
@@ -915,63 +1000,83 @@
             )
             g_small[a, b, 1, 72:80, :] = jnp.zeros((8, 128), FULL)
 
-    grad_contract(0)
-    stage((0, 0))
-    grad_expand(0)
-    stage((1, 0))
-    grad_contract(1)
-    stage((0, 1))
-    advance()
-    grad_expand(1)
-    stage((1, 1))
-    grad_contract(2)
-    stage((0, 2))
-    advance()
-    row_blocks(16, norm_second_back)
-    grad_expand(2)
-    stage((1, 2))
-    advance()
-    grad_expand(3)
-    stage((1, 3))
-    advance()
-    back_g[...] = dot_nt(back_m[...], matrix_of(1, pl.ds(0, 768), 768))
-    grad_rows(gated, back_m[...], g_out, pl.ds(0, 768), 768)
-    stage((2, 0))
-    advance()
-    convolve_back(0, 3)
-    advance()
-    convolve_back(3, 6)
-    advance()
-    convolve_back(6, 9)
-    advance()
-    convolve_back(9, 12)
-    for key, k in (((3, 0), 0), ((4, 0), 1), ((3, 1), 2)):
-        grad_rows(normed1, bp[k], g_in, pl.ds(k * 768, 768), 768)
-        stage(key)
-        advance()
-    for k in range(3):
-        value = dot_nt(bp[k], matrix_of(0, pl.ds(k * 768, 768), 768))
-        if k == 0:
-            back_s[...] = value
-        else:
-            back_s[...] += value
-    row_blocks(16, norm_first_back)
-    small_grads()
-    stage((5, 0))
-    while steps_left[0] < len(REDUCE_ORDER) + 6:
-        advance()
-
-    for g, (matrix, columns, width, split) in enumerate(REDUCE_GROUPS):
+    def back_gate():
+        back_g[...] = dot_nt(back_m[...], matrix_of(1, pl.ds(0, 768), 768))
+
+    def back_first():
+        for k in range(3):
+            value = dot_nt(bp[k], matrix_of(0, pl.ds(k * 768, 768), 768))
+            if k == 0:
+                back_s[...] = value
+            else:
+                back_s[...] += value
+
+    def unpack(k):
+        settled(4, 0, 128)
+        unpack_small()
+
+    def projected(k):
+        settled(0, k * 768, k * 768 + 768)
+        project(k)
+
+    def mix(k):
+        settled(1, 0, 768)
+        mix_out()
+
+    def expanded(k):
+        settled(3, k * 768, k * 768 + 768)
+        expand(k)
+
+    def fed(k):
+        settled(2, 0, 768)
+        feed(k)
+
+    def expand_back(k):
+        drain(3, k * 768, k * 768 + 768)
+        grad_expand(k)
+
+    def end(k):
+        for m in range(5):
+            drain(m, 0, full[m].shape[4])
+
+    actions = {
+        DO_FIRST: first, DO_NEAR: near, DO_FAR: far, DO_SIDE: side, DO_CROSS: cross,
+        DO_PLACES: lambda k: find_places(),
+        DO_UNPACK: unpack,
+        DO_NORM1: lambda k: row_blocks(NORM_ROWS, norm_first),
+        DO_PROJECT: projected,
+        DO_CONV: lambda k: convolve(3 * k, 3 * k + 3),
+        DO_MIX: mix,
+        DO_EXPAND: expanded,
+        DO_FEED: fed,
+        DO_DRAIN: lambda k: drain(2, 0, 768),
+        DO_GCON: lambda k: grad_contract(),
+        DO_GEXP: expand_back,
+        DO_NORM2B: lambda k: row_blocks(NORM_ROWS, norm_second_back),
+        DO_BACKG: lambda k: back_gate(),
+        DO_GOUT: lambda k: grad_rows(gated, back_m[...], g_out, pl.ds(0, 768), 768),
+        DO_CONVB: lambda k: convolve_back(3 * k, 3 * k + 3),
+        DO_GIN: lambda k: grad_rows(normed1, bp[k], g_in, pl.ds(k * 768, 768), 768),
+        DO_BFIRST: lambda k: back_first(),
+        DO_NORM1B: lambda k: row_blocks(NORM_ROWS, norm_first_back),
+        DO_SMALL: lambda k: small_grads(),
+        DO_STAGE: stage, DO_ACORE: add_core, DO_AY: add_y, DO_AX: add_x, DO_AZ1: add_z1,
+        DO_AZ2: add_z2, DO_AZ3: add_z3, DO_FIN: finish, DO_END: end,
+    }
+    for name, which in SCHEDULE:
+        actions[name](which)
+
+    for g, (matrix, columns, width, kind) in enumerate(REDUCE_GROUPS):
         piece = sums[matrix].at[1 - c, :, pl.ds(0, width * len(columns))]
         remote(piece, piece, rs_send.at[W_END, g], rs_end.at[g], to_c).wait_recv()
-    for g, (matrix, columns, width, split) in enumerate(REDUCE_GROUPS):
+    for g, (matrix, columns, width, kind) in enumerate(REDUCE_GROUPS):
         buf = groups[g]
 
         def leave(kind, ref, g=g):
             remote(ref, ref, rs_send.at[kind, g], rs_end.at[g], to_c).wait_send()
 
         leave(W_CORE, buf["core"])
-        if split:
+        if kind == SPLIT:
             leave(W_Y, buf["y"])
         leave(W_X, buf["x"])
         leave(W_Z3, buf["z3"])
@@ -1010,7 +1115,8 @@
     o_exp_bias[...] = wide[5:6].reshape(384)
     for row, target in enumerate((o_inner_b, o_scale, o_middle_b)):
         target[...] = s_small[0, 32 + row : 33 + row, 0:8].reshape(8)
-    o_inner_w[...] = s_small[0, 40:73, 0:8]
+    tile = jnp.concatenate([s_small[0, 40:80, :], jnp.zeros((88, 128), FULL)], axis=0).T
+    o_inner_w[...] = tile[0:8, 0:33]
     o_middle_w[...] = s_small[1, 0:8, 0:64]
     o_filter_w[...] = s_small[1, 8:72, 0:96]
 
@@ -1040,9 +1146,6 @@
     rows = blocks * length
     features, decay = filter_constants(length, width)
 
-    def line(member):
-        return member.reshape(1, -1) if member.ndim == 1 else member
-
     small_members = (
         first_gain, first_shift, input_bias, short_weight, short_bias, inner_weight, inner_bias,
         sine_scale, middle_weight, middle_bias, filter_weight, direct_gain, output_bias,
@@ -1056,7 +1159,7 @@
     inputs = (
         tokens.reshape(rows, width), segment_ids.reshape(blocks, length),
         cotangent.reshape(rows, width),
-    ) + tuple(line(m) for m in small_members) + tuple(shards) + (
+    ) + tuple(m.T if m is inner_weight else m for m in small_members) + tuple(shards) + (
         jnp.asarray(features), jnp.asarray(decay),
     )
     shapes = [m.shape[1:] for m in shards] + [(SMALL_ROWS, 128)]
@@ -1065,7 +1168,7 @@
         jax.ShapeDtypeStruct((rows, width), FULL),
     ] + [jax.ShapeDtypeStruct((2,) + s, FULL) for s in shapes]
     count = len(GATHER_CHUNKS)
-    crossing = sum(1 for chunk in GATHER_CHUNKS if chunk[3])
+    crossing = sum(1 for chunk in GATHER_CHUNKS if chunk[3] == SPLIT)
     vm = pltpu.VMEM
     scratch = [vm((4, 2, 2) + s, LOW) for s in shapes]
     scratch += [
@@ -1083,25 +1186,26 @@
         vm((rows, width), LOW),
         vm((rows, 4 * width), FULL), vm((rows, 4 * width), LOW), vm((rows, 4 * width), LOW),
         vm((rows, width), FULL), vm((rows, width), FULL), vm((rows, width), FULL),
-        vm((rows, width), FULL), vm((rows, width), LOW), vm((rows, width), FULL),
-        vm((3, rows, width), LOW),
+        vm((rows, width), LOW), vm((3, rows, width), LOW),
         vm((7, 8, width), FULL), vm((5, 8, 3 * width), FULL), vm((8, 4 * width), FULL),
     ]
-    for matrix, columns, span, split in REDUCE_GROUPS:
+    for matrix, columns, span, kind in REDUCE_GROUPS:
         n, high = len(columns), shapes[matrix][0]
-        kind = FULL if matrix == 4 else LOW
-        v = span // 2 if split else span
+        of = FULL if matrix == 4 else LOW
+        v = span // 2 if kind == SPLIT else span
+        side_planes, line_planes = ((), (2,)) if kind == LINE else ((4,), ())
         scratch += [
-            vm((n, 4, 2, high, span), kind), vm((n, 4, high, v), kind), vm((n, 2, high, v), kind),
-            vm((n, 2, high, v), kind), vm((n, high, v), kind), vm((n, 2, high, v), kind),
+            vm((n, 4, 2, high, span), of), vm((n,) + side_planes + (high, v), of),
+            vm((n, 2) + line_planes + (high, v), of), vm((n, 2) + line_planes + (high, v), of),
+            vm((n,) + line_planes + (high, v), of), vm((n, 2, high, v), of),
         ]
-        if split:
-            scratch.append(vm((n, 4, 2, high, v), kind))
+        if kind == SPLIT:
+            scratch.append(vm((n, 4, 2, high, v), of))
     total = len(REDUCE_ORDER)
-    splits = sum(len(g[1]) for g in REDUCE_GROUPS if g[3])
+    splits = sum(len(g[1]) for g in REDUCE_GROUPS if g[3] == SPLIT)
     dma = pltpu.SemaphoreType.DMA
     scratch += [
-        dma((4, count)), dma((3, crossing)), dma((8,)), dma((6, 5)), dma((5,)),
+        dma((4, count)), dma((3, crossing)), dma((count,)), dma((6, 8)), dma((5,)),
         dma((6, total)), dma((splits,)), dma((8, len(REDUCE_GROUPS))), dma((len(REDUCE_GROUPS),)),
     ]
     in_vmem = pl.BlockSpec(memory_space=pltpu.VMEM)
@@ -1121,13 +1225,16 @@
         output_weight, output_bias, second_gain, second_shift, expand_weight, expand_bias,
         contract_weight, contract_bias,
     )
-    final = [outs[0], outs[1]] + [jax.ShapeDtypeStruct(m.shape, FULL) for m in members]
+    final = [outs[0], outs[1]] + [
+        jax.ShapeDtypeStruct(m.shape[::-1] if m is inner_weight else m.shape, FULL) for m in members
+    ]
     done = pl.pallas_call(
         unpack_kernel,
         out_shape=final,
         in_specs=[in_vmem] * 7,
         out_specs=[in_vmem] * len(final),
     )(*parts)
+    done = [m.T if n == INNER_OUT else m for n, m in enumerate(done)]
     return (done[0].reshape(tokens.shape), done[1].reshape(tokens.shape)) + tuple(done[2:])
 
 

time: 251 us -> 150 us (0.60)
  Pallas kernels: 243 us -> 149 us
  local copies, waits for them, and re-layouts: 6.49 us -> 0 us
    pallas_call x1, Pallas kernels: 239 us -> 145 us  [block_device(): pl.pallas_call(block_kernel, out_shape=outs, in_specs=[in_vmem] * len(inp...]
    reshape x3 -> x0, local copies, waits for them, and re-layouts: 3.73 us -> none  [line(): return member.reshape(1, -1) if member.ndim == 1 else member]
    unnamed x2 -> x0, local copies, waits for them, and re-layouts: 2.76 us -> none
where the time goes in v3:
time: 150 us
  Pallas kernels  149 us (99%)
    pallas_call x1, Pallas kernels, block_device(): pl.pallas_call(block_kernel, out_shape=outs, in_specs=[in_vmem] * len(inp...  145 us
    pallas_call x1, Pallas kernels, block_device(): pl.pallas_call(unpack_kernel, out_shape=final, in_specs=[in_vmem] * 7, ou...  4.68 us

profile of v3, /device:TPU:0, one launch (start us, length us, event | category | flops | bytes accessed | tf_op | source)
XLA Modules:
  0.0 150.1 jit_solution(5280114761568035676)
XLA Ops:
  0.7 144.6 %shard_map.425 = (bf16[256,768]{1,0:T(8,128)(2,1)}, f32[256,768]{1,0:T(8,128)}, f32[2,48,2304]{2,1,0:T(8,128)}, f32[2,48,768]{2,1,0:T(8,128)}, f32[2,192,768]{2,...) custom-call(bf16[256,768]{1,0:T(8,128)(2,1)} %bitcast.18, s32[2,128]{1,0:T(2,128)} %bitcast.22, ...), custom_call_target="tpu_custom_call" | custom-call | tf_op jit(solution)/shard_map/pallas_call | solution.py:1212
  145.3 4.7 %shard_map.426 = (bf16[256,768]{1,0:T(8,128)(2,1)}, f32[256,768]{1,0:T(8,128)}, f32[96]{0:T(128)}, f32[96]{0:T(128)}, f32[96,2304]{1,0:T(8,128)}, /*index=5*/f32...) custom-call(bf16[256,768]{1,0:T(8,128)(2,1)} %get-tuple-element.53.r, ...), custom_call_target="tpu_custom_call" | custom-call | tf_op jit(solution)/shard_map/pallas_call | solution.py:1231

commit v4 on v3

--- a/solution.py
+++ b/solution.py
@@ -115,13 +115,14 @@
     (0, 1536, 768, SPLIT),
     (0, 0, 768, SPLIT),
     (1, 0, 768, SPLIT),
-    (3, 0, 768, WHOLE),
+    (3, 0, 768, LINE),
     (2, 0, 256, SPLIT),
     (2, 256, 256, SPLIT),
-    (3, 768, 768, LINE),
     (2, 512, 256, SPLIT),
+    (3, 768, 768, WHOLE),
     (3, 1536, 768, WHOLE),
-    (3, 2304, 768, WHOLE),
+    (3, 2304, 384, WHOLE),
+    (3, 2688, 384, WHOLE),
 )
 REDUCE_GROUPS = (
     (2, (0, 256), 256, SPLIT),
@@ -146,45 +147,46 @@
     DO_END,
 ) = range(33)
 SCHEDULE = (
-    (DO_FIRST, 0), (DO_FIRST, 8), (DO_FIRST, 1), (DO_FIRST, 2), (DO_FIRST, 3), (DO_FIRST, 4),
-    (DO_NEAR, 1), (DO_NEAR, 2), (DO_FIRST, 5), (DO_NEAR, 3), (DO_NEAR, 4), (DO_FAR, 1), (DO_FAR, 2),
-    (DO_NEAR, 0), (DO_PLACES, 0), (DO_FAR, 3), (DO_FAR, 4), (DO_SIDE, 1), (DO_FIRST, 6),
-    (DO_FIRST, 7), (DO_SIDE, 2), (DO_FAR, 0), (DO_FIRST, 9), (DO_FIRST, 10), (DO_FIRST, 11),
-    (DO_NEAR, 8), (DO_CROSS, 1), (DO_NEAR, 6), (DO_SIDE, 4), (DO_NEAR, 9), (DO_SIDE, 3),
-    (DO_SIDE, 0), (DO_CROSS, 2), (DO_NEAR, 7), (DO_FAR, 9), (DO_NEAR, 5), (DO_FAR, 6),
-    (DO_UNPACK, 0), (DO_NORM1, 0), (DO_NEAR, 11), (DO_PROJECT, 1), (DO_FAR, 8), (DO_CROSS, 4),
-    (DO_SIDE, 9), (DO_FAR, 7), (DO_PROJECT, 2), (DO_CONV, 0), (DO_FAR, 5), (DO_CONV, 1),
-    (DO_FAR, 11), (DO_CROSS, 3), (DO_CONV, 2), (DO_CONV, 3), (DO_SIDE, 6), (DO_PROJECT, 0),
-    (DO_NEAR, 10), (DO_SIDE, 8), (DO_SIDE, 5), (DO_SIDE, 7), (DO_CROSS, 9), (DO_MIX, 0),
-    (DO_EXPAND, 0), (DO_SIDE, 11), (DO_FAR, 10), (DO_EXPAND, 1), (DO_CROSS, 6), (DO_CROSS, 7),
-    (DO_EXPAND, 3), (DO_SIDE, 10), (DO_FEED, 0), (DO_GEXP, 0), (DO_STAGE, (2, 0)), (DO_FEED, 1),
-    (DO_GEXP, 1), (DO_STAGE, (4, 0)), (DO_ACORE, (2, 0)), (DO_EXPAND, 2), (DO_FEED, 2),
-    (DO_GEXP, 2), (DO_STAGE, (2, 1)), (DO_ACORE, (4, 0)), (DO_FEED, 3), (DO_DRAIN, 0),
-    (DO_ACORE, (2, 1)), (DO_GCON, 0), (DO_STAGE, (0, 0)), (DO_STAGE, (0, 1)), (DO_STAGE, (1, 0)),
-    (DO_AX, (2, 0)), (DO_NORM2B, 0), (DO_GEXP, 3), (DO_ACORE, (0, 0)), (DO_BACKG, 0),
-    (DO_STAGE, (3, 0)), (DO_AX, (2, 1)), (DO_GOUT, 0), (DO_STAGE, (5, 0)), (DO_AY, (4, 0)),
-    (DO_ACORE, (1, 0)), (DO_ACORE, (3, 0)), (DO_ACORE, (0, 1)), (DO_CONVB, 0), (DO_CONVB, 1),
-    (DO_CONVB, 2), (DO_AZ1, (2, 1)), (DO_AY, (0, 0)), (DO_ACORE, (5, 0)), (DO_AX, (1, 0)),
-    (DO_CONVB, 3), (DO_AY, (0, 1)), (DO_GIN, 1), (DO_AZ1, (2, 0)), (DO_STAGE, (7, 0)), (DO_GIN, 0),
-    (DO_STAGE, (6, 0)), (DO_GIN, 2), (DO_STAGE, (7, 1)), (DO_STAGE, (6, 1)), (DO_AZ1, (3, 0)),
-    (DO_AX, (4, 0)), (DO_ACORE, (7, 0)), (DO_ACORE, (6, 0)), (DO_AX, (0, 0)), (DO_ACORE, (7, 1)),
-    (DO_AX, (0, 1)), (DO_ACORE, (6, 1)), (DO_AY, (5, 0)), (DO_BFIRST, 0), (DO_STAGE, (8, 0)),
-    (DO_AZ1, (4, 0)), (DO_NORM1B, 0), (DO_AX, (7, 0)), (DO_AZ1, (1, 0)), (DO_SMALL, 0),
-    (DO_STAGE, (9, 0)), (DO_AY, (6, 0)), (DO_ACORE, (8, 0)), (DO_AZ2, (2, 1)), (DO_AZ3, (2, 1)),
-    (DO_AX, (7, 1)), (DO_AZ2, (3, 0)), (DO_AZ1, (0, 0)), (DO_ACORE, (9, 0)), (DO_AX, (5, 0)),
-    (DO_AZ2, (1, 0)), (DO_AZ3, (1, 0)), (DO_AZ1, (0, 1)), (DO_AX, (6, 0)), (DO_AY, (6, 1)),
-    (DO_AZ2, (2, 0)), (DO_AY, (8, 0)), (DO_AZ3, (2, 0)), (DO_AZ3, (3, 0)), (DO_AZ1, (7, 1)),
-    (DO_AZ2, (4, 0)), (DO_AX, (9, 0)), (DO_AZ2, (0, 1)), (DO_AZ1, (7, 0)), (DO_AZ2, (0, 0)),
-    (DO_AZ3, (0, 1)), (DO_AX, (6, 1)), (DO_AZ3, (4, 0)), (DO_AZ2, (7, 1)), (DO_AZ3, (7, 1)),
-    (DO_AZ1, (5, 0)), (DO_AZ1, (6, 0)), (DO_AZ2, (7, 0)), (DO_AZ3, (7, 0)), (DO_AZ1, (9, 0)),
-    (DO_AX, (8, 0)), (DO_FIN, (2, 0)), (DO_AZ3, (0, 0)), (DO_AZ1, (6, 1)), (DO_AZ2, (6, 0)),
-    (DO_AX, (3, 0)), (DO_AZ2, (5, 0)), (DO_AZ3, (6, 0)), (DO_AZ3, (5, 0)), (DO_FIN, (7, 0)),
-    (DO_AZ2, (9, 0)), (DO_FIN, (0, 0)), (DO_AZ1, (8, 0)), (DO_AZ2, (6, 1)), (DO_AZ3, (6, 1)),
-    (DO_AZ2, (8, 0)), (DO_FIN, (6, 0)), (DO_AZ3, (9, 0)), (DO_AZ3, (8, 0)), (DO_FIN, (0, 1)),
-    (DO_FIN, (4, 0)), (DO_FIN, (2, 1)), (DO_FIN, (1, 0)), (DO_FIN, (6, 1)), (DO_FIN, (7, 1)),
-    (DO_FIN, (5, 0)), (DO_FIN, (3, 0)), (DO_FIN, (9, 0)), (DO_FIN, (8, 0)), (DO_END, 0),
+    (DO_FIRST, 0), (DO_FIRST, 5), (DO_FIRST, 1), (DO_FIRST, 2), (DO_FIRST, 3), (DO_NEAR, 0),
+    (DO_FIRST, 4), (DO_NEAR, 1), (DO_FIRST, 6), (DO_FIRST, 7), (DO_PLACES, 0), (DO_NEAR, 2),
+    (DO_NEAR, 3), (DO_FIRST, 8), (DO_NEAR, 4), (DO_NEAR, 6), (DO_FAR, 1), (DO_FAR, 2), (DO_FAR, 3),
+    (DO_FAR, 4), (DO_FAR, 0), (DO_FIRST, 9), (DO_FIRST, 10), (DO_NEAR, 8), (DO_SIDE, 1),
+    (DO_NEAR, 7), (DO_FIRST, 11), (DO_FIRST, 12), (DO_SIDE, 2), (DO_FAR, 8), (DO_SIDE, 3),
+    (DO_SIDE, 0), (DO_NEAR, 11), (DO_FAR, 6), (DO_UNPACK, 0), (DO_CROSS, 1), (DO_NEAR, 12),
+    (DO_SIDE, 4), (DO_NEAR, 5), (DO_CROSS, 2), (DO_NEAR, 10), (DO_NORM1, 0), (DO_PROJECT, 2),
+    (DO_PROJECT, 1), (DO_SIDE, 8), (DO_FAR, 11), (DO_FAR, 7), (DO_FAR, 12), (DO_NEAR, 9),
+    (DO_CONV, 0), (DO_CONV, 1), (DO_SIDE, 6), (DO_FAR, 10), (DO_FAR, 5), (DO_CROSS, 3),
+    (DO_CONV, 2), (DO_CONV, 3), (DO_FAR, 9), (DO_SIDE, 11), (DO_PROJECT, 0), (DO_SIDE, 12),
+    (DO_CROSS, 4), (DO_SIDE, 7), (DO_CROSS, 8), (DO_SIDE, 5), (DO_SIDE, 10), (DO_CROSS, 6),
+    (DO_MIX, 0), (DO_EXPAND, 0), (DO_CROSS, 7), (DO_SIDE, 9), (DO_EXPAND, 3), (DO_EXPAND, 2),
+    (DO_FEED, 2), (DO_GEXP, 2), (DO_STAGE, (2, 1)), (DO_EXPAND, 1), (DO_FEED, 1), (DO_GEXP, 1),
+    (DO_STAGE, (4, 0)), (DO_ACORE, (2, 1)), (DO_FEED, 0), (DO_GEXP, 0), (DO_STAGE, (2, 0)),
+    (DO_ACORE, (4, 0)), (DO_FEED, 3), (DO_DRAIN, 0), (DO_GCON, 0), (DO_STAGE, (0, 0)),
+    (DO_ACORE, (2, 0)), (DO_STAGE, (1, 0)), (DO_AX, (2, 1)), (DO_GEXP, 3), (DO_STAGE, (3, 0)),
+    (DO_STAGE, (0, 1)), (DO_ACORE, (0, 0)), (DO_NORM2B, 0), (DO_GOUT, 0), (DO_ACORE, (3, 0)),
+    (DO_ACORE, (1, 0)), (DO_STAGE, (5, 0)), (DO_AY, (4, 0)), (DO_BACKG, 0), (DO_CONVB, 0),
+    (DO_ACORE, (5, 0)), (DO_AX, (2, 0)), (DO_CONVB, 1), (DO_CONVB, 2), (DO_AY, (0, 0)),
+    (DO_AX, (1, 0)), (DO_AZ1, (2, 1)), (DO_ACORE, (0, 1)), (DO_AY, (5, 0)), (DO_CONVB, 3),
+    (DO_GIN, 1), (DO_STAGE, (7, 0)), (DO_AZ1, (2, 0)), (DO_AX, (4, 0)), (DO_GIN, 2),
+    (DO_STAGE, (7, 1)), (DO_STAGE, (8, 0)), (DO_ACORE, (7, 0)), (DO_GIN, 0), (DO_STAGE, (6, 1)),
+    (DO_AZ1, (3, 0)), (DO_ACORE, (7, 1)), (DO_ACORE, (8, 0)), (DO_AX, (0, 0)), (DO_BFIRST, 0),
+    (DO_AZ2, (2, 1)), (DO_STAGE, (6, 0)), (DO_AZ2, (2, 0)), (DO_AY, (0, 1)), (DO_AX, (5, 0)),
+    (DO_ACORE, (6, 1)), (DO_AZ1, (1, 0)), (DO_ACORE, (6, 0)), (DO_AX, (7, 0)), (DO_NORM1B, 0),
+    (DO_SMALL, 0), (DO_STAGE, (9, 0)), (DO_ACORE, (9, 0)), (DO_AZ2, (3, 0)), (DO_AX, (7, 1)),
+    (DO_AZ1, (0, 0)), (DO_AZ3, (2, 0)), (DO_AX, (0, 1)), (DO_AY, (8, 0)), (DO_AZ1, (5, 0)),
+    (DO_AY, (6, 1)), (DO_AZ1, (4, 0)), (DO_AZ2, (1, 0)), (DO_AZ3, (1, 0)), (DO_AX, (9, 0)),
+    (DO_AY, (6, 0)), (DO_AZ3, (3, 0)), (DO_AZ1, (7, 1)), (DO_AZ3, (2, 1)), (DO_AZ1, (7, 0)),
+    (DO_AX, (8, 0)), (DO_AZ2, (0, 0)), (DO_AZ2, (5, 0)), (DO_AZ3, (0, 0)), (DO_AZ3, (5, 0)),
+    (DO_AZ1, (0, 1)), (DO_AX, (6, 1)), (DO_AZ2, (7, 1)), (DO_FIN, (1, 0)), (DO_AX, (6, 0)),
+    (DO_AZ3, (7, 1)), (DO_AZ1, (9, 0)), (DO_AZ2, (7, 0)), (DO_AZ3, (7, 0)), (DO_FIN, (2, 1)),
+    (DO_AX, (3, 0)), (DO_AZ2, (0, 1)), (DO_AZ1, (8, 0)), (DO_AZ1, (6, 1)), (DO_FIN, (7, 1)),
+    (DO_FIN, (0, 0)), (DO_AZ3, (0, 1)), (DO_AZ2, (9, 0)), (DO_AZ3, (9, 0)), (DO_AZ1, (6, 0)),
+    (DO_AZ2, (8, 0)), (DO_AZ3, (8, 0)), (DO_FIN, (7, 0)), (DO_AZ2, (4, 0)), (DO_AZ3, (4, 0)),
+    (DO_AZ2, (6, 1)), (DO_FIN, (0, 1)), (DO_AZ3, (6, 1)), (DO_AZ2, (6, 0)), (DO_AZ3, (6, 0)),
+    (DO_FIN, (2, 0)), (DO_FIN, (4, 0)), (DO_FIN, (9, 0)), (DO_FIN, (6, 1)), (DO_FIN, (3, 0)),
+    (DO_FIN, (5, 0)), (DO_FIN, (8, 0)), (DO_FIN, (6, 0)), (DO_END, 0),
 )
-SMALL_ROWS = 80
+SMALL_ROWS = 64
 NORM_ROWS = 128
 INNER_OUT = 8
 
@@ -238,7 +240,7 @@
         del refs[:number]
         return taken
 
-    tokens, segs, cot = take(3)
+    tokens_in, segs, cot_in = take(3)
     (
         r_first_gain, r_first_shift, r_in_bias, r_short_w, r_short_b, r_inner_w, r_inner_b,
         r_scale, r_middle_w, r_middle_b, r_filter_w, r_direct, r_out_bias, r_second_gain,
@@ -246,7 +248,9 @@
     ) = take(17)
     own = take(4)
     features, decay = take(2)
-    result, delta = take(2)
+    result_out, delta_out = take(2)
+    sums_out = take(5)
+    tokens, cot, result, delta = take(4)
     sums = take(5)
     full = take(5)
     g_in, g_out, g_small, own_small, pack = take(5)
@@ -263,7 +267,7 @@
         members = take(7 if kind == SPLIT else 6)
         names = ("core", "x", "z1", "z2", "z3", "last") + (("y",) if kind == SPLIT else ())
         groups.append(dict(zip(names, members)))
-    ag_recv, ag_cross, ag_core, ag_send, own_sem, rs_recv, rs_y, rs_send, rs_end = take(9)
+    ag_recv, ag_cross, ag_core, ag_send, own_sem, rs_recv, rs_y, rs_send, rs_end, out_sem = take(10)
     assert not refs
 
     own = list(own) + [own_small]
@@ -284,6 +288,12 @@
     own_pair = pl.ds(pair * 2, 2)
     other_pair = pl.ds((1 - pair) * 2, 2)
 
+    loads = [
+        pltpu.make_async_copy(own[m].at[c], full[m].at[z, x, c], own_sem.at[m]) for m in range(4)
+    ] + [
+        pltpu.make_async_copy(tokens_in, tokens, own_sem.at[5]),
+        pltpu.make_async_copy(cot_in, cot, own_sem.at[6]),
+    ]
     barrier = pltpu.get_barrier_semaphore()
     for target in (to_near, to_x, to_y, to_c):
         pl.semaphore_signal(barrier, inc=1, device_id=target, device_id_type=MESH_ID)
@@ -291,6 +301,9 @@
     @pl.when(inner)
     def _():
         pl.semaphore_signal(barrier, inc=1, device_id=to_mirror, device_id_type=MESH_ID)
+
+    for load in loads:
+        load.start()
 
     def remote(source, landing, send, recv, device):
         return pltpu.make_async_remote_copy(
@@ -315,13 +328,11 @@
         pack[top + 5 : top + 6, :] = exp_bias[:, block * 128 : block * 128 + 128]
     for row, member in enumerate((r_inner_b, r_scale, r_middle_b)):
         pack[32 + row : 33 + row, 0:8] = member[...].astype(FULL).reshape(1, 8)
-    pack[40:80, :] = jnp.concatenate(
-        [widen(r_inner_w[...].astype(FULL), 128), jnp.zeros((120, 128), FULL)], axis=0
-    ).T[0:40]
-    pack[80:88, 0:64] = r_middle_w[...].astype(FULL)
-    pack[88:152, 0:96] = r_filter_w[...].astype(FULL)
-    own_small[0] = pack[0:80, :].astype(LOW)
-    own_small[1] = pack[80:160, :].astype(LOW)
+    pack[40:48, 0:64] = r_middle_w[...].astype(FULL)
+    pack[48:56, 0:33] = r_inner_w[...].astype(FULL)
+    pack[64:128, 0:96] = r_filter_w[...].astype(FULL)
+    own_small[0] = pack[0:64, :].astype(LOW)
+    own_small[1] = pack[64:128, :].astype(LOW)
 
     acc96[...] = jnp.zeros_like(acc96)
     acc288[...] = jnp.zeros_like(acc288)
@@ -348,8 +359,9 @@
     def whole(chunk):
         return pl.ds(chunk[1], chunk[2])
 
-    for matrix in range(5):
-        pltpu.make_async_copy(own[matrix].at[c], full[matrix].at[z, x, c], own_sem.at[matrix]).start()
+    small_load = pltpu.make_async_copy(own_small.at[c], full[4].at[z, x, c], own_sem.at[4])
+    small_load.start()
+    loads.append(small_load)
 
     send_groups = []
     for chunk in chunks:
@@ -486,8 +498,14 @@
                 send = ag_send.at[S_CORE, group_of(chunk)]
                 remote(piece, piece, send, ag_core.at[index], to_c).wait_recv()
 
-    for matrix in range(5):
-        pltpu.make_async_copy(own[matrix].at[c], full[matrix].at[z, x, c], own_sem.at[matrix]).wait()
+    loaded = []
+
+    def ready():
+        if not loaded:
+            loaded.append(True)
+            for load in loads:
+                load.wait()
+
 
     def row_blocks(size, action):
         def body(step, carry):
@@ -512,7 +530,7 @@
         total96 = jnp.zeros((8, 768), FULL)
         total288 = jnp.zeros((8, 2304), FULL)
         total8 = jnp.zeros((8, 128), FULL)
-        inner_total = jnp.zeros((40, 128), FULL)
+        inner_rows = []
         fil_w[...] = jnp.zeros_like(fil_w)
         mid_w[...] = jnp.zeros_like(mid_w)
         for s in range(8):
@@ -523,14 +541,15 @@
             vexp[:, s * 384 : s * 384 + 384] = wide[5:6]
             total288 = total288 + turn(widen(wide, 2304), 288 * s, 1)
             total8 = total8 + turn(top[32:40], 8 * s, 1)
-            inner_total = inner_total + turn(top[40:80], 8 * s, 1)
-            mid_w[8 * s : 8 * s + 8, :] = low[0:8]
-            fil_w[0:64, :] += turn(widen(low[8:72], 768), 96 * s, 1)
+            inner_rows.append(top[48:56])
+            mid_w[8 * s : 8 * s + 8, :] = top[40:48]
+            fil_w[0:64, :] += turn(widen(low, 768), 96 * s, 1)
         v96[...] = total96
         v288[...] = total288
         v8[...] = total8
         scale = total8[1:2]
-        inner1 = exact(features[...], inner_total, (1, 0)) + total8[0:1]
+        inner_all = jnp.concatenate(inner_rows + [jnp.zeros((64, 128), FULL)], axis=0)
+        inner1 = exact(features[...], inner_all, (1, 1)) + total8[0:1]
         s_inner1[...] = inner1
         s_first[...] = jnp.sin(scale * inner1)
         s_cos1[...] = jnp.cos(scale * inner1)
@@ -696,7 +715,8 @@
         if REDUCE_GROUPS[key[0]][3] == SPLIT:
             split_position[key] = len(split_position)
     R_CORE, R_X, R_Z1, R_Z2, R_Z3, R_LAST = range(6)
-    W_CORE, W_Y, W_X, W_Z1, W_Z2, W_Z3, W_LAST, W_END = range(8)
+    W_CORE, W_Y, W_X, W_Z1, W_Z3, W_LAST, W_END = range(7)
+    W_Z2 = W_Z1
 
     def info(key):
         g, i = key
@@ -848,13 +868,15 @@
         if kind == SPLIT:
             for which, slot in ((y, 0), (1 - y, 1)):
                 columns = pl.ds(pl.multiple_of(column + which * (width // 2), 128), width // 2)
-                sums[m][c, :, columns] = buf["last"][i, slot].astype(FULL)
+                sums[m][:, columns] = buf["last"][i, slot].astype(FULL)
         else:
-            sums[m][c, :, pl.ds(column, width)] = buf["last"][i, 0].astype(FULL) + buf["last"][
+            sums[m][:, pl.ds(column, width)] = buf["last"][i, 0].astype(FULL) + buf["last"][
                 i, 1
             ].astype(FULL)
-        piece = sums[m].at[c, :, pl.ds(column, width)]
-        remote(piece, piece, rs_send.at[W_END, g], rs_end.at[g], to_c).start()
+        piece = sums[m].at[:, pl.ds(column, width)]
+        place = sums_out[m].at[c, :, pl.ds(column, width)]
+        remote(piece, place, rs_send.at[W_END, g], rs_end.at[g], to_c).start()
+        pltpu.make_async_copy(piece, place, out_sem.at[g]).start()
 
     def grad_contract():
         def body(s, carry):
@@ -958,7 +980,7 @@
         d_mid = exact(s_first[...], b2s, (0, 0))
         b1 = exact(b2s, mid_w[...], (1, 1)) * s_cos1[...]
         b1s = b1 * scale
-        d_inner = exact(features[...], b1s, (0, 0))
+        d_inner = exact(b1s, features[...], (0, 0))
         d_scale = jnp.sum(b2 * s_inner2[...] + b1 * s_inner1[...], axis=0, keepdims=True)
         rows8 = jnp.concatenate(
             [
@@ -980,7 +1002,6 @@
         lane = lax.broadcasted_iota(jnp.int32, (8, 128), 1)
         row = lax.broadcasted_iota(jnp.int32, (8, 128), 0)
         wide_lane = lax.broadcasted_iota(jnp.int32, (64, 128), 1)
-        long_lane = lax.broadcasted_iota(jnp.int32, (40, 128), 1)
         for s in range(8):
             a, b = s // 2, s % 2
             g_small[a, b, 0, 0:8, :] = jnp.where(lane < 96, turn(rows96, -96 * s, 1)[:, :128], 0.0)
@@ -993,12 +1014,12 @@
                 value = jnp.where(row == 5, jnp.broadcast_to(bias, (8, 128)), value)
                 g_small[a, b, 0, 8 + block * 8 : 16 + block * 8, :] = value
             g_small[a, b, 0, 32:40, :] = jnp.where(lane < 8, turn(rows8, -8 * s, 1), 0.0)
-            g_small[a, b, 0, 40:80, :] = jnp.where(long_lane < 8, turn(d_inner, -8 * s, 1), 0.0)
-            g_small[a, b, 1, 0:8, :] = d_mid[8 * s : 8 * s + 8]
-            g_small[a, b, 1, 8:72, :] = jnp.where(
+            g_small[a, b, 0, 40:48, :] = d_mid[8 * s : 8 * s + 8]
+            g_small[a, b, 0, 48:56, :] = d_inner[8 * s : 8 * s + 8]
+            g_small[a, b, 0, 56:64, :] = jnp.zeros((8, 128), FULL)
+            g_small[a, b, 1] = jnp.where(
                 wide_lane < 96, turn(d_fil[0:64], -96 * s, 1)[:, :128], 0.0
             )
-            g_small[a, b, 1, 72:80, :] = jnp.zeros((8, 128), FULL)
 
     def back_gate():
         back_g[...] = dot_nt(back_m[...], matrix_of(1, pl.ds(0, 768), 768))
@@ -1031,11 +1052,26 @@
         settled(2, 0, 768)
         feed(k)
 
+    outgoing = [
+        pltpu.make_async_copy(result, result_out, own_sem.at[7]),
+        pltpu.make_async_copy(delta, delta_out, own_sem.at[8]),
+    ]
+
+    def second_back(k):
+        row_blocks(NORM_ROWS, norm_second_back)
+        outgoing[0].start()
+
+    def first_back(k):
+        row_blocks(NORM_ROWS, norm_first_back)
+        outgoing[1].start()
+
     def expand_back(k):
         drain(3, k * 768, k * 768 + 768)
         grad_expand(k)
 
     def end(k):
+        for copy in outgoing:
+            copy.wait()
         for m in range(5):
             drain(m, 0, full[m].shape[4])
 
@@ -1052,23 +1088,27 @@
         DO_DRAIN: lambda k: drain(2, 0, 768),
         DO_GCON: lambda k: grad_contract(),
         DO_GEXP: expand_back,
-        DO_NORM2B: lambda k: row_blocks(NORM_ROWS, norm_second_back),
+        DO_NORM2B: second_back,
         DO_BACKG: lambda k: back_gate(),
         DO_GOUT: lambda k: grad_rows(gated, back_m[...], g_out, pl.ds(0, 768), 768),
         DO_CONVB: lambda k: convolve_back(3 * k, 3 * k + 3),
         DO_GIN: lambda k: grad_rows(normed1, bp[k], g_in, pl.ds(k * 768, 768), 768),
         DO_BFIRST: lambda k: back_first(),
-        DO_NORM1B: lambda k: row_blocks(NORM_ROWS, norm_first_back),
+        DO_NORM1B: first_back,
         DO_SMALL: lambda k: small_grads(),
         DO_STAGE: stage, DO_ACORE: add_core, DO_AY: add_y, DO_AX: add_x, DO_AZ1: add_z1,
         DO_AZ2: add_z2, DO_AZ3: add_z3, DO_FIN: finish, DO_END: end,
     }
     for name, which in SCHEDULE:
+        if name != DO_FIRST:
+            ready()
         actions[name](which)
 
     for g, (matrix, columns, width, kind) in enumerate(REDUCE_GROUPS):
-        piece = sums[matrix].at[1 - c, :, pl.ds(0, width * len(columns))]
-        remote(piece, piece, rs_send.at[W_END, g], rs_end.at[g], to_c).wait_recv()
+        held = sums[matrix].at[:, pl.ds(0, width * len(columns))]
+        place = sums_out[matrix].at[1 - c, :, pl.ds(0, width * len(columns))]
+        remote(held, place, rs_send.at[W_END, g], rs_end.at[g], to_c).wait_recv()
+        pltpu.make_async_copy(held, place, out_sem.at[g]).wait()
     for g, (matrix, columns, width, kind) in enumerate(REDUCE_GROUPS):
         buf = groups[g]
 
@@ -1081,15 +1121,9 @@
         leave(W_X, buf["x"])
         leave(W_Z3, buf["z3"])
         leave(W_LAST, buf["last"].at[:, 0])
-        leave(W_END, sums[matrix].at[1 - c, :, pl.ds(0, width * len(columns))])
-
-        @pl.when(inner)
-        def _(leave=leave, buf=buf):
-            leave(W_Z2, buf["z2"])
-
-        @pl.when(jnp.logical_not(inner))
-        def _(leave=leave, buf=buf):
-            leave(W_Z1, buf["z1"])
+        leave(W_END, sums[matrix].at[:, pl.ds(0, width * len(columns))])
+
+        leave(W_Z1, buf["z1"])
 
 
 def unpack_kernel(result, delta, s_in, s_out, s_con, s_exp, s_small, *outs):
@@ -1115,10 +1149,9 @@
     o_exp_bias[...] = wide[5:6].reshape(384)
     for row, target in enumerate((o_inner_b, o_scale, o_middle_b)):
         target[...] = s_small[0, 32 + row : 33 + row, 0:8].reshape(8)
-    tile = jnp.concatenate([s_small[0, 40:80, :], jnp.zeros((88, 128), FULL)], axis=0).T
-    o_inner_w[...] = tile[0:8, 0:33]
-    o_middle_w[...] = s_small[1, 0:8, 0:64]
-    o_filter_w[...] = s_small[1, 8:72, 0:96]
+    o_inner_w[...] = s_small[0, 48:56, 0:33]
+    o_middle_w[...] = s_small[0, 40:48, 0:64]
+    o_filter_w[...] = s_small[1, :, 0:96]
 
 
 def filter_constants(length, width):
@@ -1126,7 +1159,7 @@
     scales = 0.0001 + np.arange(16, dtype=np.float64) * ((15.0 - 0.0001) / 15.0)
     phases = (2.0 * math.pi * places / length)[:, None] * scales[None, :]
     ramp = places / (length - 1)
-    table = np.zeros((LAGS, 40), np.float32)
+    table = np.zeros((LAGS, 128), np.float32)
     table[:, 0] = ramp
     table[:, 1:17] = np.cos(phases)
     table[:, 17:33] = -np.sin(phases)
@@ -1169,8 +1202,11 @@
     ] + [jax.ShapeDtypeStruct((2,) + s, FULL) for s in shapes]
     count = len(GATHER_CHUNKS)
     crossing = sum(1 for chunk in GATHER_CHUNKS if chunk[3] == SPLIT)
+    leaving = len({chunk[:1] if chunk[0] != 3 else chunk[:2] for chunk in GATHER_CHUNKS})
     vm = pltpu.VMEM
-    scratch = [vm((4, 2, 2) + s, LOW) for s in shapes]
+    scratch = [vm((rows, width), kind) for kind in (LOW, LOW, LOW, FULL)]
+    scratch += [vm(s, FULL) for s in shapes]
+    scratch += [vm((4, 2, 2) + s, LOW) for s in shapes]
     scratch += [
         vm((4, 2, 2) + shapes[0], LOW), vm((4, 2, 2) + shapes[1], LOW),
         vm((4, 2, 2) + shapes[4], FULL), vm((2, SMALL_ROWS, 128), LOW),
@@ -1205,15 +1241,17 @@
     splits = sum(len(g[1]) for g in REDUCE_GROUPS if g[3] == SPLIT)
     dma = pltpu.SemaphoreType.DMA
     scratch += [
-        dma((4, count)), dma((3, crossing)), dma((count,)), dma((6, 8)), dma((5,)),
-        dma((6, total)), dma((splits,)), dma((8, len(REDUCE_GROUPS))), dma((len(REDUCE_GROUPS),)),
+        dma((4, count)), dma((3, crossing)), dma((count,)), dma((6, leaving)), dma((9,)),
+        dma((6, total)), dma((splits,)), dma((7, len(REDUCE_GROUPS))), dma((len(REDUCE_GROUPS),)),
+        dma((len(REDUCE_GROUPS),)),
     ]
     in_vmem = pl.BlockSpec(memory_space=pltpu.VMEM)
+    anywhere = pl.BlockSpec(memory_space=pl.ANY)
     parts = pl.pallas_call(
         block_kernel,
         out_shape=outs,
-        in_specs=[in_vmem] * len(inputs),
-        out_specs=[in_vmem] * len(outs),
+        in_specs=[anywhere, in_vmem, anywhere] + [in_vmem] * 17 + [anywhere] * 4 + [in_vmem] * 2,
+        out_specs=[anywhere] * len(outs),
         scratch_shapes=scratch,
         compiler_params=pltpu.CompilerParams(
             collective_id=0, has_side_effects=True, vmem_limit_bytes=67043328

time: 150 us -> 143 us (0.953)
  Pallas kernels: 149 us -> 142 us
    pallas_call x1, Pallas kernels: 145 us -> 137 us  [block_device(): pl.pallas_call(block_kernel, out_shape=outs, in_specs=[anywhere, in_vmem,...]
where the time goes in v4:
time: 143 us
  Pallas kernels  142 us (99%)
    pallas_call x1, Pallas kernels, block_device(): pl.pallas_call(block_kernel, out_shape=outs, in_specs=[anywhere, in_vmem,...  137 us
    pallas_call x1, Pallas kernels, block_device(): pl.pallas_call(unpack_kernel, out_shape=final, in_specs=[in_vmem] * 7, ou...  4.67 us

profile of v4, /device:TPU:0, one launch (start us, length us, event | category | flops | bytes accessed | tf_op | source)
XLA Modules:
  0.0 142.7 jit_solution(15142984715999015987)
XLA Ops:
  0.7 137.1 %shard_map.425 = (bf16[256,768]{1,0:T(8,128)(2,1)}, f32[256,768]{1,0:T(8,128)}, f32[2,48,2304]{2,1,0:T(8,128)}, f32[2,48,768]{2,1,0:T(8,128)}, f32[2,192,768]{2,...) custom-call(bf16[256,768]{1,0:T(8,128)(2,1)} %bitcast.18, s32[2,128]{1,0:T(2,128)} %bitcast.22, ...), custom_call_target="tpu_custom_call" | custom-call | tf_op jit(solution)/shard_map/pallas_call | solution.py:1250
  137.8 4.7 %shard_map.426 = (bf16[256,768]{1,0:T(8,128)(2,1)}, f32[256,768]{1,0:T(8,128)}, f32[96]{0:T(128)}, f32[96]{0:T(128)}, f32[96,2304]{1,0:T(8,128)}, /*index=5*/f32...) custom-call(bf16[256,768]{1,0:T(8,128)(2,1)} %get-tuple-element.53.r, ...), custom_call_target="tpu_custom_call" | custom-call | tf_op jit(solution)/shard_map/pallas_call | solution.py:1269

commit v5 on v4

--- a/solution.py
+++ b/solution.py
@@ -108,85 +108,86 @@
 LAGS = 64
 LOW = jnp.bfloat16
 FULL = jnp.float32
-WHOLE, SPLIT, LINE = range(3)
+WHOLE, SPLIT, LINE, WHOLE_FAR, SPLIT_FAR = range(5)
+SPLITS = (SPLIT, SPLIT_FAR)
+FARS = (WHOLE_FAR, SPLIT_FAR)
 GATHER_CHUNKS = (
     (4, 0, 128, WHOLE),
     (0, 768, 768, SPLIT),
     (0, 1536, 768, SPLIT),
     (0, 0, 768, SPLIT),
     (1, 0, 768, SPLIT),
-    (3, 0, 768, LINE),
+    (3, 0, 768, SPLIT),
+    (3, 768, 768, WHOLE),
+    (3, 1536, 768, SPLIT),
+    (3, 2304, 768, WHOLE),
     (2, 0, 256, SPLIT),
-    (2, 256, 256, SPLIT),
-    (2, 512, 256, SPLIT),
-    (3, 768, 768, WHOLE),
-    (3, 1536, 768, WHOLE),
-    (3, 2304, 384, WHOLE),
-    (3, 2688, 384, WHOLE),
+    (2, 256, 256, LINE),
+    (2, 512, 256, WHOLE),
 )
 REDUCE_GROUPS = (
-    (2, (0, 256), 256, SPLIT),
+    (2, (0,), 256, LINE),
+    (2, (256,), 256, SPLIT),
     (2, (512,), 256, WHOLE),
-    (3, (0, 1536), 768, WHOLE),
-    (3, (2304,), 768, LINE),
-    (3, (768,), 768, SPLIT),
+    (3, (0, 1536), 768, SPLIT),
+    (3, (768, 2304), 768, WHOLE),
     (1, (0,), 768, SPLIT),
-    (0, (0, 512), 512, SPLIT),
-    (0, (1024, 1408), 384, WHOLE),
-    (0, (1792,), 512, SPLIT),
-    (4, (0,), 128, WHOLE),
+    (0, (0, 768, 1536), 512, SPLIT_FAR),
+    (0, (512, 1280, 2048), 256, WHOLE),
+    (4, (0,), 128, WHOLE_FAR),
 )
 REDUCE_ORDER = (
-    (2, 0), (4, 0), (2, 1), (3, 0), (0, 0), (0, 1), (1, 0), (5, 0), (6, 0), (6, 1), (7, 0), (7, 1), (8, 0), (9, 0),
+    (0, 0), (1, 0), (2, 0), (3, 0), (4, 0), (3, 1), (4, 1), (5, 0), (6, 0), (7, 0), (6, 1), (7, 1), (6, 2), (7, 2), (8, 0),
 )
 (
     DO_FIRST, DO_NEAR, DO_FAR, DO_SIDE, DO_CROSS, DO_PLACES, DO_UNPACK, DO_NORM1,
-    DO_PROJECT, DO_CONV, DO_MIX, DO_EXPAND, DO_FEED, DO_DRAIN, DO_GCON, DO_GEXP,
-    DO_NORM2B, DO_BACKG, DO_GOUT, DO_CONVB, DO_GIN, DO_BFIRST, DO_NORM1B, DO_SMALL,
-    DO_STAGE, DO_ACORE, DO_AY, DO_AX, DO_AZ1, DO_AZ2, DO_AZ3, DO_FIN,
-    DO_END,
-) = range(33)
+    DO_PROJECT, DO_CONV, DO_MIX, DO_EXPAND, DO_BEND, DO_FEED, DO_DRAIN, DO_GCON,
+    DO_GEXP, DO_NORM2B, DO_BACKG, DO_GOUT, DO_CONVB, DO_GIN, DO_BFIRST, DO_NORM1B,
+    DO_SMALL, DO_STAGE, DO_ACORE, DO_AY, DO_AX, DO_AZ1, DO_AZ2, DO_AZ3,
+    DO_FIN, DO_END,
+) = range(34)
 SCHEDULE = (
-    (DO_FIRST, 0), (DO_FIRST, 5), (DO_FIRST, 1), (DO_FIRST, 2), (DO_FIRST, 3), (DO_NEAR, 0),
-    (DO_FIRST, 4), (DO_NEAR, 1), (DO_FIRST, 6), (DO_FIRST, 7), (DO_PLACES, 0), (DO_NEAR, 2),
-    (DO_NEAR, 3), (DO_FIRST, 8), (DO_NEAR, 4), (DO_NEAR, 6), (DO_FAR, 1), (DO_FAR, 2), (DO_FAR, 3),
-    (DO_FAR, 4), (DO_FAR, 0), (DO_FIRST, 9), (DO_FIRST, 10), (DO_NEAR, 8), (DO_SIDE, 1),
-    (DO_NEAR, 7), (DO_FIRST, 11), (DO_FIRST, 12), (DO_SIDE, 2), (DO_FAR, 8), (DO_SIDE, 3),
-    (DO_SIDE, 0), (DO_NEAR, 11), (DO_FAR, 6), (DO_UNPACK, 0), (DO_CROSS, 1), (DO_NEAR, 12),
-    (DO_SIDE, 4), (DO_NEAR, 5), (DO_CROSS, 2), (DO_NEAR, 10), (DO_NORM1, 0), (DO_PROJECT, 2),
-    (DO_PROJECT, 1), (DO_SIDE, 8), (DO_FAR, 11), (DO_FAR, 7), (DO_FAR, 12), (DO_NEAR, 9),
-    (DO_CONV, 0), (DO_CONV, 1), (DO_SIDE, 6), (DO_FAR, 10), (DO_FAR, 5), (DO_CROSS, 3),
-    (DO_CONV, 2), (DO_CONV, 3), (DO_FAR, 9), (DO_SIDE, 11), (DO_PROJECT, 0), (DO_SIDE, 12),
-    (DO_CROSS, 4), (DO_SIDE, 7), (DO_CROSS, 8), (DO_SIDE, 5), (DO_SIDE, 10), (DO_CROSS, 6),
-    (DO_MIX, 0), (DO_EXPAND, 0), (DO_CROSS, 7), (DO_SIDE, 9), (DO_EXPAND, 3), (DO_EXPAND, 2),
-    (DO_FEED, 2), (DO_GEXP, 2), (DO_STAGE, (2, 1)), (DO_EXPAND, 1), (DO_FEED, 1), (DO_GEXP, 1),
-    (DO_STAGE, (4, 0)), (DO_ACORE, (2, 1)), (DO_FEED, 0), (DO_GEXP, 0), (DO_STAGE, (2, 0)),
-    (DO_ACORE, (4, 0)), (DO_FEED, 3), (DO_DRAIN, 0), (DO_GCON, 0), (DO_STAGE, (0, 0)),
-    (DO_ACORE, (2, 0)), (DO_STAGE, (1, 0)), (DO_AX, (2, 1)), (DO_GEXP, 3), (DO_STAGE, (3, 0)),
-    (DO_STAGE, (0, 1)), (DO_ACORE, (0, 0)), (DO_NORM2B, 0), (DO_GOUT, 0), (DO_ACORE, (3, 0)),
-    (DO_ACORE, (1, 0)), (DO_STAGE, (5, 0)), (DO_AY, (4, 0)), (DO_BACKG, 0), (DO_CONVB, 0),
-    (DO_ACORE, (5, 0)), (DO_AX, (2, 0)), (DO_CONVB, 1), (DO_CONVB, 2), (DO_AY, (0, 0)),
-    (DO_AX, (1, 0)), (DO_AZ1, (2, 1)), (DO_ACORE, (0, 1)), (DO_AY, (5, 0)), (DO_CONVB, 3),
-    (DO_GIN, 1), (DO_STAGE, (7, 0)), (DO_AZ1, (2, 0)), (DO_AX, (4, 0)), (DO_GIN, 2),
-    (DO_STAGE, (7, 1)), (DO_STAGE, (8, 0)), (DO_ACORE, (7, 0)), (DO_GIN, 0), (DO_STAGE, (6, 1)),
-    (DO_AZ1, (3, 0)), (DO_ACORE, (7, 1)), (DO_ACORE, (8, 0)), (DO_AX, (0, 0)), (DO_BFIRST, 0),
-    (DO_AZ2, (2, 1)), (DO_STAGE, (6, 0)), (DO_AZ2, (2, 0)), (DO_AY, (0, 1)), (DO_AX, (5, 0)),
-    (DO_ACORE, (6, 1)), (DO_AZ1, (1, 0)), (DO_ACORE, (6, 0)), (DO_AX, (7, 0)), (DO_NORM1B, 0),
-    (DO_SMALL, 0), (DO_STAGE, (9, 0)), (DO_ACORE, (9, 0)), (DO_AZ2, (3, 0)), (DO_AX, (7, 1)),
-    (DO_AZ1, (0, 0)), (DO_AZ3, (2, 0)), (DO_AX, (0, 1)), (DO_AY, (8, 0)), (DO_AZ1, (5, 0)),
-    (DO_AY, (6, 1)), (DO_AZ1, (4, 0)), (DO_AZ2, (1, 0)), (DO_AZ3, (1, 0)), (DO_AX, (9, 0)),
-    (DO_AY, (6, 0)), (DO_AZ3, (3, 0)), (DO_AZ1, (7, 1)), (DO_AZ3, (2, 1)), (DO_AZ1, (7, 0)),
-    (DO_AX, (8, 0)), (DO_AZ2, (0, 0)), (DO_AZ2, (5, 0)), (DO_AZ3, (0, 0)), (DO_AZ3, (5, 0)),
-    (DO_AZ1, (0, 1)), (DO_AX, (6, 1)), (DO_AZ2, (7, 1)), (DO_FIN, (1, 0)), (DO_AX, (6, 0)),
-    (DO_AZ3, (7, 1)), (DO_AZ1, (9, 0)), (DO_AZ2, (7, 0)), (DO_AZ3, (7, 0)), (DO_FIN, (2, 1)),
-    (DO_AX, (3, 0)), (DO_AZ2, (0, 1)), (DO_AZ1, (8, 0)), (DO_AZ1, (6, 1)), (DO_FIN, (7, 1)),
-    (DO_FIN, (0, 0)), (DO_AZ3, (0, 1)), (DO_AZ2, (9, 0)), (DO_AZ3, (9, 0)), (DO_AZ1, (6, 0)),
-    (DO_AZ2, (8, 0)), (DO_AZ3, (8, 0)), (DO_FIN, (7, 0)), (DO_AZ2, (4, 0)), (DO_AZ3, (4, 0)),
-    (DO_AZ2, (6, 1)), (DO_FIN, (0, 1)), (DO_AZ3, (6, 1)), (DO_AZ2, (6, 0)), (DO_AZ3, (6, 0)),
-    (DO_FIN, (2, 0)), (DO_FIN, (4, 0)), (DO_FIN, (9, 0)), (DO_FIN, (6, 1)), (DO_FIN, (3, 0)),
-    (DO_FIN, (5, 0)), (DO_FIN, (8, 0)), (DO_FIN, (6, 0)), (DO_END, 0),
+    (DO_FIRST, 0), (DO_FIRST, 1), (DO_FIRST, 2), (DO_FIRST, 10), (DO_FIRST, 3), (DO_NEAR, 0),
+    (DO_FIRST, 4), (DO_FIRST, 5), (DO_FIRST, 6), (DO_FIRST, 7), (DO_FIRST, 8), (DO_NEAR, 1),
+    (DO_PLACES, 0), (DO_NEAR, 2), (DO_NEAR, 3), (DO_FAR, 0), (DO_NEAR, 4), (DO_FAR, 1), (DO_FAR, 2),
+    (DO_FAR, 3), (DO_FAR, 4), (DO_NEAR, 10), (DO_NEAR, 5), (DO_SIDE, 1), (DO_NEAR, 8), (DO_SIDE, 0),
+    (DO_UNPACK, 0), (DO_SIDE, 2), (DO_NORM1, 0), (DO_SIDE, 4), (DO_FIRST, 9), (DO_NEAR, 7),
+    (DO_FIRST, 11), (DO_CROSS, 1), (DO_PROJECT, 1), (DO_SIDE, 3), (DO_FAR, 5), (DO_FAR, 7),
+    (DO_CROSS, 2), (DO_FAR, 8), (DO_NEAR, 6), (DO_PROJECT, 2), (DO_CONV, 0), (DO_CONV, 1),
+    (DO_FAR, 6), (DO_CROSS, 4), (DO_SIDE, 7), (DO_NEAR, 11), (DO_CROSS, 3), (DO_SIDE, 5),
+    (DO_CONV, 2), (DO_CONV, 3), (DO_SIDE, 8), (DO_NEAR, 9), (DO_PROJECT, 0), (DO_FAR, 10),
+    (DO_MIX, 0), (DO_CROSS, 7), (DO_EXPAND, 3), (DO_BEND, 3), (DO_SIDE, 6), (DO_FAR, 9),
+    (DO_EXPAND, 2), (DO_BEND, 2), (DO_CROSS, 5), (DO_EXPAND, 1), (DO_BEND, 1), (DO_FAR, 11),
+    (DO_EXPAND, 0), (DO_BEND, 0), (DO_GCON, 0), (DO_STAGE, (2, 0)), (DO_STAGE, (0, 0)),
+    (DO_SIDE, 9), (DO_STAGE, (1, 0)), (DO_SIDE, 10), (DO_SIDE, 11), (DO_ACORE, (0, 0)),
+    (DO_ACORE, (1, 0)), (DO_CROSS, 9), (DO_ACORE, (2, 0)), (DO_FEED, 0), (DO_FEED, 1), (DO_GEXP, 0),
+    (DO_STAGE, (3, 0)), (DO_GEXP, 1), (DO_STAGE, (4, 0)), (DO_FEED, 2), (DO_GEXP, 2),
+    (DO_STAGE, (3, 1)), (DO_ACORE, (4, 0)), (DO_ACORE, (3, 0)), (DO_FEED, 3), (DO_GEXP, 3),
+    (DO_DRAIN, 0), (DO_STAGE, (4, 1)), (DO_AX, (2, 0)), (DO_NORM2B, 0), (DO_BACKG, 0), (DO_GOUT, 0),
+    (DO_STAGE, (5, 0)), (DO_ACORE, (3, 1)), (DO_ACORE, (4, 1)), (DO_AZ1, (0, 0)), (DO_CONVB, 0),
+    (DO_AX, (4, 0)), (DO_ACORE, (5, 0)), (DO_AY, (1, 0)), (DO_CONVB, 1), (DO_AY, (3, 1)),
+    (DO_AY, (3, 0)), (DO_AX, (4, 1)), (DO_AZ1, (2, 0)), (DO_CONVB, 2), (DO_CONVB, 3),
+    (DO_AX, (1, 0)), (DO_AY, (5, 0)), (DO_AZ2, (2, 0)), (DO_AZ3, (2, 0)), (DO_GIN, 1),
+    (DO_STAGE, (6, 1)), (DO_AZ2, (0, 0)), (DO_AZ3, (0, 0)), (DO_AX, (3, 1)), (DO_ACORE, (6, 1)),
+    (DO_STAGE, (7, 1)), (DO_GIN, 2), (DO_STAGE, (6, 2)), (DO_STAGE, (7, 2)), (DO_AZ1, (4, 0)),
+    (DO_ACORE, (7, 1)), (DO_GIN, 0), (DO_AZ1, (4, 1)), (DO_STAGE, (7, 0)), (DO_STAGE, (6, 0)),
+    (DO_AX, (3, 0)), (DO_AX, (5, 0)), (DO_ACORE, (6, 2)), (DO_ACORE, (7, 2)), (DO_ACORE, (7, 0)),
+    (DO_ACORE, (6, 0)), (DO_BFIRST, 0), (DO_AX, (7, 1)), (DO_AZ1, (1, 0)), (DO_AY, (6, 1)),
+    (DO_NORM1B, 0), (DO_SMALL, 0), (DO_STAGE, (8, 0)), (DO_AZ1, (3, 1)), (DO_AX, (7, 2)),
+    (DO_AZ2, (4, 0)), (DO_ACORE, (8, 0)), (DO_AY, (6, 2)), (DO_AX, (0, 0)), (DO_AX, (7, 0)),
+    (DO_AZ1, (3, 0)), (DO_AZ2, (3, 1)), (DO_AZ2, (4, 1)), (DO_AZ3, (3, 1)), (DO_AZ3, (4, 1)),
+    (DO_AX, (6, 1)), (DO_AZ1, (5, 0)), (DO_AZ1, (7, 1)), (DO_AY, (6, 0)), (DO_AZ2, (3, 0)),
+    (DO_AZ3, (3, 0)), (DO_AZ2, (1, 0)), (DO_AZ3, (1, 0)), (DO_AX, (8, 0)), (DO_AZ1, (7, 2)),
+    (DO_AZ2, (7, 1)), (DO_AZ1, (7, 0)), (DO_AX, (6, 2)), (DO_AZ3, (4, 0)), (DO_AZ2, (5, 0)),
+    (DO_AZ3, (5, 0)), (DO_FIN, (0, 0)), (DO_AX, (6, 0)), (DO_AZ3, (6, 1)), (DO_AZ3, (7, 1)),
+    (DO_AZ3, (8, 0)), (DO_AZ2, (7, 2)), (DO_FIN, (4, 0)), (DO_AZ2, (7, 0)), (DO_FIN, (3, 0)),
+    (DO_AZ3, (6, 2)), (DO_FIN, (4, 1)), (DO_FIN, (3, 1)), (DO_AZ3, (7, 2)), (DO_AZ3, (7, 0)),
+    (DO_FIN, (6, 1)), (DO_AZ3, (6, 0)), (DO_FIN, (7, 1)), (DO_FIN, (1, 0)), (DO_FIN, (2, 0)),
+    (DO_FIN, (6, 2)), (DO_FIN, (5, 0)), (DO_FIN, (8, 0)), (DO_FIN, (7, 0)), (DO_FIN, (7, 2)),
+    (DO_FIN, (6, 0)), (DO_END, 0),
 )
 SMALL_ROWS = 64
+HALF = 48
 NORM_ROWS = 128
 INNER_OUT = 8
 
@@ -253,7 +254,7 @@
     tokens, cot, result, delta = take(4)
     sums = take(5)
     full = take(5)
-    g_in, g_out, g_small, own_small, pack = take(5)
+    g_con, g_small, own_small, pack = take(4)
     v96, v288, vexp, v8 = take(4)
     mid_w, fil_w, taps, d_taps = take(4)
     s_inner1, s_first, s_cos1, s_inner2, s_second, s_cos2 = take(6)
@@ -264,14 +265,21 @@
     acc96, acc288, accexp = take(3)
     groups = []
     for matrix, columns, width, kind in REDUCE_GROUPS:
-        members = take(7 if kind == SPLIT else 6)
-        names = ("core", "x", "z1", "z2", "z3", "last") + (("y",) if kind == SPLIT else ())
-        groups.append(dict(zip(names, members)))
+        names = ("core", "x", "z3", "last") if kind in FARS else ("core", "x", "z1", "z2", "z3", "last")
+        names += ("y",) if kind in SPLITS else ()
+        groups.append(dict(zip(names, take(len(names)))))
     ag_recv, ag_cross, ag_core, ag_send, own_sem, rs_recv, rs_y, rs_send, rs_end, out_sem = take(10)
     assert not refs
 
     own = list(own) + [own_small]
-    grads = (g_in, g_out, full[2], full[3], g_small)
+    grads = (full[2], full[2], g_con, full[3], g_small)
+
+    def spot(m, column, width):
+        if m in (0, 1):
+            block = column // 768 if m == 0 else 3
+            assert column % 768 + width <= 768
+            return pl.ds(block * HALF, HALF), pl.ds(column % 768, width)
+        return slice(None), pl.ds(column, width)
 
     rep = lax.axis_index("rep")
     shard = lax.axis_index("shard")
@@ -365,12 +373,12 @@
 
     send_groups = []
     for chunk in chunks:
-        key = chunk[:1] if chunk[0] != 3 else chunk[:2]
+        key = (chunk[0], chunk[3]) if chunk[0] != 3 else chunk[:2]
         if key not in send_groups:
             send_groups.append(key)
 
     def group_of(chunk):
-        return send_groups.index(chunk[:1] if chunk[0] != 3 else chunk[:2])
+        return send_groups.index((chunk[0], chunk[3]) if chunk[0] != 3 else chunk[:2])
 
     def first(index):
         chunk = chunks[index]
@@ -639,26 +647,32 @@
 
     fed_before = []
 
-    def feed(k):
+    def bend(k):
         span = slice(k * 768, k * 768 + 768)
-        rows_of = full[2][k].reshape(768, 768)
-        back_h[...] = dot_nt(cot[...], rows_of)
-
-        def bend(rows):
+
+        def curve(rows):
             values = hidden[rows, span]
             cube = values * values
             grow = math.sqrt(2.0 / math.pi)
             slope = jnp.tanh(grow * (values + 0.044715 * cube * values))
             half_up = 0.5 + 0.5 * slope
             post[rows, span] = (values * half_up).astype(LOW)
-            steep = half_up + (0.5 * values) * (1.0 - slope * slope) * (
+            hidden[rows, span] = half_up + (0.5 * values) * (1.0 - slope * slope) * (
                 grow * (1.0 + 3.0 * 0.044715 * cube)
             )
-            grad = (back_h[rows, :] * steep).astype(LOW)
+
+        row_blocks(16, curve)
+
+    def feed(k):
+        span = slice(k * 768, k * 768 + 768)
+        back_h[...] = dot_nt(cot[...], full[2][k].reshape(768, 768))
+
+        def scale_back(rows):
+            grad = (back_h[rows, :] * hidden[rows, span]).astype(LOW)
             pre[rows, span] = grad
             accexp[:, span] += fold8(grad.astype(FULL))
 
-        row_blocks(16, bend)
+        row_blocks(32, scale_back)
         out_part = dot_nn(post[:, span], full[2][k].reshape(768, 768))
         back_part = dot_nt(pre[:, span], matrix_of(3, pl.ds(k * 768, 768), 768))
         if not fed_before:
@@ -712,10 +726,10 @@
     split_position = {}
     for index, key in enumerate(REDUCE_ORDER):
         position[key] = index
-        if REDUCE_GROUPS[key[0]][3] == SPLIT:
+        if REDUCE_GROUPS[key[0]][3] in SPLITS:
             split_position[key] = len(split_position)
     R_CORE, R_X, R_Z1, R_Z2, R_Z3, R_LAST = range(6)
-    W_CORE, W_Y, W_X, W_Z1, W_Z3, W_LAST, W_END = range(7)
+    W_CORE, W_Y, W_X, W_Z1, W_Z3, W_LAST, W_END, W_Z4 = range(8)
     W_Z2 = W_Z1
 
     def info(key):
@@ -728,8 +742,9 @@
 
     def stage(key):
         g, i, m, column, width, kind, buf, n = info(key)
+        high, wide = spot(m, column, width)
         remote(
-            grads[m].at[:, :, 1 - c, :, pl.ds(column, width)], buf["core"].at[i],
+            grads[m].at[:, :, 1 - c, high, wide], buf["core"].at[i],
             rs_send.at[W_CORE, g], rs_recv.at[R_CORE, n], to_c,
         ).start()
 
@@ -740,6 +755,14 @@
     def send_line(key):
         g, i, m, column, width, kind, buf, n = info(key)
         sums_ref = running(key)
+        if kind in FARS:
+            for step, sent, slot in ((1, W_Z1, R_Z1), (2, W_Z3, R_Z2), (3, W_Z4, R_Z3)):
+                at = (z + step) % 4
+                remote(
+                    sums_ref.at[i, at], buf["z3"].at[i, step - 1],
+                    rs_send.at[sent, g], rs_recv.at[slot, n], (rep, at * 2 + x),
+                ).start()
+            return
 
         @pl.when(jnp.logical_not(inner))
         def _():
@@ -756,19 +779,20 @@
         g, i, m, column, width, kind, buf, n = info(key)
         landing = buf["core"].at[i]
         remote(landing, landing, rs_send.at[W_CORE, g], rs_recv.at[R_CORE, n], to_c).wait_recv()
+        high, wide = spot(m, column, width)
 
         def body(step, carry):
             a, b = step // 2, step % 2
-            buf["core"][i, a, b] = buf["core"][i, a, b] + grads[m][a, b, c, :, pl.ds(column, width)]
+            buf["core"][i, a, b] = buf["core"][i, a, b] + grads[m][a, b, c, high, wide]
             return carry
 
         lax.fori_loop(0, 8, body, 0)
-        if kind == SPLIT:
+        if kind in SPLITS:
             remote(
                 buf["core"].at[i, :, :, :, halves(width, 1 - y)], buf["y"].at[i],
                 rs_send.at[W_Y, g], rs_y.at[split_position[key]], to_y,
             ).start()
-        elif kind == WHOLE:
+        elif kind != LINE:
             remote(
                 buf["core"].at[i, :, 1 - x], buf["x"].at[i],
                 rs_send.at[W_X, g], rs_recv.at[R_X, n], to_x,
@@ -806,7 +830,7 @@
             buf["last"][i, 0] = buf["core"][i, z, x] + buf["x"][i]
             send_last(key)
             return
-        own_part = buf["y"] if kind == SPLIT else buf["core"]
+        own_part = buf["y"] if kind in SPLITS else buf["core"]
 
         def body(step, carry):
             buf["x"][i, step] = buf["x"][i, step] + own_part[i, step, x]
@@ -849,6 +873,15 @@
 
     def add_z3(key):
         g, i, m, column, width, kind, buf, n = info(key)
+        if kind in FARS:
+            total = buf["x"][i, z].astype(FULL)
+            for step, sent, slot in ((1, W_Z1, R_Z1), (2, W_Z3, R_Z2), (3, W_Z4, R_Z3)):
+                landing = buf["z3"].at[i, step - 1]
+                remote(landing, landing, rs_send.at[sent, g], rs_recv.at[slot, n], to_near).wait_recv()
+                total = total + buf["z3"][i, step - 1].astype(FULL)
+            buf["last"][i, 0] = total.astype(buf["last"].dtype)
+            send_last(key)
+            return
         landing = buf["z3"].at[i]
         remote(landing, landing, rs_send.at[W_Z3, g], rs_recv.at[R_Z3, n], to_near).wait_recv()
         if kind == LINE:
@@ -865,7 +898,7 @@
         g, i, m, column, width, kind, buf, n = info(key)
         landing = buf["last"].at[i, 1]
         remote(landing, landing, rs_send.at[W_LAST, g], rs_recv.at[R_LAST, n], to_y).wait_recv()
-        if kind == SPLIT:
+        if kind in SPLITS:
             for which, slot in ((y, 0), (1 - y, 1)):
                 columns = pl.ds(pl.multiple_of(column + which * (width // 2), 128), width // 2)
                 sums[m][:, columns] = buf["last"][i, slot].astype(FULL)
@@ -882,19 +915,19 @@
         def body(s, carry):
             lanes = pl.ds(pl.multiple_of(s * 384, 128), 384)
             value = dot_tn(post[:, lanes], cot[...]).astype(LOW)
-            full[2][s // 2, s % 2] = value.reshape(2, 192, 768)
+            g_con[s // 2, s % 2] = value.reshape(2, 192, 768)
             return carry
 
         lax.fori_loop(0, 8, body, 0)
 
-    def grad_rows(source, other, target, columns, width):
+    def grad_rows(source, other, target, high, columns, width):
         for half in range(2):
             value = dot_tn(source[:, half * 384 : half * 384 + 384], other).astype(LOW)
-            target[2 * half : 2 * half + 2, :, :, :, columns] = value.reshape(2, 2, 2, 48, width)
+            target[2 * half : 2 * half + 2, :, :, high, columns] = value.reshape(2, 2, 2, 48, width)
 
     def grad_expand(i):
         span = slice(i * 768, i * 768 + 768)
-        grad_rows(normed2, pre[:, span], full[3], pl.ds(i * 768, 768), 768)
+        grad_rows(normed2, pre[:, span], full[3], slice(None), pl.ds(i * 768, 768), 768)
 
     def norm_second_back(rows):
         unit, scale = center(resid[rows, :])
@@ -1084,15 +1117,16 @@
         DO_CONV: lambda k: convolve(3 * k, 3 * k + 3),
         DO_MIX: mix,
         DO_EXPAND: expanded,
+        DO_BEND: bend,
         DO_FEED: fed,
         DO_DRAIN: lambda k: drain(2, 0, 768),
         DO_GCON: lambda k: grad_contract(),
         DO_GEXP: expand_back,
         DO_NORM2B: second_back,
         DO_BACKG: lambda k: back_gate(),
-        DO_GOUT: lambda k: grad_rows(gated, back_m[...], g_out, pl.ds(0, 768), 768),
+        DO_GOUT: lambda k: grad_rows(gated, back_m[...], full[2], pl.ds(3 * HALF, HALF), pl.ds(0, 768), 768),
         DO_CONVB: lambda k: convolve_back(3 * k, 3 * k + 3),
-        DO_GIN: lambda k: grad_rows(normed1, bp[k], g_in, pl.ds(k * 768, 768), 768),
+        DO_GIN: lambda k: grad_rows(normed1, bp[k], full[2], pl.ds(k * HALF, HALF), pl.ds(0, 768), 768),
         DO_BFIRST: lambda k: back_first(),
         DO_NORM1B: first_back,
         DO_SMALL: lambda k: small_grads(),
@@ -1116,14 +1150,17 @@
             remote(ref, ref, rs_send.at[kind, g], rs_end.at[g], to_c).wait_send()
 
         leave(W_CORE, buf["core"])
-        if kind == SPLIT:
+        if kind in SPLITS:
             leave(W_Y, buf["y"])
         leave(W_X, buf["x"])
-        leave(W_Z3, buf["z3"])
+        if kind in FARS:
+            for step, sent in enumerate((W_Z1, W_Z3, W_Z4)):
+                leave(sent, buf["z3"].at[:, step])
+        else:
+            leave(W_Z3, buf["z3"])
+            leave(W_Z1, buf["z1"])
         leave(W_LAST, buf["last"].at[:, 0])
         leave(W_END, sums[matrix].at[:, pl.ds(0, width * len(columns))])
-
-        leave(W_Z1, buf["z1"])
 
 
 def unpack_kernel(result, delta, s_in, s_out, s_con, s_exp, s_small, *outs):
@@ -1202,14 +1239,13 @@
     ] + [jax.ShapeDtypeStruct((2,) + s, FULL) for s in shapes]
     count = len(GATHER_CHUNKS)
     crossing = sum(1 for chunk in GATHER_CHUNKS if chunk[3] == SPLIT)
-    leaving = len({chunk[:1] if chunk[0] != 3 else chunk[:2] for chunk in GATHER_CHUNKS})
+    leaving = len({(chunk[0], chunk[3]) if chunk[0] != 3 else chunk[:2] for chunk in GATHER_CHUNKS})
     vm = pltpu.VMEM
     scratch = [vm((rows, width), kind) for kind in (LOW, LOW, LOW, FULL)]
     scratch += [vm(s, FULL) for s in shapes]
     scratch += [vm((4, 2, 2) + s, LOW) for s in shapes]
     scratch += [
-        vm((4, 2, 2) + shapes[0], LOW), vm((4, 2, 2) + shapes[1], LOW),
-        vm((4, 2, 2) + shapes[4], FULL), vm((2, SMALL_ROWS, 128), LOW),
+        vm((4, 2, 2) + shapes[2], LOW), vm((4, 2, 2) + shapes[4], FULL), vm((2, SMALL_ROWS, 128), LOW),
         vm((2 * SMALL_ROWS, 128), FULL),
         vm((8, width), FULL), vm((8, 3 * width), FULL), vm((1, 4 * width), FULL), vm((8, 128), FULL),
         vm((128, 128), FULL), vm((128, width), FULL), vm((LAGS, width), FULL), vm((LAGS, width), FULL),
@@ -1228,21 +1264,26 @@
     for matrix, columns, span, kind in REDUCE_GROUPS:
         n, high = len(columns), shapes[matrix][0]
         of = FULL if matrix == 4 else LOW
-        v = span // 2 if kind == SPLIT else span
-        side_planes, line_planes = ((), (2,)) if kind == LINE else ((4,), ())
-        scratch += [
-            vm((n, 4, 2, high, span), of), vm((n,) + side_planes + (high, v), of),
-            vm((n, 2) + line_planes + (high, v), of), vm((n, 2) + line_planes + (high, v), of),
-            vm((n,) + line_planes + (high, v), of), vm((n, 2, high, v), of),
-        ]
-        if kind == SPLIT:
+        v = span // 2 if kind in SPLITS else span
+        core = vm((n, 4, 2, high, span), of)
+        last = vm((n, 2, high, v), of)
+        if kind in FARS:
+            scratch += [core, vm((n, 4, high, v), of), vm((n, 3, high, v), of), last]
+        else:
+            side_planes, line_planes = ((), (2,)) if kind == LINE else ((4,), ())
+            scratch += [
+                core, vm((n,) + side_planes + (high, v), of),
+                vm((n, 2) + line_planes + (high, v), of), vm((n, 2) + line_planes + (high, v), of),
+                vm((n,) + line_planes + (high, v), of), last,
+            ]
+        if kind in SPLITS:
             scratch.append(vm((n, 4, 2, high, v), of))
     total = len(REDUCE_ORDER)
-    splits = sum(len(g[1]) for g in REDUCE_GROUPS if g[3] == SPLIT)
+    splits = sum(len(g[1]) for g in REDUCE_GROUPS if g[3] in SPLITS)
     dma = pltpu.SemaphoreType.DMA
     scratch += [
         dma((4, count)), dma((3, crossing)), dma((count,)), dma((6, leaving)), dma((9,)),
-        dma((6, total)), dma((splits,)), dma((7, len(REDUCE_GROUPS))), dma((len(REDUCE_GROUPS),)),
+        dma((6, total)), dma((splits,)), dma((8, len(REDUCE_GROUPS))), dma((len(REDUCE_GROUPS),)),
         dma((len(REDUCE_GROUPS),)),
     ]
     in_vmem = pl.BlockSpec(memory_space=pltpu.VMEM)

time: 143 us -> 135 us (0.944)
  Pallas kernels: 142 us -> 134 us
    pallas_call x1, Pallas kernels: 137 us -> 129 us  [block_device(): pl.pallas_call(block_kernel, out_shape=outs, in_specs=[anywhere, in_vmem,...]
where the time goes in v5:
time: 135 us
  Pallas kernels  134 us (99%)
    pallas_call x1, Pallas kernels, block_device(): pl.pallas_call(block_kernel, out_shape=outs, in_specs=[anywhere, in_vmem,...  129 us
    pallas_call x1, Pallas kernels, block_device(): pl.pallas_call(unpack_kernel, out_shape=final, in_specs=[in_vmem] * 7, ou...  4.67 us

profile of v5, /device:TPU:0, one launch (start us, length us, event | category | flops | bytes accessed | tf_op | source)
XLA Modules:
  0.0 134.8 jit_solution(16280288757523294758)
XLA Ops:
  0.7 129.3 %shard_map.425 = (bf16[256,768]{1,0:T(8,128)(2,1)}, f32[256,768]{1,0:T(8,128)}, f32[2,48,2304]{2,1,0:T(8,128)}, f32[2,48,768]{2,1,0:T(8,128)}, f32[2,192,768]{2,...) custom-call(bf16[256,768]{1,0:T(8,128)(2,1)} %bitcast.18, s32[2,128]{1,0:T(2,128)} %bitcast.22, ...), custom_call_target="tpu_custom_call" | custom-call | tf_op jit(solution)/shard_map/pallas_call | solution.py:1291
  130.0 4.7 %shard_map.426 = (bf16[256,768]{1,0:T(8,128)(2,1)}, f32[256,768]{1,0:T(8,128)}, f32[96]{0:T(128)}, f32[96]{0:T(128)}, f32[96,2304]{1,0:T(8,128)}, /*index=5*/f32...) custom-call(bf16[256,768]{1,0:T(8,128)(2,1)} %get-tuple-element.53.r, ...), custom_call_target="tpu_custom_call" | custom-call | tf_op jit(solution)/shard_map/pallas_call | solution.py:1310

commit v6 on v5

--- a/solution.py
+++ b/solution.py
@@ -387,8 +387,32 @@
         landing = full[m].at[z, x, c, :, part(chunk, y)]
         if chunk[3] == LINE:
             remote(piece, landing, ag_send.at[S_SIDE, s], ag_recv.at[SIDE0, index], to_x).start()
+        elif chunk[3] == WHOLE_FAR:
+            for step, sent, slot in straight:
+                remote(
+                    piece, landing, ag_send.at[sent, s], ag_recv.at[slot, index],
+                    (rep, ((z + step) % 4) * 2 + x),
+                ).start()
         else:
             remote(piece, landing, ag_send.at[S_NEAR, s], ag_recv.at[NEAR, index], to_near).start()
+
+    straight = ((1, S_NEAR, NEAR), (2, S_MIRROR, FAR), (3, S_BACK, SIDE1))
+
+    def straight_far(index):
+        chunk = chunks[index]
+        m, s = chunk[0], group_of(chunk)
+        for step, sent, slot in straight:
+            arrived = full[m].at[(z + 4 - step) % 4, x, c, :, whole(chunk)]
+            remote(arrived, arrived, ag_send.at[sent, s], ag_recv.at[slot, index], to_near).wait_recv()
+        column = full[m].at[:, x, c, :, whole(chunk)]
+        remote(column, column, ag_send.at[S_SIDE, s], ag_recv.at[SIDE0, index], to_x).start()
+
+    def straight_side(index):
+        chunk = chunks[index]
+        m, s = chunk[0], group_of(chunk)
+        column = full[m].at[:, 1 - x, c, :, whole(chunk)]
+        remote(column, column, ag_send.at[S_SIDE, s], ag_recv.at[SIDE0, index], to_x).wait_recv()
+        to_core(index)
 
     def line_near(index):
         chunk = chunks[index]
@@ -444,6 +468,8 @@
         chunk = chunks[index]
         if chunk[3] == LINE:
             return line_far(index)
+        if chunk[3] == WHOLE_FAR:
+            return straight_far(index)
         m, s = chunk[0], group_of(chunk)
         both = full[m].at[other_pair, x, c, :, part(chunk, y)]
         remote(both, both, ag_send.at[S_MIRROR, s], ag_recv.at[FAR, index], to_near).wait_recv()
@@ -468,6 +494,8 @@
         chunk = chunks[index]
         if chunk[3] == LINE:
             return line_side(index)
+        if chunk[3] == WHOLE_FAR:
+            return straight_side(index)
         m, s = chunk[0], group_of(chunk)
         for place, slot in ((own_pair, SIDE0), (other_pair, SIDE1)):
             both = full[m].at[place, 1 - x, c, :, part(chunk, y)]
@@ -712,6 +740,12 @@
                 gone(S_NEAR, 1, 1)
                 gone(S_SIDE, 4, 1)
 
+            if kind == WHOLE_FAR:
+                gone(S_MIRROR, 1, 1)
+                gone(S_BACK, 1, 1)
+                gone(S_CORE, 4, 2, wide)
+                continue
+
             @pl.when(inner)
             def _(gone=gone, kind=kind):
                 gone(S_MIRROR, 2, 2 if kind == LINE else 1)
@@ -901,11 +935,10 @@
         if kind in SPLITS:
             for which, slot in ((y, 0), (1 - y, 1)):
                 columns = pl.ds(pl.multiple_of(column + which * (width // 2), 128), width // 2)
-                sums[m][:, columns] = buf["last"][i, slot].astype(FULL)
+                sums[m][:, columns] = buf["last"][i, slot].astype(sums[m].dtype)
         else:
-            sums[m][:, pl.ds(column, width)] = buf["last"][i, 0].astype(FULL) + buf["last"][
-                i, 1
-            ].astype(FULL)
+            total = buf["last"][i, 0].astype(FULL) + buf["last"][i, 1].astype(FULL)
+            sums[m][:, pl.ds(column, width)] = total.astype(sums[m].dtype)
         piece = sums[m].at[:, pl.ds(column, width)]
         place = sums_out[m].at[c, :, pl.ds(column, width)]
         remote(piece, place, rs_send.at[W_END, g], rs_end.at[g], to_c).start()
@@ -1174,7 +1207,7 @@
     for source, target in ((s_in, o_in), (s_out, o_out), (s_con, o_con), (s_exp, o_exp)):
         height = source.shape[1]
         for half in range(2):
-            target[half * height : half * height + height, :] = source[half]
+            target[half * height : half * height + height, :] = source[half].astype(FULL)
     for row, target in enumerate(
         (o_first_gain, o_first_shift, o_direct, o_out_bias, o_second_gain, o_second_shift, o_con_bias)
     ):
@@ -1236,13 +1269,13 @@
     outs = [
         jax.ShapeDtypeStruct((rows, width), LOW),
         jax.ShapeDtypeStruct((rows, width), FULL),
-    ] + [jax.ShapeDtypeStruct((2,) + s, FULL) for s in shapes]
+    ] + [jax.ShapeDtypeStruct((2,) + s, kind) for s, kind in zip(shapes, (LOW,) * 4 + (FULL,))]
     count = len(GATHER_CHUNKS)
     crossing = sum(1 for chunk in GATHER_CHUNKS if chunk[3] == SPLIT)
     leaving = len({(chunk[0], chunk[3]) if chunk[0] != 3 else chunk[:2] for chunk in GATHER_CHUNKS})
     vm = pltpu.VMEM
     scratch = [vm((rows, width), kind) for kind in (LOW, LOW, LOW, FULL)]
-    scratch += [vm(s, FULL) for s in shapes]
+    scratch += [vm(s, kind) for s, kind in zip(shapes, (LOW,) * 4 + (FULL,))]
     scratch += [vm((4, 2, 2) + s, LOW) for s in shapes]
     scratch += [
         vm((4, 2, 2) + shapes[2], LOW), vm((4, 2, 2) + shapes[4], FULL), vm((2, SMALL_ROWS, 128), LOW),

time: 135 us -> 134 us (level)
  no operation moved by 1% of the time
where the time goes in v6:
time: 134 us
  Pallas kernels  133 us (99%)
    pallas_call x1, Pallas kernels, block_device(): pl.pallas_call(block_kernel, out_shape=outs, in_specs=[anywhere, in_vmem,...  129 us
    pallas_call x1, Pallas kernels, block_device(): pl.pallas_call(unpack_kernel, out_shape=final, in_specs=[in_vmem] * 7, ou...  4.13 us

profile of v6, /device:TPU:0, one launch (start us, length us, event | category | flops | bytes accessed | tf_op | source)
XLA Modules:
  0.0 134.2 jit_solution(15121931739827367271)
XLA Ops:
  0.7 129.3 %shard_map.425 = (bf16[256,768]{1,0:T(8,128)(2,1)}, f32[256,768]{1,0:T(8,128)}, bf16[2,48,2304]{2,1,0:T(8,128)(2,1)}, bf16[2,48,768]{2,1,0:T(8,128)(2,1)}, bf16[...) custom-call(bf16[256,768]{1,0:T(8,128)(2,1)} %bitcast.18, s32[2,128]{1,0:T(2,128)} %bitcast.22, ...), custom_call_target="tpu_custom_call" | custom-call | tf_op jit(solution)/shard_map/pallas_call | solution.py:1324
  129.9 4.1 %shard_map.426 = (bf16[256,768]{1,0:T(8,128)(2,1)}, f32[256,768]{1,0:T(8,128)}, f32[96]{0:T(128)}, f32[96]{0:T(128)}, f32[96,2304]{1,0:T(8,128)}, /*index=5*/f32...) custom-call(bf16[256,768]{1,0:T(8,128)(2,1)} %get-tuple-element.53.r, ...), custom_call_target="tpu_custom_call" | custom-call | tf_op jit(solution)/shard_map/pallas_call | solution.py:1343
